TPU v7x, 32 devices: a whole 2x2x4 slice. The times are simulated.
32 devices in a mesh: grp: 2 (over y), blk: 4 (over z), sub: 2 (over x), pair: 2 (over core).
Axes of the slice: x: 2, y: 2, z: 4, core: 2. Of those that a mesh axis runs over, the one named last changes fastest.
Arguments:
- grad_volume: bfloat16 [16, 128, 8192], P(('grp', 'blk', 'sub'), 'pair'), parts along dimension 0, may hold values from -6 to 6
- query_feats: bfloat16 [16384, 1024], P(('grp', 'blk')), parts along dimension 0, may hold values from -6 to 6
- support_feats: bfloat16 [16, 128, 1024], P(('grp', 'blk', 'sub'), 'pair'), parts along dimension 0, may hold values from -6 to 6
- query_kernel: float32 [3, 3], replicated, may hold values from -2 to 2
- support_kernel: float32 [3, 3], replicated, may hold values from -2 to 2
Outputs:
- query_grad: float32 [16384, 1024], P(('grp', 'blk', 'sub', 'pair')), parts along dimension 0
- support_grad: float32 [16, 128, 1024], P(('grp', 'blk', 'sub'), 'pair'), parts along dimension 0
There are 2 independent parts, one for each index of `grp`. A program takes and returns all parts, laid end to end along the dimension named above; an argument that names none is the same for every part. Nothing has to cross between parts.
All inputs are finite; a program needn't handle non-finite values.
Results may differ from a plain program's by a relative error of at most 0.0029.
Values may be sent and summed in bfloat16 or wider, within the bound.
No kernel may reach another device: no remote copies, remote signals or barrier semaphores. Data moves between devices by JAX's collectives and lax.ppermute only.
A program may use at most 64 MiB of HBM per device.

v0:
```python
import math

import jax
import jax.numpy as jnp
from jax import lax
from jax.sharding import PartitionSpec as P

QW = 128
QH = 64


def extended(cells, sides, width):
    for axis, dim in sides:
        count = lax.axis_size(axis)
        ends = count - 1
        head = lax.slice_in_dim(cells, 0, width, axis=dim)
        tail = lax.slice_in_dim(cells, cells.shape[dim] - width, cells.shape[dim], axis=dim)
        cells = jnp.concatenate(
            [
                lax.ppermute(tail, axis, [(i, (i + 1) % count) for i in range(ends)]),
                cells,
                lax.ppermute(head, axis, [((i + 1) % count, i) for i in range(ends)]),
            ],
            axis=dim,
        )
    return cells


def shifted(value, axis, steps):
    count = lax.axis_size(axis)
    pairs = [(source, (source + steps) % count) for source in range(count)]
    return lax.ppermute(value, axis, pairs)


def query_pass(volume, kernel):
    planes, columns, queries = volume.shape
    grid = volume.astype(jnp.float32).reshape(planes, columns, QH, QW)
    padded = jnp.pad(grid, ((0, 0), (0, 0), (1, 1), (1, 1)))
    total = jnp.zeros_like(grid)
    for row_shift in range(3):
        for col_shift in range(3):
            total = (
                total
                + kernel[row_shift, col_shift]
                * padded[:, :, row_shift : row_shift + QH, col_shift : col_shift + QW]
            )
    return total.reshape(planes, columns, queries)


def support_pass(rimmed, kernel, planes, columns):
    total = jnp.zeros((planes, columns, rimmed.shape[2]), jnp.float32)
    for row_shift in range(3):
        for col_shift in range(3):
            total = total + kernel[row_shift, col_shift] * rimmed[
                row_shift : row_shift + planes, col_shift : col_shift + columns
            ].astype(jnp.float32)
    return total


def shards(grad_volume, query_feats, support_feats, query_kernel, support_kernel):
    planes, columns, queries = grad_volume.shape
    rimmed = extended(grad_volume, ((("blk", "sub"), 0), ("pair", 1)), 1)
    corr_grad = (
        query_pass(grad_volume, query_kernel)
        + support_pass(rimmed, support_kernel, planes, columns)
    ).astype(jnp.bfloat16)
    moved = lax.all_to_all(corr_grad, "blk", split_axis=2, concat_axis=0, tiled=True)
    cycle_size = lax.axis_size("blk")
    own_index = lax.axis_index("blk")
    tile_len = moved.shape[2]
    tiles = moved.reshape(cycle_size, planes, columns, tile_len)
    width = query_feats.shape[1]
    scale_factor = 1.0 / math.sqrt(width)

    def project(piece_index, feat_piece, acc_piece, count):
        whole_block = lax.dynamic_index_in_dim(tiles, piece_index, 0, keepdims=False)
        block = whole_block.reshape(planes * count, tile_len)
        feat_flat = feat_piece.reshape(planes * count, width)
        query_term = lax.dot_general(
            block, feat_flat, (((0,), (0,)), ((), ())), preferred_element_type=jnp.float32
        )
        acc_new = acc_piece + jnp.dot(
            block, query_feats, preferred_element_type=jnp.float32
        ).reshape(planes, count, width)
        return (query_term, acc_new)

    query_start = jnp.zeros((tile_len, width), jnp.float32)

    def turn_one(turn_index, carry):
        query_total, feat_piece, acc_piece = carry
        term_piece, acc_piece = project(
            (own_index - turn_index) % cycle_size, feat_piece, acc_piece, columns
        )
        feat_piece = shifted(feat_piece, "blk", 1)
        acc_piece = shifted(acc_piece, "blk", 1)
        return (query_total + term_piece, feat_piece, acc_piece)

    start = (query_start, support_feats, jnp.zeros((planes, columns, width), jnp.float32))
    query_total, feat_piece, support_total = lax.fori_loop(0, cycle_size, turn_one, start)
    query_grad = (
        lax.psum_scatter(query_total, ("sub", "pair"), scatter_dimension=0, tiled=True)
        * scale_factor
    )
    return (query_grad, support_total * scale_factor)


def solution(mesh):
    in_specs = (
        P(("grp", "blk", "sub"), "pair", None),
        P(("grp", "blk"), None),
        P(("grp", "blk", "sub"), "pair", None),
        P(),
        P(),
    )
    out_specs = (P(("grp", "blk", "sub", "pair"), None), P(("grp", "blk", "sub"), "pair", None))
    return jax.shard_map(shards, mesh=mesh, in_specs=in_specs, out_specs=out_specs, check_vma=False)
```

profile of v0, /device:TPU:0, one launch (start us, length us, event | category | flops | bytes accessed | tf_op | source)
XLA Modules:
  0.0 318.6 jit_solution(11927447084421412007)
XLA Ops:
  7.2 5.0 %collective-permute-start.2 = (bf16[1,64,8192]{2,1,0:T(8,128)(2,1)}, bf16[1,64,8192]{2,1,0:T(8,128)(2,1)S(1)}, u32[]{:S(2)}, u32[]{:S(2)}) collective-permute-start(bf16[1,64,8192]{2,1,0:T(8,128)(2,1)} %param.7), channel_id=1, source_target_pairs={{0,2},{2,4},{4,6},{6,8},{8,10},{10,12},{12,14},{1,3},{3,5},{5,7},{... | collective-permute-start | bytes 3145736 | tf_op jit(solution)/shard_map/ppermute | solution.py:20
  12.2 1.3 collective-permute-start.3
  13.5 1.7 fusion.33
  15.2 1.7 fusion.32
  16.9 40.4 %collective-permute-done.2 = bf16[1,64,8192]{2,1,0:T(8,128)(2,1)S(1)} collective-permute-done((bf16[1,64,8192]{2,1,0:T(8,128)(2,1)}, bf16[1,64,8192]{2,1,0:T(8,128)(2,1)S(1)}, u32[]{:S(2)}, u32[]{:S(2)}) %collective-permute-start.2) | collective-permute-done | bytes 1048608 | tf_op jit(solution)/shard_map/ppermute | solution.py:20
  57.4 0.2 constant_dynamic-update-slice_fusion.1
  57.7 0.1 constant_dynamic-update-slice_fusion
  57.8 0.2 fusion.31
  57.9 0.1 copy.21
  58.0 0.1 copy.22
  58.1 1.3 collective-permute-start.5
  59.4 3.0 collective-permute-start.4
  62.4 0.4 copy.23
  62.8 9.4 %fusion.23 = f32[1,64,64,128]{3,2,1,0:T(8,128)S(1)} fusion(f32[1,64,64,128]{3,2,1,0:T(8,128)S(1)} %bitcast.53, f32[]{:T(128)} %bitcast.8, f32[]{:T(128)} %bitcast.7, f32[]{:T(128)} %bitcast.6, f32[]{:T(128)} %bitcast.5, f32[]{:T(128)} %bitcast.4, f32[]{:T(128)} %bitcast.3, f32[]{:T(128)} %bitcast.2, f32[]{:T(128)} %bitcast.1, f32[]{:T(128)} %bitcast), kind=kLoop, calls=%fused_computation.35 | loop fusion | flops 8912896 | bytes 4194340 | tf_op jit(solution)/shard_map/add | solution.py:43
  72.3 1.5 reshape.56
  73.8 0.1 copy.17
  73.9 0.1 copy.15
  74.0 11.4 %fusion.14 = bf16[1,64,8192]{2,1,0:T(8,128)(2,1)S(1)} fusion(f32[1,64,8192]{2,1,0:T(8,128)} %reshape.56, bf16[1,64,8192]{2,1,0:T(8,128)(2,1)} %param.7, bf16[1,64,8192]{2,1,0:T(8,128)(2,1)} %copy-done.2, bf16[1,64,8192]{2,1,0:T(8,128)(2,1)S(1)} %collective-permute-done.2, bf16[3,1,8192]{2,1,0:T(2,128)(2,1)S(1)} %copy.17, bf16[3,64,8192]{2,1,0:T(8,128)(2,1)} %copy-done, ...), kind=kLoop, calls=%fused_computation.26 | loop fusion | flops 24117248 | bytes 9535524 | tf_op jit(solution)/shard_map/convert_element_type | solution.py:66
  85.4 6.8 %copy.18 = bf16[1,64,8192]{1,0,2:T(2,128)(2,1)} copy(bf16[1,64,8192]{2,1,0:T(8,128)(2,1)S(1)} %fusion.14) | data formatting | bytes 2097152 | tf_op jit(solution)/shard_map/convert_element_type | solution.py:66
  92.2 0.5 broadcast.17
  92.7 45.2 %reduce = bf16[8192,64]{1,0:T(8,128)(2,1)S(1)} reduce(bf16[8192,1,64]{2,1,0:T(2,128)(2,1)} %bitcast.51, bf16[]{:T(256)} %broadcast.17), dimensions={1}, to_apply=%bitcast.38.reduce_sub_computation | reduce | bytes 2097154
  138.0 2.7 reshape.60
  140.6 6.3 %all-to-all-start = ((bf16[4,2,65536]{2,1,0:T(2,128)(2,1)}), bf16[4,2,65536]{2,1,0:T(2,128)(2,1)S(1)}, u32[]{:S(2)}, u32[]{:S(2)}) async-start(bf16[4,2,65536]{2,1,0:T(2,128)(2,1)} %reshape.60), calls=%async_computation | async-start | bytes 2097152 | tf_op jit(solution)/shard_map/all_to_all | solution.py:67
  146.9 25.3 %all-to-all-done = bf16[4,2,65536]{2,1,0:T(2,128)(2,1)S(1)} async-done(((bf16[4,2,65536]{2,1,0:T(2,128)(2,1)}), bf16[4,2,65536]{2,1,0:T(2,128)(2,1)S(1)}, u32[]{:S(2)}, u32[]{:S(2)}) %all-to-all-start) | async-done | bytes 1048608 | tf_op jit(solution)/shard_map/all_to_all | solution.py:67
  172.2 3.2 reshape.61
  175.4 8.2 %copy.19 = bf16[1,64,8192]{2,1,0:T(8,128)(2,1)S(1)} copy(bf16[1,64,8192]{1,0,2:T(2,128)(2,1)} %bitcast.52) | data formatting | bytes 2097152 | tf_op jit(solution)/shard_map/all_to_all | solution.py:67
  183.5 0.8 all_to_all.12
  184.3 0.6 copy.20
  185.0 52.0 %while.20 = (s32[]{:T(128)}, f32[2048,1024]{1,0:T(8,128)}, bf16[1,64,1024]{2,1,0:T(8,128)(2,1)S(1)}, f32[1,64,1024]{2,1,0:T(8,128)S(1)}, s32[]{:T(128)}, /*index...) while((s32[]{:T(128)}, f32[2048,1024]{1,0:T(8,128)}, ...), condition=%wide.region_1.2_spmd.clone, body=%wide.region_0.1_spmd.clone.sunk | while | flops 541130752 | bytes 23986536 | solution.py:99
  185.1 3.0 fusion.44
  188.1 0.2 collective-permute-start.1
  188.4 4.5 %select_add_fusion.2 = f32[2048,1024]{1,0:T(8,128)} fusion(f32[2048,1024]{1,0:T(8,128)} %get-tuple-element.318, pred[]{:T(512)S(6)} %compare.5, bf16[4,1,64,2048]{3,2,1,0:T(8,128)(2,1)S(1)} %get-tuple-element.333, s32[]{:T(128)S(6)} %select_n.36, bf16[1,64,1024]{2,1,0:T(8,128)(2,1)S(1)} %copy.32), kind=kOutput, calls=%fused_computation.clone.1 | convolution fusion | flops 272629760 | bytes 17170436 | tf_op jit(solution)/shard_map/while/body/eval_jaxpr/dot_general | solution.py:79
  192.9 4.6 %collective-permute-done.1 = f32[1,64,1024]{2,1,0:T(8,128)S(1)} collective-permute-done((f32[1,64,1024]{2,1,0:T(8,128)S(1)}, f32[1,64,1024]{2,1,0:T(8,128)S(1)}, u32[]{:S(2)}, u32[]{:S(2)}) %collective-permute-start.1) | collective-permute-done | bytes 262176 | tf_op jit(solution)/shard_map/while/body/eval_jaxpr/ppermute | solution.py:32
  197.5 3.0 fusion.44
  200.6 0.2 collective-permute-start.1
  200.8 7.9 %select_add_fusion.2 = f32[2048,1024]{1,0:T(8,128)} fusion(f32[2048,1024]{1,0:T(8,128)} %get-tuple-element.318, pred[]{:T(512)S(6)} %compare.5, bf16[4,1,64,2048]{3,2,1,0:T(8,128)(2,1)S(1)} %get-tuple-element.333, s32[]{:T(128)S(6)} %select_n.36, bf16[1,64,1024]{2,1,0:T(8,128)(2,1)S(1)} %copy.32), kind=kOutput, calls=%fused_computation.clone.1 | convolution fusion | flops 272629760 | bytes 17170436 | tf_op jit(solution)/shard_map/while/body/eval_jaxpr/dot_general | solution.py:79
  208.6 1.2 collective-permute-done.1
  209.9 1.3 collective-permute-start
  211.2 3.0 fusion.44
  214.2 2.4 collective-permute-start.1
  216.6 7.9 %select_add_fusion.2 = f32[2048,1024]{1,0:T(8,128)} fusion(f32[2048,1024]{1,0:T(8,128)} %get-tuple-element.318, pred[]{:T(512)S(6)} %compare.5, bf16[4,1,64,2048]{3,2,1,0:T(8,128)(2,1)S(1)} %get-tuple-element.333, s32[]{:T(128)S(6)} %select_n.36, bf16[1,64,1024]{2,1,0:T(8,128)(2,1)S(1)} %copy.32), kind=kOutput, calls=%fused_computation.clone.1 | convolution fusion | flops 272629760 | bytes 17170436 | tf_op jit(solution)/shard_map/while/body/eval_jaxpr/dot_general | solution.py:79
  224.5 0.1 collective-permute-start
  224.6 3.0 fusion.44
  227.6 1.4 collective-permute-start.1
  229.0 7.9 %select_add_fusion.2 = f32[2048,1024]{1,0:T(8,128)} fusion(f32[2048,1024]{1,0:T(8,128)} %get-tuple-element.318, pred[]{:T(512)S(6)} %compare.5, bf16[4,1,64,2048]{3,2,1,0:T(8,128)(2,1)S(1)} %get-tuple-element.333, s32[]{:T(128)S(6)} %select_n.36, bf16[1,64,1024]{2,1,0:T(8,128)(2,1)S(1)} %copy.32), kind=kOutput, calls=%fused_computation.clone.1 | convolution fusion | flops 272629760 | bytes 17170436 | tf_op jit(solution)/shard_map/while/body/eval_jaxpr/dot_general | solution.py:79
  236.9 0.7 broadcast_multiply_fusion.1
  237.7 70.9 %reduce-scatter.2.cloned.1.call-done = f32[512,1024]{1,0:T(8,128)} async-done(((f32[2048,1024]{1,0:T(8,128)}), f32[512,1024]{1,0:T(8,128)}) %reduce-scatter.2.cloned.1.call-update) | async-done | bytes 2097168 | tf_op jit(solution)/shard_map/reduce_scatter | solution.py:101
  308.5 3.2 %broadcast_multiply_fusion = f32[512,1024]{1,0:T(8,128)} fusion(f32[512,1024]{1,0:T(8,128)} %reduce-scatter.2.cloned.1.call-done), kind=kLoop, calls=%fused_computation.45 | loop fusion | flops 524288 | bytes 4194304 | tf_op jit(solution)/shard_map/mul | solution.py:101
  (28 shorter events, 0.3 us)
Async XLA Ops:
  7.2 50.3 %copy-start.3 = (bf16[1,64,8192]{2,1,0:T(8,128)(2,1)S(1)}, bf16[1,64,8192]{2,1,0:T(8,128)(2,1)}, u32[]{:S(2)}) copy-start(bf16[1,64,8192]{2,1,0:T(8,128)(2,1)} %param.7) | copy-start | bytes 3145732
  7.2 50.2 %collective-permute-start.2 = (bf16[1,64,8192]{2,1,0:T(8,128)(2,1)}, bf16[1,64,8192]{2,1,0:T(8,128)(2,1)S(1)}, u32[]{:S(2)}, u32[]{:S(2)}) collective-permute-start(bf16[1,64,8192]{2,1,0:T(8,128)(2,1)} %param.7), channel_id=1, source_target_pairs={{0,2},{2,4},{4,6},{6,8},{8,10},{10,12},{12,14},{1,3},{3,5},{5,7},{... | collective-permute-start | bytes 3145736 | tf_op jit(solution)/shard_map/ppermute | solution.py:20
  12.2 45.5 %collective-permute-start.3 = (bf16[1,64,8192]{2,1,0:T(8,128)(2,1)}, bf16[1,64,8192]{2,1,0:T(8,128)(2,1)S(1)}, u32[]{:S(2)}, u32[]{:S(2)}) collective-permute-start(bf16[1,64,8192]{2,1,0:T(8,128)(2,1)} %param.7), channel_id=1, source_target_pairs={{2,0},{4,2},{6,4},{8,6},{10,8},{12,10},{14,12},{3,1},{5,3},{7,5},{... | collective-permute-start | bytes 3145736 | tf_op jit(solution)/shard_map/ppermute | solution.py:22
  57.7 5.1 %copy-start.2 = (bf16[1,64,8192]{2,1,0:T(8,128)(2,1)}, bf16[1,64,8192]{2,1,0:T(8,128)(2,1)S(1)}, u32[]{:S(2)}) copy-start(bf16[1,64,8192]{2,1,0:T(8,128)(2,1)S(1)} %collective-permute-done.3) | copy-start | bytes 3145732
  57.8 5.1 %copy-start = (bf16[3,64,8192]{2,1,0:T(8,128)(2,1)}, bf16[3,64,8192]{2,1,0:T(8,128)(2,1)S(1)}, u32[]{:S(2)}) copy-start(bf16[3,64,8192]{2,1,0:T(8,128)(2,1)S(1)} %constant_dynamic-update-slice_fusion) | copy-start | bytes 9437188
  58.1 15.7 %collective-permute-start.5 = (bf16[3,1,8192]{2,0,1:T(4,128)(2,1)S(1)}, bf16[3,1,8192]{2,0,1:T(4,128)(2,1)S(1)}, u32[]{:S(2)}, u32[]{:S(2)}) collective-permute-start(bf16[3,1,8192]{2,0,1:T(4,128)(2,1)S(1)} %copy.22), channel_id=1, source_target_pairs={{1,0},{3,2},{5,4},{7,6},{9,8},{11,10},{13,12},{15,14},{17,16},{19,... | collective-permute-start | bytes 147464 | tf_op jit(solution)/shard_map/ppermute | solution.py:22
  59.4 14.5 %collective-permute-start.4 = (bf16[3,1,8192]{2,0,1:T(4,128)(2,1)S(1)}, bf16[3,1,8192]{2,0,1:T(4,128)(2,1)S(1)}, u32[]{:S(2)}, u32[]{:S(2)}) collective-permute-start(bf16[3,1,8192]{2,0,1:T(4,128)(2,1)S(1)} %copy.21), channel_id=1, source_target_pairs={{0,1},{2,3},{4,5},{6,7},{8,9},{10,11},{12,13},{14,15},{16,17},{18,... | collective-permute-start | bytes 147464 | tf_op jit(solution)/shard_map/ppermute | solution.py:20
  140.6 31.6 %all-to-all-start = ((bf16[4,2,65536]{2,1,0:T(2,128)(2,1)}), bf16[4,2,65536]{2,1,0:T(2,128)(2,1)S(1)}, u32[]{:S(2)}, u32[]{:S(2)}) async-start(bf16[4,2,65536]{2,1,0:T(2,128)(2,1)} %reshape.60), calls=%async_computation | async-start | bytes 2097152 | tf_op jit(solution)/shard_map/all_to_all | solution.py:67
  146.9 161.6 %reduce-scatter.2.cloned.1.call-start = ((), (), s32[]{:S(2)}) async-start(), calls=%async_computation.2 | async-start | bytes 10485760 | tf_op jit(solution)/shard_map/reduce_scatter | solution.py:101
  183.5 1.4 copy-start.1
  185.0 7.9 %collective-permute-start = (bf16[1,64,1024]{2,1,0:T(8,128)(2,1)S(1)}, bf16[1,64,1024]{2,1,0:T(8,128)(2,1)S(1)}, u32[]{:S(2)}, u32[]{:S(2)}) collective-permute-start(bf16[1,64,1024]{2,1,0:T(8,128)(2,1)S(1)} %copy.32), channel_id=1, source_target_pairs={{0,4},{4,8},{8,12},{12,0},{1,5},{5,9},{9,13},{13,1},{2,6},{6,10},{... | collective-permute-start | bytes 393224 | tf_op jit(solution)/shard_map/while/body/eval_jaxpr/ppermute | solution.py:32
  188.1 9.3 %collective-permute-start.1 = (f32[1,64,1024]{2,1,0:T(8,128)S(1)}, f32[1,64,1024]{2,1,0:T(8,128)S(1)}, u32[]{:S(2)}, u32[]{:S(2)}) collective-permute-start(f32[1,64,1024]{2,1,0:T(8,128)S(1)} %fusion.44), channel_id=1, source_target_pairs={{0,4},{4,8},{8,12},{12,0},{1,5},{5,9},{9,13},{13,1},{2,6},{6,10},{... | collective-permute-start | bytes 786440 | tf_op jit(solution)/shard_map/while/body/eval_jaxpr/ppermute | solution.py:32
  197.4 11.2 %collective-permute-start = (bf16[1,64,1024]{2,1,0:T(8,128)(2,1)S(1)}, bf16[1,64,1024]{2,1,0:T(8,128)(2,1)S(1)}, u32[]{:S(2)}, u32[]{:S(2)}) collective-permute-start(bf16[1,64,1024]{2,1,0:T(8,128)(2,1)S(1)} %copy.32), channel_id=1, source_target_pairs={{0,4},{4,8},{8,12},{12,0},{1,5},{5,9},{9,13},{13,1},{2,6},{6,10},{... | collective-permute-start | bytes 393224 | tf_op jit(solution)/shard_map/while/body/eval_jaxpr/ppermute | solution.py:32
  200.6 9.3 %collective-permute-start.1 = (f32[1,64,1024]{2,1,0:T(8,128)S(1)}, f32[1,64,1024]{2,1,0:T(8,128)S(1)}, u32[]{:S(2)}, u32[]{:S(2)}) collective-permute-start(f32[1,64,1024]{2,1,0:T(8,128)S(1)} %fusion.44), channel_id=1, source_target_pairs={{0,4},{4,8},{8,12},{12,0},{1,5},{5,9},{9,13},{13,1},{2,6},{6,10},{... | collective-permute-start | bytes 786440 | tf_op jit(solution)/shard_map/while/body/eval_jaxpr/ppermute | solution.py:32
  209.9 14.6 %collective-permute-start = (bf16[1,64,1024]{2,1,0:T(8,128)(2,1)S(1)}, bf16[1,64,1024]{2,1,0:T(8,128)(2,1)S(1)}, u32[]{:S(2)}, u32[]{:S(2)}) collective-permute-start(bf16[1,64,1024]{2,1,0:T(8,128)(2,1)S(1)} %copy.32), channel_id=1, source_target_pairs={{0,4},{4,8},{8,12},{12,0},{1,5},{5,9},{9,13},{13,1},{2,6},{6,10},{... | collective-permute-start | bytes 393224 | tf_op jit(solution)/shard_map/while/body/eval_jaxpr/ppermute | solution.py:32
  214.2 10.3 %collective-permute-start.1 = (f32[1,64,1024]{2,1,0:T(8,128)S(1)}, f32[1,64,1024]{2,1,0:T(8,128)S(1)}, u32[]{:S(2)}, u32[]{:S(2)}) collective-permute-start(f32[1,64,1024]{2,1,0:T(8,128)S(1)} %fusion.44), channel_id=1, source_target_pairs={{0,4},{4,8},{8,12},{12,0},{1,5},{5,9},{9,13},{13,1},{2,6},{6,10},{... | collective-permute-start | bytes 786440 | tf_op jit(solution)/shard_map/while/body/eval_jaxpr/ppermute | solution.py:32
  224.5 12.4 %collective-permute-start = (bf16[1,64,1024]{2,1,0:T(8,128)(2,1)S(1)}, bf16[1,64,1024]{2,1,0:T(8,128)(2,1)S(1)}, u32[]{:S(2)}, u32[]{:S(2)}) collective-permute-start(bf16[1,64,1024]{2,1,0:T(8,128)(2,1)S(1)} %copy.32), channel_id=1, source_target_pairs={{0,4},{4,8},{8,12},{12,0},{1,5},{5,9},{9,13},{13,1},{2,6},{6,10},{... | collective-permute-start | bytes 393224 | tf_op jit(solution)/shard_map/while/body/eval_jaxpr/ppermute | solution.py:32
  227.6 9.3 %collective-permute-start.1 = (f32[1,64,1024]{2,1,0:T(8,128)S(1)}, f32[1,64,1024]{2,1,0:T(8,128)S(1)}, u32[]{:S(2)}, u32[]{:S(2)}) collective-permute-start(f32[1,64,1024]{2,1,0:T(8,128)S(1)} %fusion.44), channel_id=1, source_target_pairs={{0,4},{4,8},{8,12},{12,0},{1,5},{5,9},{9,13},{13,1},{2,6},{6,10},{... | collective-permute-start | bytes 786440 | tf_op jit(solution)/shard_map/while/body/eval_jaxpr/ppermute | solution.py:32
Sparse Core Ops, SparseCore 0:
  237.1 71.4 reduce-scatter.1
where the time goes:
time: 320 us; the launch traced here: 319 us
  waiting for transfers between devices  142 us (44%)
  other arithmetic  70.3 us (22%)
  matrix products  40.3 us (13%)
  local copies, waits for them, and re-layouts  28.6 us (9%)
  starting transfers between devices  22.6 us (7%)
  between operations  14.2 us (4%)
    reduce_scatter x1, waiting for transfers between devices, shards(): lax.psum_scatter(query_total, ('sub', 'pair'), scatter_dimension=0, tiled...  70.9 us
    unnamed x3, other arithmetic  45.5 us
    ppermute x2, waiting for transfers between devices, extended(): lax.ppermute(tail, axis, [(i, (i + 1) % count) for i in range(ends)])  40.4 us
    dot_general x4, matrix products, project(): lax.dot_general(block, feat_flat, (((0,), (0,)), ((), ())), preferred_ele...  28.1 us
    all_to_all x1, waiting for transfers between devices, shards(): lax.all_to_all(corr_grad, 'blk', split_axis=2, concat_axis=0, tiled=True)  25.3 us
    dot_general x4, matrix products, project(): jnp.dot(block, query_feats, preferred_element_type=jnp.float32)  12.1 us
    convert_element_type x1, other arithmetic, shards(): corr_grad = (query_pass(grad_volume, query_kernel) + support_pass(rimmed,...  11.4 us
    add x1, other arithmetic, query_pass(): total + kernel[row_shift, col_shift] * padded[:, :, row_shift:row_shift +...  9.43 us
  transfers between devices with their start and end apart: 14, of which 5 were waited for; matrix products, arithmetic and copies ran while one was open for 18% of the time, Pallas kernels for 0%

commit v1 on v0

--- a/solution.py
+++ b/solution.py
@@ -3,6 +3,8 @@
 import jax
 import jax.numpy as jnp
 from jax import lax
+from jax.experimental import pallas as pl
+from jax.experimental.pallas import tpu as pltpu
 from jax.sharding import PartitionSpec as P
 
 QW = 128
@@ -57,7 +59,7 @@
     return total
 
 
-def shards(grad_volume, query_feats, support_feats, query_kernel, support_kernel):
+def ring_shards(grad_volume, query_feats, support_feats, query_kernel, support_kernel):
     planes, columns, queries = grad_volume.shape
     rimmed = extended(grad_volume, ((("blk", "sub"), 0), ("pair", 1)), 1)
     corr_grad = (
@@ -104,6 +106,210 @@
     return (query_grad, support_total * scale_factor)
 
 
+def split_taps(kernel):
+    high = lax.reduce_precision(kernel, 8, 7)
+    return high, kernel - high
+
+
+def tap_matrix(taps, row_step, col_step):
+    total = jnp.zeros(row_step.shape, jnp.float32)
+    for a in range(3):
+        for b in range(3):
+            hit = (row_step == a - 1) & (col_step == b - 1)
+            total = jnp.where(hit, taps[a, b], total)
+    return total.astype(jnp.bfloat16)
+
+
+def query_matrices(kernel):
+    shape = (4 * QW, 2 * QW)
+    source = lax.broadcasted_iota(jnp.int32, shape, 0)
+    target = lax.broadcasted_iota(jnp.int32, shape, 1)
+    row_step = source // QW - target // QW - 1
+    col_step = source % QW - target % QW
+    return [tap_matrix(taps, row_step, col_step) for taps in split_taps(kernel)]
+
+
+def support_matrices(kernel, own, core, count, columns, edge):
+    cells = count * columns
+    shape = (cells, cells + edge)
+    target = lax.broadcasted_iota(jnp.int32, shape, 0)
+    source = lax.broadcasted_iota(jnp.int32, shape, 1)
+    rim = source >= cells
+    slot = jnp.where(rim, source - cells, source // columns)
+    beside = jnp.where(core == 0, columns, -1)
+    column = jnp.where(rim, beside, source % columns)
+    row_step = (own ^ slot) - (own ^ (target // columns))
+    row_step = jnp.where(slot < count, row_step, 2)
+    col_step = column - target % columns
+    return [tap_matrix(taps, row_step, col_step) for taps in split_taps(kernel)]
+
+
+def tile_kernel(count, columns, tile, edge, width, *refs):
+    side_ref = refs[0]
+    pieces = refs[1 : 1 + count]
+    rim_ref, th_ref, tl_ref, wh_ref, wl_ref, feats_ref = refs[1 + count : 7 + count]
+    keep_ref, send_ref, own_ref = refs[7 + count : 10 + count]
+    parts = refs[10 + count : 9 + 2 * count]
+    cells_ref, corr_ref, feats, sem = refs[9 + 2 * count :]
+    cells = count * columns
+    side = side_ref[0]
+    core = side_ref[1]
+    start = pl.multiple_of(side * tile, tile)
+    fetch = pltpu.make_async_copy(feats_ref.at[pl.ds(start, tile), :], feats, sem)
+    fetch.start()
+    for k in range(count):
+        cells_ref[k * columns : (k + 1) * columns, :] = pieces[k][...]
+    cells_ref[cells:, QW : QW + tile] = rim_ref[...]
+    step = 2 * QW
+    for low in range(0, tile, step):
+        window = cells_ref[:cells, low : low + 2 * step]
+        middle = cells_ref[:, low + QW : low + QW + step]
+        total = jnp.dot(window, wh_ref[...], preferred_element_type=jnp.float32)
+        total += jnp.dot(window, wl_ref[...], preferred_element_type=jnp.float32)
+        total += jnp.dot(th_ref[...], middle, preferred_element_type=jnp.float32)
+        total += jnp.dot(tl_ref[...], middle, preferred_element_type=jnp.float32)
+        corr_ref[:, low : low + step] = total.astype(jnp.bfloat16)
+    half = tile // 2
+    keep_ref[...] = corr_ref[:, pl.ds(pl.multiple_of(core * half, half), half)]
+    send_ref[...] = corr_ref[:, pl.ds(pl.multiple_of((1 - core) * half, half), half)]
+    fetch.wait()
+    for low in range(0, width, step):
+        total = jnp.dot(
+            corr_ref[...], feats[:, low : low + step], preferred_element_type=jnp.float32
+        )
+        own_ref[:, low : low + step] = total[:columns]
+        for k in range(1, count):
+            parts[k - 1][:, low : low + step] = total[k * columns : (k + 1) * columns].astype(
+                jnp.bfloat16
+            )
+
+
+def tile_call(side, pieces, rim, support_mats, query_mats, feats, count, columns, tile):
+    width = feats.shape[1]
+    edge = rim.shape[0]
+    cells = count * columns
+    vmem = pl.BlockSpec(memory_space=pltpu.VMEM)
+    flops = 2 * cells * tile * (2 * (cells + edge) + 8 * QW + width)
+    moved = 2 * (2 * cells * tile + 4 * cells * cells + tile * width + cells * width)
+    return pl.pallas_call(
+        lambda *refs: tile_kernel(count, columns, tile, edge, width, *refs),
+        out_shape=[
+            jax.ShapeDtypeStruct((cells, tile // 2), jnp.bfloat16),
+            jax.ShapeDtypeStruct((cells, tile // 2), jnp.bfloat16),
+            jax.ShapeDtypeStruct((columns, width), jnp.float32),
+        ]
+        + [jax.ShapeDtypeStruct((columns, width), jnp.bfloat16)] * (count - 1),
+        in_specs=[pl.BlockSpec(memory_space=pltpu.SMEM)]
+        + [vmem] * (count + 5)
+        + [pl.BlockSpec(memory_space=pl.ANY)],
+        out_specs=[vmem] * (count + 2),
+        scratch_shapes=[
+            pltpu.VMEM((cells + edge, tile + 2 * QW), jnp.bfloat16),
+            pltpu.VMEM((cells, tile), jnp.bfloat16),
+            pltpu.VMEM((tile, width), jnp.bfloat16),
+            pltpu.SemaphoreType.DMA,
+        ],
+        compiler_params=pltpu.CompilerParams(vmem_limit_bytes=40 << 20),
+        cost_estimate=pl.CostEstimate(flops=flops, bytes_accessed=moved, transcendentals=0),
+        name="tile_kernel",
+    )(side, *pieces, rim, *support_mats, *query_mats, feats)
+
+
+def gathered(feats, count, columns, bits):
+    held = {0: feats}
+    for bit in bits:
+        slots = sorted(held)
+        block = jnp.concatenate([held[k] for k in slots], axis=0) if len(slots) > 1 else held[0]
+        moved = lax.ppermute(block, ("blk", "sub"), [(i, i ^ bit) for i in range(count)])
+        for at, k in enumerate(slots):
+            held[k ^ bit] = moved[at * columns : (at + 1) * columns]
+    return jnp.concatenate([held[k] for k in range(count)], axis=0)
+
+
+def tile_shards(grad_volume, query_feats, support_feats, query_kernel, support_kernel):
+    _, columns, queries = grad_volume.shape
+    width = query_feats.shape[1]
+    outer = lax.axis_size("blk")
+    inner = lax.axis_size("sub")
+    count = outer * inner
+    tile = queries // count
+    scale_factor = 1.0 / math.sqrt(width)
+    own = lax.axis_index(("blk", "sub"))
+    side = lax.axis_index("sub")
+    core = lax.axis_index("pair")
+    swap = [(0, 1), (1, 0)]
+
+    def exchanged(value, mask):
+        return lax.ppermute(value, ("blk", "sub"), [(i, i ^ mask) for i in range(count)])
+
+    volume = jnp.pad(grad_volume[0], ((0, 0), (QW, QW)))
+
+    def piece(mask):
+        return lax.dynamic_slice(volume, (0, (own ^ mask) * tile), (columns, tile + 2 * QW))
+
+    pieces = [piece(0)] + [None] * (count - 1)
+    for mask in range(count - 1, 0, -1):
+        pieces[mask] = exchanged(piece(mask), mask)
+
+    bits = []
+    bit = count // 2
+    while bit:
+        bits.append(bit)
+        bit //= 2
+    feats_own = gathered(support_feats[0], count, columns, bits)
+    feats_other = lax.ppermute(feats_own, "pair", swap)
+
+    edge = 16 * -(-count // 16)
+    border = jnp.where(core == 0, columns - 1, 0)
+    rim = jnp.concatenate(
+        [lax.dynamic_slice(cell, (border, QW), (1, tile)) for cell in pieces]
+        + [jnp.zeros((edge - count, tile), jnp.bfloat16)],
+        axis=0,
+    )
+    rim = lax.ppermute(rim, "pair", swap)
+    outs = tile_call(
+        jnp.stack([side, core]).astype(jnp.int32),
+        pieces,
+        rim,
+        support_matrices(support_kernel, own, core, count, columns, edge),
+        query_matrices(query_kernel),
+        query_feats,
+        count,
+        columns,
+        tile,
+    )
+    keep, send, support_own = outs[:3]
+    parts = outs[3:]
+    landed = [exchanged(parts[mask - 1], mask) for mask in range(count - 1, 0, -1)]
+    other = lax.ppermute(send, "pair", swap)
+
+    def query_term(block, feats):
+        return lax.dot_general(
+            block, feats, (((0,), (0,)), ((), ())), preferred_element_type=jnp.float32
+        )
+
+    query_grad = (query_term(keep, feats_own) + query_term(other, feats_other)) * scale_factor
+    support_grad = support_own
+    for term in landed:
+        support_grad = support_grad + term.astype(jnp.float32)
+    return (query_grad, (support_grad * scale_factor)[None])
+
+
+def tiles_fit(mesh, grad_volume):
+    shape = dict(mesh.shape)
+    count = shape["blk"] * shape["sub"]
+    planes = grad_volume.shape[0] // (shape["grp"] * count)
+    columns = grad_volume.shape[1] // shape["pair"]
+    return (
+        planes == 1
+        and shape["pair"] == 2
+        and count & (count - 1) == 0
+        and count * columns <= 1024
+        and columns % 16 == 0
+        and QH * QW % (count * 2 * QW) == 0
+    )
+
+
 def solution(mesh):
     in_specs = (
         P(("grp", "blk", "sub"), "pair", None),
@@ -113,4 +319,12 @@
         P(),
     )
     out_specs = (P(("grp", "blk", "sub", "pair"), None), P(("grp", "blk", "sub"), "pair", None))
-    return jax.shard_map(shards, mesh=mesh, in_specs=in_specs, out_specs=out_specs, check_vma=False)
+
+    def program(grad_volume, *rest):
+        body = tile_shards if tiles_fit(mesh, grad_volume) else ring_shards
+        mapped = jax.shard_map(
+            body, mesh=mesh, in_specs=in_specs, out_specs=out_specs, check_vma=False
+        )
+        return mapped(grad_volume, *rest)
+
+    return program

time: 320 us -> 124 us (0.39)
  waiting for transfers between devices: 142 us -> 32 us
  other arithmetic: 70.3 us -> 31.2 us
  matrix products: 40.3 us -> 2.77 us
  between operations: 14.2 us -> 0.98 us
  starting transfers between devices: 22.6 us -> 35 us
  local copies, waits for them, and re-layouts: 28.6 us -> 16.6 us
  Pallas kernels: 0 us -> 4.89 us
    reduce_scatter x1 -> x0, waiting for transfers between devices: 70.9 us -> none  [shards(): lax.psum_scatter(query_total, ('sub', 'pair'), scatter_dimension=0, tiled...]
    unnamed x3 -> x0, other arithmetic: 45.5 us -> none
    dot_general x8 -> x2, matrix products: 40.3 us -> 2.77 us  [query_term(): lax.dot_general(block, feats, (((0,), (0,)), ((), ())), preferred_element...]
    all_to_all x1 -> x0, waiting for transfers between devices: 25.3 us -> none  [shards(): lax.all_to_all(corr_grad, 'blk', split_axis=2, concat_axis=0, tiled=True)]
    ppermute x12 -> x20, starting transfers between devices: 16.3 us -> 35 us  [the longest x14 29.6 us: exchanged(): lax.ppermute(value, ('blk', 'sub'), [(i, i ^ mask) for i in range(count)])]
    convert_element_type x1 -> x4, other arithmetic: 11.4 us -> 29.3 us  [tap_matrix(): return total.astype(jnp.bfloat16)]
    ppermute x12 -> x20, waiting for transfers between devices: 46.3 us -> 32 us  [the longest x14 20.2 us: exchanged(): lax.ppermute(value, ('blk', 'sub'), [(i, i ^ mask) for i in range(count)])]
    add x1 -> x3, other arithmetic: 9.43 us -> 0.01 us  [the longest x2 0.01 us: query_matrices(): col_step = source % QW - target % QW]
  transfers between devices with their start and end apart: 14 -> 20, of which waited for: 5 -> 10; matrix products, arithmetic and copies ran while one was open for 18% -> 35% of each run, Pallas kernels for 0% -> 4%
where the time goes in v1:
time: 124 us; the launch traced here: 123 us
  starting transfers between devices  35 us (28%)
  waiting for transfers between devices  32 us (26%)
  other arithmetic  31.2 us (25%)
  local copies, waits for them, and re-layouts  16.6 us (13%)
  Pallas kernels  4.89 us (4%)
  matrix products  2.77 us (2%)
    ppermute x14, starting transfers between devices, exchanged(): lax.ppermute(value, ('blk', 'sub'), [(i, i ^ mask) for i in range(count)])  29.6 us
    convert_element_type x4, other arithmetic, tap_matrix(): return total.astype(jnp.bfloat16)  29.3 us
    ppermute x14, waiting for transfers between devices, exchanged(): lax.ppermute(value, ('blk', 'sub'), [(i, i ^ mask) for i in range(count)])  20.2 us
    ppermute x3, waiting for transfers between devices, gathered(): lax.ppermute(block, ('blk', 'sub'), [(i, i ^ bit) for i in range(count)])  11.8 us
    unnamed x25, local copies, waits for them, and re-layouts  11 us
    ppermute x3, starting transfers between devices, gathered(): lax.ppermute(block, ('blk', 'sub'), [(i, i ^ bit) for i in range(count)])  5.09 us
    pallas_call x1, Pallas kernels, tile_call(): pl.pallas_call(lambda *refs: tile_kernel(count, columns, tile, edge, widt...  4.89 us
    dot_general x2, matrix products, query_term(): lax.dot_general(block, feats, (((0,), (0,)), ((), ())), preferred_element...  2.77 us
  transfers between devices with their start and end apart: 20, of which 10 were waited for; matrix products, arithmetic and copies ran while one was open for 35% of the time, Pallas kernels for 4%

profile of v1, /device:TPU:0, one launch (start us, length us, event | category | flops | bytes accessed | tf_op | source)
XLA Modules:
  0.0 123.4 jit_solution(5103067798689487082)
XLA Ops:
  0.7 2.3 %pad_dynamic-slice_fusion.1 = (bf16[64,1280]{1,0:T(8,128)(2,1)S(1)}, bf16[64,1280]{1,0:T(8,128)(2,1)}, bf16[64,1280]{1,0:T(8,128)(2,1)}, bf16[64,1280]{1,0:T(8,1...) fusion(s32[]{:T(128)S(6)} %select_n.348, ...), kind=kLoop, calls=%fused_computation.27 | loop fusion | bytes 2359328 | tf_op jit(solution)/shard_map/dynamic_slice | solution.py:248
  3.0 6.0 %collective-permute-start.6 = (bf16[64,1280]{1,0:T(8,128)(2,1)S(1)}, bf16[64,1280]{1,0:T(8,128)(2,1)S(1)}, u32[]{:S(2)}, u32[]{:S(2)}) collective-permute-start(bf16[64,1280]{1,0:T(8,128)(2,1)S(1)} %get-tuple-element.22), channel_id=1, source_target_pairs={{0,14},{2,12},{4,10},{6,8},{8,6},{10,4},{12,2},{14,0},{1,15},{3,13... | collective-permute-start | bytes 491528 | tf_op jit(solution)/shard_map/ppermute | solution.py:243
  9.0 0.2 collective-permute-start.5
  9.2 0.8 collective-permute-start.4
  10.0 2.0 %collective-permute-start.3 = (bf16[64,1280]{1,0:T(8,128)(2,1)}, bf16[64,1280]{1,0:T(8,128)(2,1)S(1)}, u32[]{:S(2)}, u32[]{:S(2)}) collective-permute-start(bf16[64,1280]{1,0:T(8,128)(2,1)} %get-tuple-element.26), channel_id=1, source_target_pairs={{0,8},{2,10},{4,12},{6,14},{8,0},{10,2},{12,4},{14,6},{1,9},{3,11}... | collective-permute-start | bytes 491528 | tf_op jit(solution)/shard_map/ppermute | solution.py:243
  12.0 1.0 collective-permute-start.8
  13.1 0.7 fusion.35
  13.9 0.7 fusion.33
  14.6 8.1 %select_convert_fusion.refs_11_ = bf16[512,528]{1,0:T(8,128)(2,1)S(1)} fusion(bf16[]{:T(256)} %bitcast.20, bf16[]{:T(256)} %bitcast.19, bf16[]{:T(256)} %bitcast.18, bf16[]{:T(256)} %bitcast.17, bf16[]{:T(256)} %bitcast.16, bf16[]{:T(256)} %bitcast.15, bf16[]{:T(256)} %bitcast.14, bf16[]{:T(256)} %bitcast.13, bf16[]{:T(256)} %bitcast.12, ...), kind=kLoop, calls=%fused_computation.1 | loop fusion | flops 9732096 | bytes 562058 | tf_op jit(solution)/shard_map/convert_element_type | solution.py:120
  22.7 7.7 %select_convert_fusion.1.refs_10_ = bf16[512,528]{1,0:T(8,128)(2,1)S(1)} fusion(bf16[]{:T(256)} %bitcast.11, bf16[]{:T(256)} %bitcast.10, bf16[]{:T(256)} %bitcast.9, bf16[]{:T(256)} %bitcast.8, bf16[]{:T(256)} %bitcast.7, bf16[]{:T(256)} %bitcast.6, bf16[]{:T(256)} %bitcast.5, bf16[]{:T(256)} %bitcast.4, bf16[]{:T(256)} %bitcast.3, ...), kind=kLoop, calls=%fused_computation.2 | loop fusion | flops 9732096 | bytes 562058 | tf_op jit(solution)/shard_map/convert_element_type | solution.py:120
  30.4 6.8 %select_convert_fusion.2.refs_13_ = bf16[512,256]{1,0:T(8,128)(2,1)S(1)} fusion(bf16[]{:T(256)} %bitcast.38, bf16[]{:T(256)} %bitcast.37, bf16[]{:T(256)} %bitcast.36, bf16[]{:T(256)} %bitcast.35, bf16[]{:T(256)} %bitcast.34, bf16[]{:T(256)} %bitcast.33, bf16[]{:T(256)} %bitcast.32, bf16[]{:T(256)} %bitcast.31, bf16[]{:T(256)} %bitcast.30, ...), kind=kLoop, calls=%fused_computation.14 | loop fusion | flops 4063232 | bytes 275986 | tf_op jit(solution)/shard_map/convert_element_type | solution.py:120
  37.3 6.7 %select_convert_fusion.3.refs_12_ = bf16[512,256]{1,0:T(8,128)(2,1)S(1)} fusion(bf16[]{:T(256)} %bitcast.29, bf16[]{:T(256)} %bitcast.28, bf16[]{:T(256)} %bitcast.27, bf16[]{:T(256)} %bitcast.26, bf16[]{:T(256)} %bitcast.25, bf16[]{:T(256)} %bitcast.24, bf16[]{:T(256)} %bitcast.23, bf16[]{:T(256)} %bitcast.22, bf16[]{:T(256)} %bitcast.21, ...), kind=kLoop, calls=%fused_computation.15 | loop fusion | flops 4063232 | bytes 275986 | tf_op jit(solution)/shard_map/convert_element_type | solution.py:120
  43.9 0.7 constant_dynamic-update-slice_fusion.3
  44.6 3.4 %collective-permute-start.9 = (bf16[128,1024]{1,0:T(8,128)(2,1)S(1)}, bf16[128,1024]{1,0:T(8,128)(2,1)S(1)}, u32[]{:S(2)}, u32[]{:S(2)}) collective-permute-start(bf16[128,1024]{1,0:T(8,128)(2,1)S(1)} %pad_maximum_fusion.1), channel_id=1, source_target_pairs={{0,4},{2,6},{4,0},{6,2},{8,12},{10,14},{12,8},{14,10},{1,5},{3,7},... | collective-permute-start | bytes 786440 | tf_op jit(solution)/shard_map/ppermute | solution.py:223
  48.2 1.0 collective-permute-start.2
  49.2 2.1 %collective-permute-start.1 = (bf16[64,1280]{1,0:T(8,128)(2,1)}, bf16[64,1280]{1,0:T(8,128)(2,1)S(1)}, u32[]{:S(2)}, u32[]{:S(2)}) collective-permute-start(bf16[64,1280]{1,0:T(8,128)(2,1)} %get-tuple-element.24), channel_id=1, source_target_pairs={{0,4},{2,6},{4,0},{6,2},{8,12},{10,14},{12,8},{14,10},{1,5},{3,7},... | collective-permute-start | bytes 491528 | tf_op jit(solution)/shard_map/ppermute | solution.py:243
  51.3 4.0 %collective-permute-done.9 = bf16[128,1024]{1,0:T(8,128)(2,1)S(1)} collective-permute-done((bf16[128,1024]{1,0:T(8,128)(2,1)S(1)}, bf16[128,1024]{1,0:T(8,128)(2,1)S(1)}, u32[]{:S(2)}, u32[]{:S(2)}) %collective-permute-start.9) | collective-permute-done | bytes 262176 | tf_op jit(solution)/shard_map/ppermute | solution.py:223
  55.3 1.5 %collective-permute-start = (bf16[64,1280]{1,0:T(8,128)(2,1)S(1)}, bf16[64,1280]{1,0:T(8,128)(2,1)S(1)}, u32[]{:S(2)}, u32[]{:S(2)}) collective-permute-start(bf16[64,1280]{1,0:T(8,128)(2,1)S(1)} %copy-done.6), channel_id=1, source_target_pairs={{0,2},{2,0},{4,6},{6,4},{8,10},{10,8},{12,14},{14,12},{1,3},{3,1},... | collective-permute-start | bytes 491528 | tf_op jit(solution)/shard_map/ppermute | solution.py:243
  56.8 0.8 pad_maximum_fusion
  57.7 0.7 collective-permute-start.10
  58.4 0.9 collective-permute-done.2.refs_4_
  59.3 0.7 collective-permute-done.1.refs_3_
  60.0 2.8 %collective-permute-done.refs_2_ = bf16[64,1280]{1,0:T(8,128)(2,1)S(1)} collective-permute-done((bf16[64,1280]{1,0:T(8,128)(2,1)S(1)}, bf16[64,1280]{1,0:T(8,128)(2,1)S(1)}, u32[]{:S(2)}, u32[]{:S(2)}) %collective-permute-start) | collective-permute-done | bytes 163872 | tf_op jit(solution)/shard_map/ppermute | solution.py:243
  63.0 7.8 %collective-permute-done.10 = bf16[256,1024]{1,0:T(8,128)(2,1)} collective-permute-done((bf16[256,1024]{1,0:T(8,128)(2,1)}, bf16[256,1024]{1,0:T(8,128)(2,1)}, u32[]{:S(2)}, u32[]{:S(2)}) %collective-permute-start.10) | collective-permute-done | bytes 524320 | tf_op jit(solution)/shard_map/ppermute | solution.py:223
  70.8 1.6 %slice_dynamic-update-slice_fusion.3 = bf16[512,1024]{1,0:T(8,128)(2,1)} fusion(bf16[512,1024]{1,0:T(8,128)(2,1)} %constant_dynamic-update-slice_fusion.3, bf16[256,1024]{1,0:T(8,128)(2,1)} %collective-permute-done.10), kind=kLoop, calls=%fused_computation.38 | loop fusion | bytes 262144
  72.4 1.6 %constant_dynamic-update-slice_fusion.2 = bf16[512,1024]{1,0:T(8,128)(2,1)} fusion(bf16[512,1024]{1,0:T(8,128)(2,1)} %slice_dynamic-update-slice_fusion.3, bf16[128,1024]{1,0:T(8,128)(2,1)} %copy-done.4), kind=kLoop, calls=%fused_computation.41 | loop fusion | bytes 262144
  74.0 1.6 %slice_dynamic-update-slice_fusion.2 = bf16[512,1024]{1,0:T(8,128)(2,1)} fusion(bf16[512,1024]{1,0:T(8,128)(2,1)} %constant_dynamic-update-slice_fusion.2, bf16[256,1024]{1,0:T(8,128)(2,1)} %collective-permute-done.10), kind=kLoop, calls=%fused_computation.37 | loop fusion | bytes 262144
  75.5 0.7 constant_dynamic-update-slice_fusion.1
  76.2 1.6 %slice_dynamic-update-slice_fusion.1 = bf16[512,1024]{1,0:T(8,128)(2,1)} fusion(bf16[512,1024]{1,0:T(8,128)(2,1)} %constant_dynamic-update-slice_fusion.1, bf16[256,1024]{1,0:T(8,128)(2,1)} %collective-permute-done.10), kind=kLoop, calls=%fused_computation.36 | loop fusion | bytes 262144
  77.8 0.7 constant_dynamic-update-slice_fusion
  78.4 1.6 %slice_dynamic-update-slice_fusion = bf16[512,1024]{1,0:T(8,128)(2,1)} fusion(bf16[512,1024]{1,0:T(8,128)(2,1)} %constant_dynamic-update-slice_fusion, bf16[256,1024]{1,0:T(8,128)(2,1)} %collective-permute-done.10), kind=kLoop, calls=%fused_computation.35 | loop fusion | bytes 262144 | tf_op jit(solution)/shard_map/concatenate | solution.py:226
  80.1 2.2 %copy-done = bf16[2048,1024]{1,0:T(8,128)(2,1)S(1)} copy-done((bf16[2048,1024]{1,0:T(8,128)(2,1)S(1)}, bf16[2048,1024]{1,0:T(8,128)(2,1)}, u32[]{:S(2)}) %copy-start) | copy-done | bytes 4194328
  82.3 4.9 %tile_kernel.1 = (bf16[512,512]{1,0:T(8,128)(2,1)S(1)}, bf16[512,512]{1,0:T(8,128)(2,1)S(1)}, f32[64,1024]{1,0:T(8,128)S(1)}, bf16[64,1024]{1,0:T(8,128)(2,1)S(1...) custom-call(s32[2]{0:T(128)S(1)} %pad_add_fusion.refs_0_, ...), custom_call_target="tpu_custom_call" | custom-call | flops 3254779904 | bytes 7340032 | tf_op jit(solution)/shard_map/tile_kernel/pallas_call | solution.py:194
  87.2 2.0 %collective-permute-start.13 = (bf16[64,1024]{1,0:T(8,128)(2,1)S(1)}, bf16[64,1024]{1,0:T(8,128)(2,1)S(1)}, u32[]{:S(2)}, u32[]{:S(2)}) collective-permute-start(bf16[64,1024]{1,0:T(8,128)(2,1)S(1)} %get-tuple-element.15), channel_id=1, source_target_pairs={{0,14},{2,12},{4,10},{6,8},{8,6},{10,4},{12,2},{14,0},{1,15},{3,13... | collective-permute-start | bytes 393224 | tf_op jit(solution)/shard_map/ppermute | solution.py:243
  89.2 0.2 collective-permute-start.11
  89.4 2.3 %collective-permute-start.14 = (bf16[64,1024]{1,0:T(8,128)(2,1)S(1)}, bf16[64,1024]{1,0:T(8,128)(2,1)S(1)}, u32[]{:S(2)}, u32[]{:S(2)}) collective-permute-start(bf16[64,1024]{1,0:T(8,128)(2,1)S(1)} %get-tuple-element.16), channel_id=1, source_target_pairs={{0,12},{2,14},{4,8},{6,10},{8,4},{10,6},{12,0},{14,2},{1,13},{3,15... | collective-permute-start | bytes 393224 | tf_op jit(solution)/shard_map/ppermute | solution.py:243
  91.7 4.6 %collective-permute-done.13 = bf16[64,1024]{1,0:T(8,128)(2,1)S(1)} collective-permute-done((bf16[64,1024]{1,0:T(8,128)(2,1)S(1)}, bf16[64,1024]{1,0:T(8,128)(2,1)S(1)}, u32[]{:S(2)}, u32[]{:S(2)}) %collective-permute-start.13) | collective-permute-done | bytes 131104 | tf_op jit(solution)/shard_map/ppermute | solution.py:243
  96.3 7.1 %collective-permute-start.16 = (bf16[64,1024]{1,0:T(8,128)(2,1)S(1)}, bf16[64,1024]{1,0:T(8,128)(2,1)S(1)}, u32[]{:S(2)}, u32[]{:S(2)}) collective-permute-start(bf16[64,1024]{1,0:T(8,128)(2,1)S(1)} %get-tuple-element.18), channel_id=1, source_target_pairs={{0,8},{2,10},{4,12},{6,14},{8,0},{10,2},{12,4},{14,6},{1,9},{3,11}... | collective-permute-start | bytes 393224 | tf_op jit(solution)/shard_map/ppermute | solution.py:243
  103.4 3.7 %collective-permute-start.17 = (bf16[64,1024]{1,0:T(8,128)(2,1)S(1)}, bf16[64,1024]{1,0:T(8,128)(2,1)S(1)}, u32[]{:S(2)}, u32[]{:S(2)}) collective-permute-start(bf16[64,1024]{1,0:T(8,128)(2,1)S(1)} %get-tuple-element.19), channel_id=1, source_target_pairs={{0,6},{2,4},{4,2},{6,0},{8,14},{10,12},{12,10},{14,8},{1,7},{3,5},... | collective-permute-start | bytes 393224 | tf_op jit(solution)/shard_map/ppermute | solution.py:243
  107.1 5.1 %collective-permute-done.15 = bf16[64,1024]{1,0:T(8,128)(2,1)S(1)} collective-permute-done((bf16[64,1024]{1,0:T(8,128)(2,1)S(1)}, bf16[64,1024]{1,0:T(8,128)(2,1)S(1)}, u32[]{:S(2)}, u32[]{:S(2)}) %collective-permute-start.15) | collective-permute-done | bytes 131104 | tf_op jit(solution)/shard_map/ppermute | solution.py:243
  112.2 2.0 %collective-permute-done.16 = bf16[64,1024]{1,0:T(8,128)(2,1)S(1)} collective-permute-done((bf16[64,1024]{1,0:T(8,128)(2,1)S(1)}, bf16[64,1024]{1,0:T(8,128)(2,1)S(1)}, u32[]{:S(2)}, u32[]{:S(2)}) %collective-permute-start.16) | collective-permute-done | bytes 131104 | tf_op jit(solution)/shard_map/ppermute | solution.py:243
  114.2 1.0 collective-permute-start.19
  115.2 2.0 %collective-permute-done.18 = bf16[64,1024]{1,0:T(8,128)(2,1)S(1)} collective-permute-done((bf16[64,1024]{1,0:T(8,128)(2,1)S(1)}, bf16[64,1024]{1,0:T(8,128)(2,1)S(1)}, u32[]{:S(2)}, u32[]{:S(2)}) %collective-permute-start.18) | collective-permute-done | bytes 131104 | tf_op jit(solution)/shard_map/ppermute | solution.py:243
  117.2 2.1 %collective-permute-done.19 = bf16[64,1024]{1,0:T(8,128)(2,1)S(1)} collective-permute-done((bf16[64,1024]{1,0:T(8,128)(2,1)S(1)}, bf16[64,1024]{1,0:T(8,128)(2,1)S(1)}, u32[]{:S(2)}, u32[]{:S(2)}) %collective-permute-start.19) | collective-permute-done | bytes 131104 | tf_op jit(solution)/shard_map/ppermute | solution.py:243
  119.3 0.9 multiply_bitcast_fusion
  120.2 0.7 fusion.37
  120.9 0.5 copy-done.2
  121.4 2.0 %add_multiply_fusion = f32[512,1024]{1,0:T(8,128)} fusion(f32[512,1024]{1,0:T(8,128)S(1)} %fusion.37, bf16[512,512]{1,0:T(8,128)(2,1)S(1)} %get-tuple-element.12, bf16[512,1024]{1,0:T(8,128)(2,1)S(1)} %copy-done.2), kind=kOutput, calls=%fused_computation | convolution fusion | flops 537919488 | bytes 5767168 | tf_op jit(solution)/shard_map/dot_general | solution.py:287
  (59 shorter events, 0.6 us)
Async XLA Ops:
  0.6 11.3 %copy-start.3 = (bf16[1,64,1024]{2,1,0:T(8,128)(2,1)S(1)}, bf16[1,64,1024]{2,1,0:T(8,128)(2,1)}, u32[]{:S(2)}) copy-start(bf16[1,64,1024]{2,1,0:T(8,128)(2,1)} %param.7) | copy-start | bytes 393220
  0.6 12.4 %copy-start.7 = (f32[3,3]{1,0:T(4,128)S(1)}, f32[3,3]{1,0:T(4,128)}, u32[]{:S(2)}) copy-start(f32[3,3]{1,0:T(4,128)} %param.9) | copy-start | bytes 112
  0.7 12.5 %copy-start.8 = (f32[3,3]{1,0:T(4,128)S(1)}, f32[3,3]{1,0:T(4,128)}, u32[]{:S(2)}) copy-start(f32[3,3]{1,0:T(4,128)} %param.8) | copy-start | bytes 112
  3.0 45.1 %collective-permute-start.6 = (bf16[64,1280]{1,0:T(8,128)(2,1)S(1)}, bf16[64,1280]{1,0:T(8,128)(2,1)S(1)}, u32[]{:S(2)}, u32[]{:S(2)}) collective-permute-start(bf16[64,1280]{1,0:T(8,128)(2,1)S(1)} %get-tuple-element.22), channel_id=1, source_target_pairs={{0,14},{2,12},{4,10},{6,8},{8,6},{10,4},{12,2},{14,0},{1,15},{3,13... | collective-permute-start | bytes 491528 | tf_op jit(solution)/shard_map/ppermute | solution.py:243
  9.0 40.2 %collective-permute-start.5 = (bf16[64,1280]{1,0:T(8,128)(2,1)S(1)}, bf16[64,1280]{1,0:T(8,128)(2,1)S(1)}, u32[]{:S(2)}, u32[]{:S(2)}) collective-permute-start(bf16[64,1280]{1,0:T(8,128)(2,1)S(1)} %get-tuple-element.28), channel_id=1, source_target_pairs={{0,12},{2,14},{4,8},{6,10},{8,4},{10,6},{12,0},{14,2},{1,13},{3,15... | collective-permute-start | bytes 491528 | tf_op jit(solution)/shard_map/ppermute | solution.py:243
  9.2 48.4 %collective-permute-start.4 = (bf16[64,1280]{1,0:T(8,128)(2,1)}, bf16[64,1280]{1,0:T(8,128)(2,1)S(1)}, u32[]{:S(2)}, u32[]{:S(2)}) collective-permute-start(bf16[64,1280]{1,0:T(8,128)(2,1)} %get-tuple-element.27), channel_id=1, source_target_pairs={{0,10},{2,8},{4,14},{6,12},{8,2},{10,0},{12,6},{14,4},{1,11},{3,9}... | collective-permute-start | bytes 491528 | tf_op jit(solution)/shard_map/ppermute | solution.py:243
  10.0 48.4 %collective-permute-start.3 = (bf16[64,1280]{1,0:T(8,128)(2,1)}, bf16[64,1280]{1,0:T(8,128)(2,1)S(1)}, u32[]{:S(2)}, u32[]{:S(2)}) collective-permute-start(bf16[64,1280]{1,0:T(8,128)(2,1)} %get-tuple-element.26), channel_id=1, source_target_pairs={{0,8},{2,10},{4,12},{6,14},{8,0},{10,2},{12,4},{14,6},{1,9},{3,11}... | collective-permute-start | bytes 491528 | tf_op jit(solution)/shard_map/ppermute | solution.py:243
  12.0 32.6 %collective-permute-start.8 = (bf16[64,1024]{1,0:T(8,128)(2,1)S(1)}, bf16[64,1024]{1,0:T(8,128)(2,1)S(1)}, u32[]{:S(2)}, u32[]{:S(2)}) collective-permute-start(bf16[64,1024]{1,0:T(8,128)(2,1)S(1)} %bitcast.49), channel_id=1, source_target_pairs={{0,8},{2,10},{4,12},{6,14},{8,0},{10,2},{12,4},{14,6},{1,9},{3,11}... | collective-permute-start | bytes 393224 | tf_op jit(solution)/shard_map/ppermute | solution.py:223
  14.6 33.5 %copy-start.1 = (bf16[1,64,8192]{2,1,0:T(8,128)(2,1)S(1)}, bf16[1,64,8192]{2,1,0:T(8,128)(2,1)}, u32[]{:S(2)}) copy-start(bf16[1,64,8192]{2,1,0:T(8,128)(2,1)} %param.5) | copy-start | bytes 3145732
  30.4 24.9 %copy-start.6 = (bf16[64,1280]{1,0:T(8,128)(2,1)S(1)}, bf16[64,1280]{1,0:T(8,128)(2,1)}, u32[]{:S(2)}) copy-start(bf16[64,1280]{1,0:T(8,128)(2,1)} %get-tuple-element.23) | copy-start | bytes 491524
  44.6 10.7 %collective-permute-start.9 = (bf16[128,1024]{1,0:T(8,128)(2,1)S(1)}, bf16[128,1024]{1,0:T(8,128)(2,1)S(1)}, u32[]{:S(2)}, u32[]{:S(2)}) collective-permute-start(bf16[128,1024]{1,0:T(8,128)(2,1)S(1)} %pad_maximum_fusion.1), channel_id=1, source_target_pairs={{0,4},{2,6},{4,0},{6,2},{8,12},{10,14},{12,8},{14,10},{1,5},{3,7},... | collective-permute-start | bytes 786440 | tf_op jit(solution)/shard_map/ppermute | solution.py:223
  48.2 11.1 %collective-permute-start.2 = (bf16[64,1280]{1,0:T(8,128)(2,1)}, bf16[64,1280]{1,0:T(8,128)(2,1)S(1)}, u32[]{:S(2)}, u32[]{:S(2)}) collective-permute-start(bf16[64,1280]{1,0:T(8,128)(2,1)} %get-tuple-element.25), channel_id=1, source_target_pairs={{0,6},{2,4},{4,2},{6,0},{8,14},{10,12},{12,10},{14,8},{1,7},{3,5},... | collective-permute-start | bytes 491528 | tf_op jit(solution)/shard_map/ppermute | solution.py:243
  49.2 10.8 %collective-permute-start.1 = (bf16[64,1280]{1,0:T(8,128)(2,1)}, bf16[64,1280]{1,0:T(8,128)(2,1)S(1)}, u32[]{:S(2)}, u32[]{:S(2)}) collective-permute-start(bf16[64,1280]{1,0:T(8,128)(2,1)} %get-tuple-element.24), channel_id=1, source_target_pairs={{0,4},{2,6},{4,0},{6,2},{8,12},{10,14},{12,8},{14,10},{1,5},{3,7},... | collective-permute-start | bytes 491528 | tf_op jit(solution)/shard_map/ppermute | solution.py:243
  55.3 1.5 %copy-start.4 = (bf16[128,1024]{1,0:T(8,128)(2,1)}, bf16[128,1024]{1,0:T(8,128)(2,1)S(1)}, u32[]{:S(2)}) copy-start(bf16[128,1024]{1,0:T(8,128)(2,1)S(1)} %collective-permute-done.9) | copy-start | bytes 786436
  55.3 7.5 %collective-permute-start = (bf16[64,1280]{1,0:T(8,128)(2,1)S(1)}, bf16[64,1280]{1,0:T(8,128)(2,1)S(1)}, u32[]{:S(2)}, u32[]{:S(2)}) collective-permute-start(bf16[64,1280]{1,0:T(8,128)(2,1)S(1)} %copy-done.6), channel_id=1, source_target_pairs={{0,2},{2,0},{4,6},{6,4},{8,10},{10,8},{12,14},{14,12},{1,3},{3,1},... | collective-permute-start | bytes 491528 | tf_op jit(solution)/shard_map/ppermute | solution.py:243
  57.7 13.2 %collective-permute-start.10 = (bf16[256,1024]{1,0:T(8,128)(2,1)}, bf16[256,1024]{1,0:T(8,128)(2,1)}, u32[]{:S(2)}, u32[]{:S(2)}) collective-permute-start(bf16[256,1024]{1,0:T(8,128)(2,1)} %pad_maximum_fusion), channel_id=1, source_target_pairs={{0,2},{2,0},{4,6},{6,4},{8,10},{10,8},{12,14},{14,12},{1,3},{3,1},... | collective-permute-start | bytes 1572872 | tf_op jit(solution)/shard_map/ppermute | solution.py:223
  62.9 14.8 %copy-start.5 = (bf16[128,1024]{1,0:T(8,128)(2,1)S(1)}, bf16[128,1024]{1,0:T(8,128)(2,1)}, u32[]{:S(2)}) copy-start(bf16[128,1024]{1,0:T(8,128)(2,1)} %copy-done.4) | copy-start | bytes 786436
  62.9 17.1 %collective-permute-start.7 = (bf16[16,1024]{1,0:T(8,128)(2,1)S(1)}, bf16[16,1024]{1,0:T(8,128)(2,1)S(1)}, u32[]{:S(2)}, u32[]{:S(2)}) collective-permute-start(bf16[16,1024]{1,0:T(8,128)(2,1)S(1)} %concatenate.12), channel_id=1, source_target_pairs={{0,1},{1,0},{2,3},{3,2},{4,5},{5,4},{6,7},{7,6},{8,9},{9,8},{10,11... | collective-permute-start | bytes 98312 | tf_op jit(solution)/shard_map/ppermute | solution.py:269
  80.0 40.1 %collective-permute-start.12 = (bf16[512,1024]{1,0:T(8,128)(2,1)}, bf16[512,1024]{1,0:T(8,128)(2,1)S(1)}, u32[]{:S(2)}, u32[]{:S(2)}) collective-permute-start(bf16[512,1024]{1,0:T(8,128)(2,1)} %slice_dynamic-update-slice_fusion), channel_id=1, source_target_pairs={{0,1},{1,0},{2,3},{3,2},{4,5},{5,4},{6,7},{7,6},{8,9},{9,8},{10,11... | collective-permute-start | bytes 3145736 | tf_op jit(solution)/shard_map/ppermute | solution.py:260
  80.1 2.2 %copy-start = (bf16[2048,1024]{1,0:T(8,128)(2,1)S(1)}, bf16[2048,1024]{1,0:T(8,128)(2,1)}, u32[]{:S(2)}) copy-start(bf16[2048,1024]{1,0:T(8,128)(2,1)} %refs_14_.1) | copy-start | bytes 12582916
  87.2 9.2 %collective-permute-start.13 = (bf16[64,1024]{1,0:T(8,128)(2,1)S(1)}, bf16[64,1024]{1,0:T(8,128)(2,1)S(1)}, u32[]{:S(2)}, u32[]{:S(2)}) collective-permute-start(bf16[64,1024]{1,0:T(8,128)(2,1)S(1)} %get-tuple-element.15), channel_id=1, source_target_pairs={{0,14},{2,12},{4,10},{6,8},{8,6},{10,4},{12,2},{14,0},{1,15},{3,13... | collective-permute-start | bytes 393224 | tf_op jit(solution)/shard_map/ppermute | solution.py:243
  89.2 31.0 %collective-permute-start.11 = (bf16[512,512]{1,0:T(8,128)(2,1)S(1)}, bf16[512,512]{1,0:T(8,128)(2,1)S(1)}, u32[]{:S(2)}, u32[]{:S(2)}) collective-permute-start(bf16[512,512]{1,0:T(8,128)(2,1)S(1)} %get-tuple-element.13), channel_id=1, source_target_pairs={{0,1},{1,0},{2,3},{3,2},{4,5},{5,4},{6,7},{7,6},{8,9},{9,8},{10,11... | collective-permute-start | bytes 1572872 | tf_op jit(solution)/shard_map/ppermute | solution.py:284
  89.4 14.0 %collective-permute-start.14 = (bf16[64,1024]{1,0:T(8,128)(2,1)S(1)}, bf16[64,1024]{1,0:T(8,128)(2,1)S(1)}, u32[]{:S(2)}, u32[]{:S(2)}) collective-permute-start(bf16[64,1024]{1,0:T(8,128)(2,1)S(1)} %get-tuple-element.16), channel_id=1, source_target_pairs={{0,12},{2,14},{4,8},{6,10},{8,4},{10,6},{12,0},{14,2},{1,13},{3,15... | collective-permute-start | bytes 393224 | tf_op jit(solution)/shard_map/ppermute | solution.py:243
  91.7 20.4 %collective-permute-start.15 = (bf16[64,1024]{1,0:T(8,128)(2,1)S(1)}, bf16[64,1024]{1,0:T(8,128)(2,1)S(1)}, u32[]{:S(2)}, u32[]{:S(2)}) collective-permute-start(bf16[64,1024]{1,0:T(8,128)(2,1)S(1)} %get-tuple-element.17), channel_id=1, source_target_pairs={{0,10},{2,8},{4,14},{6,12},{8,2},{10,0},{12,6},{14,4},{1,11},{3,9}... | collective-permute-start | bytes 393224 | tf_op jit(solution)/shard_map/ppermute | solution.py:243
  96.3 17.8 %collective-permute-start.16 = (bf16[64,1024]{1,0:T(8,128)(2,1)S(1)}, bf16[64,1024]{1,0:T(8,128)(2,1)S(1)}, u32[]{:S(2)}, u32[]{:S(2)}) collective-permute-start(bf16[64,1024]{1,0:T(8,128)(2,1)S(1)} %get-tuple-element.18), channel_id=1, source_target_pairs={{0,8},{2,10},{4,12},{6,14},{8,0},{10,2},{12,4},{14,6},{1,9},{3,11}... | collective-permute-start | bytes 393224 | tf_op jit(solution)/shard_map/ppermute | solution.py:243
  103.4 11.8 %collective-permute-start.17 = (bf16[64,1024]{1,0:T(8,128)(2,1)S(1)}, bf16[64,1024]{1,0:T(8,128)(2,1)S(1)}, u32[]{:S(2)}, u32[]{:S(2)}) collective-permute-start(bf16[64,1024]{1,0:T(8,128)(2,1)S(1)} %get-tuple-element.19), channel_id=1, source_target_pairs={{0,6},{2,4},{4,2},{6,0},{8,14},{10,12},{12,10},{14,8},{1,7},{3,5},... | collective-permute-start | bytes 393224 | tf_op jit(solution)/shard_map/ppermute | solution.py:243
  112.2 5.0 %collective-permute-start.18 = (bf16[64,1024]{1,0:T(8,128)(2,1)S(1)}, bf16[64,1024]{1,0:T(8,128)(2,1)S(1)}, u32[]{:S(2)}, u32[]{:S(2)}) collective-permute-start(bf16[64,1024]{1,0:T(8,128)(2,1)S(1)} %get-tuple-element.20), channel_id=1, source_target_pairs={{0,4},{2,6},{4,0},{6,2},{8,12},{10,14},{12,8},{14,10},{1,5},{3,7},... | collective-permute-start | bytes 393224 | tf_op jit(solution)/shard_map/ppermute | solution.py:243
  114.2 5.1 %collective-permute-start.19 = (bf16[64,1024]{1,0:T(8,128)(2,1)S(1)}, bf16[64,1024]{1,0:T(8,128)(2,1)S(1)}, u32[]{:S(2)}, u32[]{:S(2)}) collective-permute-start(bf16[64,1024]{1,0:T(8,128)(2,1)S(1)} %get-tuple-element.21), channel_id=1, source_target_pairs={{0,2},{2,0},{4,6},{6,4},{8,10},{10,8},{12,14},{14,12},{1,3},{3,1},... | collective-permute-start | bytes 393224 | tf_op jit(solution)/shard_map/ppermute | solution.py:243
  120.2 1.2 copy-start.2

commit v2 on v1

--- a/solution.py
+++ b/solution.py
@@ -111,40 +111,113 @@
     return high, kernel - high
 
 
-def tap_matrix(taps, row_step, col_step):
-    total = jnp.zeros(row_step.shape, jnp.float32)
-    for a in range(3):
-        for b in range(3):
-            hit = (row_step == a - 1) & (col_step == b - 1)
-            total = jnp.where(hit, taps[a, b], total)
-    return total.astype(jnp.bfloat16)
-
-
-def query_matrices(kernel):
-    shape = (4 * QW, 2 * QW)
-    source = lax.broadcasted_iota(jnp.int32, shape, 0)
-    target = lax.broadcasted_iota(jnp.int32, shape, 1)
-    row_step = source // QW - target // QW - 1
-    col_step = source % QW - target % QW
-    return [tap_matrix(taps, row_step, col_step) for taps in split_taps(kernel)]
-
-
-def support_matrices(kernel, own, core, count, columns, edge):
+def banded(taps, step):
+    total = jnp.where(step == 1, taps[2], 0.0)
+    return jnp.where(step == 0, taps[1], jnp.where(step == -1, taps[0], total))
+
+
+def matrix_kernel(count, columns, place_ref, taps_ref, th_ref, tl_ref, wh_ref, wl_ref):
+    own = place_ref[0]
+    beside = jnp.where(place_ref[1] == 0, columns, -1)
     cells = count * columns
-    shape = (cells, cells + edge)
-    target = lax.broadcasted_iota(jnp.int32, shape, 0)
-    source = lax.broadcasted_iota(jnp.int32, shape, 1)
-    rim = source >= cells
-    slot = jnp.where(rim, source - cells, source // columns)
-    beside = jnp.where(core == 0, columns, -1)
-    column = jnp.where(rim, beside, source % columns)
-    row_step = (own ^ slot) - (own ^ (target // columns))
-    row_step = jnp.where(slot < count, row_step, 2)
-    col_step = column - target % columns
-    return [tap_matrix(taps, row_step, col_step) for taps in split_taps(kernel)]
-
-
-def tile_kernel(count, columns, tile, edge, width, *refs):
+
+    def taps(part, kernel, a, b):
+        return taps_ref[((part * 2 + kernel) * 3 + a) * 3 + b]
+
+    def span(shape, dim):
+        return lax.broadcasted_iota(jnp.int32, shape, dim)
+
+    square = (QW, QW)
+    step = span(square, 0) - span(square, 1)
+    for part, w_ref in enumerate((wh_ref, wl_ref)):
+        bands = [
+            banded([taps(part, 0, a, b) for b in range(3)], step).astype(jnp.bfloat16)
+            for a in range(3)
+        ]
+        for source in range(4):
+            for target in range(2):
+                a = source - target
+                block = bands[a] if 0 <= a <= 2 else jnp.zeros(square, jnp.bfloat16)
+                w_ref[source * QW : (source + 1) * QW, target * QW : (target + 1) * QW] = block
+    edge = th_ref.shape[1] - cells
+    blocks = [(low, QW) for low in range(0, cells, QW)] + [(cells, edge)]
+    for low, lanes in blocks:
+        shape = (columns, lanes)
+        lane = span(shape, 1)
+        if low < cells:
+            slot = (lane + low) // columns
+            column = lax.rem(lane, columns)
+        else:
+            slot = lane
+            column = jnp.full(shape, beside, jnp.int32)
+        step = column - span(shape, 0)
+        plane = jnp.where(slot < count, own ^ slot, 2 * count)
+        for target in range(count):
+            rise = plane - (own ^ target)
+            for part, t_ref in enumerate((th_ref, tl_ref)):
+                row = [
+                    banded([taps(part, 1, a, b) for a in range(3)], rise) for b in range(3)
+                ]
+                t_ref[target * columns : (target + 1) * columns, low : low + lanes] = banded(
+                    row, step
+                ).astype(jnp.bfloat16)
+
+
+def matrix_call(place, query_kernel, support_kernel, count, columns, edge):
+    query_parts = split_taps(query_kernel)
+    support_parts = split_taps(support_kernel)
+    taps = jnp.stack(
+        [query_parts[0], support_parts[0], query_parts[1], support_parts[1]]
+    ).reshape(-1)
+    cells = count * columns
+    wide = jax.ShapeDtypeStruct((cells, cells + edge), jnp.bfloat16)
+    band = jax.ShapeDtypeStruct((4 * QW, 2 * QW), jnp.bfloat16)
+    return pl.pallas_call(
+        lambda *refs: matrix_kernel(count, columns, *refs),
+        out_shape=[wide, wide, band, band],
+        in_specs=[pl.BlockSpec(memory_space=pltpu.SMEM)] * 2,
+        out_specs=[pl.BlockSpec(memory_space=pltpu.VMEM)] * 4,
+        cost_estimate=pl.CostEstimate(
+            flops=20 * cells * cells, bytes_accessed=8 * cells * cells, transcendentals=0
+        ),
+        compiler_params=pltpu.CompilerParams(vmem_limit_bytes=4 << 20),
+        name="matrix_kernel",
+    )(place, taps)
+
+
+def rim_kernel(count, columns, tile, place_ref, *refs):
+    pieces, rim_ref = refs[:count], refs[count]
+    first = place_ref[1] != 0
+    inner = slice(QW, QW + tile)
+    rows = []
+    for piece in pieces:
+        head = piece[:16, inner].astype(jnp.float32)[:1]
+        tail = piece[columns - 16 :, inner].astype(jnp.float32)[15:]
+        rows.append(jnp.where(first, head, tail))
+    empty = rim_ref.shape[0] - count
+    if empty:
+        rows.append(jnp.zeros((empty, tile), jnp.float32))
+    rim_ref[...] = jnp.concatenate(rows, axis=0).astype(jnp.bfloat16)
+
+
+def rim_call(place, pieces, columns, tile, edge):
+    count = len(pieces)
+    return pl.pallas_call(
+        lambda *refs: rim_kernel(count, columns, tile, *refs),
+        out_shape=jax.ShapeDtypeStruct((edge, tile), jnp.bfloat16),
+        in_specs=[pl.BlockSpec(memory_space=pltpu.SMEM)]
+        + [pl.BlockSpec(memory_space=pltpu.VMEM)] * count,
+        out_specs=pl.BlockSpec(memory_space=pltpu.VMEM),
+        cost_estimate=pl.CostEstimate(
+            flops=count * tile, bytes_accessed=64 * count * tile, transcendentals=0
+        ),
+        compiler_params=pltpu.CompilerParams(vmem_limit_bytes=4 << 20),
+        name="rim_kernel",
+    )(place, *pieces)
+
+
+def tile_kernel(order, columns, tile, edge, width, *refs):
+    count = len(order)
     side_ref = refs[0]
     pieces = refs[1 : 1 + count]
     rim_ref, th_ref, tl_ref, wh_ref, wl_ref, feats_ref = refs[1 + count : 7 + count]
@@ -170,8 +243,11 @@
         total += jnp.dot(tl_ref[...], middle, preferred_element_type=jnp.float32)
         corr_ref[:, low : low + step] = total.astype(jnp.bfloat16)
     half = tile // 2
-    keep_ref[...] = corr_ref[:, pl.ds(pl.multiple_of(core * half, half), half)]
-    send_ref[...] = corr_ref[:, pl.ds(pl.multiple_of((1 - core) * half, half), half)]
+    for at, k in enumerate(order):
+        source, target = pl.ds(k * columns, columns), pl.ds(at * columns, columns)
+        for half_ref, which in ((keep_ref, core), (send_ref, 1 - core)):
+            start = pl.multiple_of(which * half, half)
+            half_ref[target, :] = corr_ref[source, pl.ds(start, half)]
     fetch.wait()
     for low in range(0, width, step):
         total = jnp.dot(
@@ -184,15 +260,16 @@
             )
 
 
-def tile_call(side, pieces, rim, support_mats, query_mats, feats, count, columns, tile):
+def tile_call(side, pieces, rim, support_mats, query_mats, feats, order, columns, tile):
     width = feats.shape[1]
+    count = len(order)
     edge = rim.shape[0]
     cells = count * columns
     vmem = pl.BlockSpec(memory_space=pltpu.VMEM)
     flops = 2 * cells * tile * (2 * (cells + edge) + 8 * QW + width)
     moved = 2 * (2 * cells * tile + 4 * cells * cells + tile * width + cells * width)
     return pl.pallas_call(
-        lambda *refs: tile_kernel(count, columns, tile, edge, width, *refs),
+        lambda *refs: tile_kernel(order, columns, tile, edge, width, *refs),
         out_shape=[
             jax.ShapeDtypeStruct((cells, tile // 2), jnp.bfloat16),
             jax.ShapeDtypeStruct((cells, tile // 2), jnp.bfloat16),
@@ -201,7 +278,7 @@
         + [jax.ShapeDtypeStruct((columns, width), jnp.bfloat16)] * (count - 1),
         in_specs=[pl.BlockSpec(memory_space=pltpu.SMEM)]
         + [vmem] * (count + 5)
-        + [pl.BlockSpec(memory_space=pl.ANY)],
+        + [pl.BlockSpec(memory_space=pltpu.HBM)],
         out_specs=[vmem] * (count + 2),
         scratch_shapes=[
             pltpu.VMEM((cells + edge, tile + 2 * QW), jnp.bfloat16),
@@ -209,21 +286,10 @@
             pltpu.VMEM((tile, width), jnp.bfloat16),
             pltpu.SemaphoreType.DMA,
         ],
-        compiler_params=pltpu.CompilerParams(vmem_limit_bytes=40 << 20),
+        compiler_params=pltpu.CompilerParams(vmem_limit_bytes=20 << 20),
         cost_estimate=pl.CostEstimate(flops=flops, bytes_accessed=moved, transcendentals=0),
         name="tile_kernel",
     )(side, *pieces, rim, *support_mats, *query_mats, feats)
-
-
-def gathered(feats, count, columns, bits):
-    held = {0: feats}
-    for bit in bits:
-        slots = sorted(held)
-        block = jnp.concatenate([held[k] for k in slots], axis=0) if len(slots) > 1 else held[0]
-        moved = lax.ppermute(block, ("blk", "sub"), [(i, i ^ bit) for i in range(count)])
-        for at, k in enumerate(slots):
-            held[k ^ bit] = moved[at * columns : (at + 1) * columns]
-    return jnp.concatenate([held[k] for k in range(count)], axis=0)
 
 
 def tile_shards(grad_volume, query_feats, support_feats, query_kernel, support_kernel):
@@ -233,6 +299,7 @@
     inner = lax.axis_size("sub")
     count = outer * inner
     tile = queries // count
+    cells = count * columns
     scale_factor = 1.0 / math.sqrt(width)
     own = lax.axis_index(("blk", "sub"))
     side = lax.axis_index("sub")
@@ -251,34 +318,35 @@
     for mask in range(count - 1, 0, -1):
         pieces[mask] = exchanged(piece(mask), mask)
 
-    bits = []
+    feats_near = support_feats[0]
+    order = [0]
     bit = count // 2
-    while bit:
-        bits.append(bit)
+    while bit > 1:
+        feats_near = jnp.concatenate([feats_near, exchanged(feats_near, bit)])
+        order += [k ^ bit for k in order]
         bit //= 2
-    feats_own = gathered(support_feats[0], count, columns, bits)
-    feats_other = lax.ppermute(feats_own, "pair", swap)
+    order += [k ^ 1 for k in order]
+    feats_far = exchanged(feats_near, 1)
+    near_other = lax.ppermute(feats_near, "pair", swap)
 
     edge = 16 * -(-count // 16)
-    border = jnp.where(core == 0, columns - 1, 0)
-    rim = jnp.concatenate(
-        [lax.dynamic_slice(cell, (border, QW), (1, tile)) for cell in pieces]
-        + [jnp.zeros((edge - count, tile), jnp.bfloat16)],
-        axis=0,
-    )
-    rim = lax.ppermute(rim, "pair", swap)
+    place = jnp.stack([own, core]).astype(jnp.int32)
+    rim = lax.ppermute(rim_call(place, pieces, columns, tile, edge), "pair", swap)
+    mats = matrix_call(place, query_kernel, support_kernel, count, columns, edge)
     outs = tile_call(
         jnp.stack([side, core]).astype(jnp.int32),
         pieces,
         rim,
-        support_matrices(support_kernel, own, core, count, columns, edge),
-        query_matrices(query_kernel),
+        mats[:2],
+        mats[2:],
         query_feats,
-        count,
+        order,
         columns,
         tile,
     )
     keep, send, support_own = outs[:3]
+    feats_far, keep = lax.optimization_barrier((feats_far, keep))
+    far_other = lax.ppermute(feats_far, "pair", swap)
     parts = outs[3:]
     landed = [exchanged(parts[mask - 1], mask) for mask in range(count - 1, 0, -1)]
     other = lax.ppermute(send, "pair", swap)
@@ -288,7 +356,13 @@
             block, feats, (((0,), (0,)), ((), ())), preferred_element_type=jnp.float32
         )
 
-    query_grad = (query_term(keep, feats_own) + query_term(other, feats_other)) * scale_factor
+    near = cells // 2
+    query_grad = query_term(keep[:near], feats_near)
+    query_grad += query_term(other[:near], near_other)
+    query_grad += query_term(keep[near:], feats_far)
+    query_grad += query_term(other[near:], far_other)
+    query_grad *= scale_factor
+    landed, query_grad = lax.optimization_barrier((landed, query_grad))
     support_grad = support_own
     for term in landed:
         support_grad = support_grad + term.astype(jnp.float32)
@@ -306,6 +380,8 @@
         and count & (count - 1) == 0
         and count * columns <= 1024
         and columns % 16 == 0
+        and QW % columns == 0
+        and count * columns % QW == 0
         and QH * QW % (count * 2 * QW) == 0
     )
 

time: 124 us -> 83.9 us (0.68)
  other arithmetic: 31.2 us -> 1.08 us
  local copies, waits for them, and re-layouts: 16.6 us -> 3.82 us
  starting transfers between devices: 35 us -> 38.5 us
  waiting for transfers between devices: 32 us -> 28.5 us
  Pallas kernels: 4.89 us -> 6.82 us
    convert_element_type x4 -> x0, other arithmetic: 29.3 us -> none  [tap_matrix(): return total.astype(jnp.bfloat16)]
    ppermute x5 -> x3, waiting for transfers between devices: 11.8 us -> 1.07 us  [the longest x1 1.06 us: tile_shards(): lax.ppermute(rim_call(place, pieces, columns, tile, edge), 'pair', swap)]
    unnamed x25 -> x8, local copies, waits for them, and re-layouts: 11 us -> 2.2 us
    ppermute x14 -> x17, starting transfers between devices: 29.6 us -> 37.8 us  [exchanged(): lax.ppermute(value, ('blk', 'sub'), [(i, i ^ mask) for i in range(count)])]
    ppermute x14 -> x17, waiting for transfers between devices: 20.2 us -> 27.4 us  [exchanged(): lax.ppermute(value, ('blk', 'sub'), [(i, i ^ mask) for i in range(count)])]
    ppermute x5 -> x3, starting transfers between devices: 5.17 us -> 0.45 us  [the longest x1 0.35 us: tile_shards(): near_other = lax.ppermute(feats_near, 'pair', swap)]
    pallas_call x1 -> x3, Pallas kernels: 4.89 us -> 6.82 us  [the longest x1 4.89 us: tile_call(): pl.pallas_call(lambda *refs: tile_kernel(order, columns, tile, edge, widt...]
    concatenate x2 -> x0, local copies, waits for them, and re-layouts: 1.63 us -> none  [the longest x1 1.57 us: gathered(): return jnp.concatenate([held[k] for k in range(count)], axis=0)]
  transfers between devices with their start and end apart: 20 -> 21, of which waited for: 10 -> 6; matrix products, arithmetic and copies ran while one was open for 35% -> 4% of each run, Pallas kernels for 4% -> 8%
where the time goes in v2:
time: 83.9 us; the launch traced here: 82.8 us
  starting transfers between devices  38.5 us (46%)
  waiting for transfers between devices  28.5 us (34%)
  Pallas kernels  6.82 us (8%)
  local copies, waits for them, and re-layouts  3.82 us (5%)
  matrix products  3.19 us (4%)
  other arithmetic  1.08 us (1%)
    ppermute x17, starting transfers between devices, exchanged(): lax.ppermute(value, ('blk', 'sub'), [(i, i ^ mask) for i in range(count)])  37.8 us
    ppermute x17, waiting for transfers between devices, exchanged(): lax.ppermute(value, ('blk', 'sub'), [(i, i ^ mask) for i in range(count)])  27.4 us
    pallas_call x1, Pallas kernels, tile_call(): pl.pallas_call(lambda *refs: tile_kernel(order, columns, tile, edge, widt...  4.89 us
    dot_general x4, matrix products, query_term(): lax.dot_general(block, feats, (((0,), (0,)), ((), ())), preferred_element...  3.19 us
    unnamed x8, local copies, waits for them, and re-layouts  2.2 us
  transfers between devices with their start and end apart: 21, of which 6 were waited for; matrix products, arithmetic and copies ran while one was open for 4% of the time, Pallas kernels for 8%

profile of v2, /device:TPU:0, one launch (start us, length us, event | category | flops | bytes accessed | tf_op | source)
XLA Modules:
  0.0 82.8 jit_solution(10561325872847912787)
XLA Ops:
  0.7 1.5 %pad_dynamic-slice_fusion = (bf16[64,1280]{1,0:T(8,128)(2,1)S(1)}, bf16[64,1280]{1,0:T(8,128)(2,1)S(1)}, bf16[64,1280]{1,0:T(8,128)(2,1)S(1)}, bf16[64,1280]{1,0...) fusion(s32[]{:T(128)S(6)} %select_n.31, ...), kind=kLoop, calls=%fused_computation.2 | loop fusion | bytes 2359328 | tf_op jit(solution)/shard_map/dynamic_slice | solution.py:315
  2.3 3.0 %collective-permute-start = (bf16[64,1280]{1,0:T(8,128)(2,1)S(1)}, bf16[64,1280]{1,0:T(8,128)(2,1)S(1)}, u32[]{:S(2)}, u32[]{:S(2)}) collective-permute-start(bf16[64,1280]{1,0:T(8,128)(2,1)S(1)} %get-tuple-element.51), channel_id=1, source_target_pairs={{0,2},{2,0},{4,6},{6,4},{8,10},{10,8},{12,14},{14,12},{1,3},{3,1},... | collective-permute-start | bytes 491528 | tf_op jit(solution)/shard_map/ppermute | solution.py:310
  5.3 1.6 %collective-permute-start.1 = (bf16[64,1280]{1,0:T(8,128)(2,1)S(1)}, bf16[64,1280]{1,0:T(8,128)(2,1)S(1)}, u32[]{:S(2)}, u32[]{:S(2)}) collective-permute-start(bf16[64,1280]{1,0:T(8,128)(2,1)S(1)} %get-tuple-element.52), channel_id=1, source_target_pairs={{0,4},{2,6},{4,0},{6,2},{8,12},{10,14},{12,8},{14,10},{1,5},{3,7},... | collective-permute-start | bytes 491528 | tf_op jit(solution)/shard_map/ppermute | solution.py:310
  6.8 0.0 collective-permute-start.2
  6.8 3.0 %collective-permute-start.3 = (bf16[64,1280]{1,0:T(8,128)(2,1)S(1)}, bf16[64,1280]{1,0:T(8,128)(2,1)S(1)}, u32[]{:S(2)}, u32[]{:S(2)}) collective-permute-start(bf16[64,1280]{1,0:T(8,128)(2,1)S(1)} %get-tuple-element.54), channel_id=1, source_target_pairs={{0,8},{2,10},{4,12},{6,14},{8,0},{10,2},{12,4},{14,6},{1,9},{3,11}... | collective-permute-start | bytes 491528 | tf_op jit(solution)/shard_map/ppermute | solution.py:310
  9.9 0.0 collective-permute-start.15
  9.9 10.0 %collective-permute-done.15 = bf16[64,1024]{1,0:T(8,128)(2,1)S(1)} collective-permute-done((bf16[64,1024]{1,0:T(8,128)(2,1)S(1)}, bf16[64,1024]{1,0:T(8,128)(2,1)S(1)}, u32[]{:S(2)}, u32[]{:S(2)}) %collective-permute-start.15) | collective-permute-done | bytes 131104 | tf_op jit(solution)/shard_map/ppermute | solution.py:310
  19.9 3.5 %collective-permute-start.16 = (bf16[128,1024]{1,0:T(8,128)(2,1)S(1)}, bf16[128,1024]{1,0:T(8,128)(2,1)S(1)}, u32[]{:S(2)}, u32[]{:S(2)}) collective-permute-start(bf16[128,1024]{1,0:T(8,128)(2,1)S(1)} %pad_maximum_fusion.1), channel_id=1, source_target_pairs={{0,4},{2,6},{4,0},{6,2},{8,12},{10,14},{12,8},{14,10},{1,5},{3,7},... | collective-permute-start | bytes 786440 | tf_op jit(solution)/shard_map/ppermute | solution.py:310
  23.4 4.3 %collective-permute-start.4 = (bf16[64,1280]{1,0:T(8,128)(2,1)S(1)}, bf16[64,1280]{1,0:T(8,128)(2,1)S(1)}, u32[]{:S(2)}, u32[]{:S(2)}) collective-permute-start(bf16[64,1280]{1,0:T(8,128)(2,1)S(1)} %get-tuple-element.55), channel_id=1, source_target_pairs={{0,10},{2,8},{4,14},{6,12},{8,2},{10,0},{12,6},{14,4},{1,11},{3,9}... | collective-permute-start | bytes 491528 | tf_op jit(solution)/shard_map/ppermute | solution.py:310
  27.7 0.0 collective-permute-done.1.refs_3_
  27.7 0.4 collective-permute-start.5
  28.1 3.5 %collective-permute-start.6 = (bf16[64,1280]{1,0:T(8,128)(2,1)S(1)}, bf16[64,1280]{1,0:T(8,128)(2,1)S(1)}, u32[]{:S(2)}, u32[]{:S(2)}) collective-permute-start(bf16[64,1280]{1,0:T(8,128)(2,1)S(1)} %get-tuple-element.50), channel_id=1, source_target_pairs={{0,14},{2,12},{4,10},{6,8},{8,6},{10,4},{12,2},{14,0},{1,15},{3,13... | collective-permute-start | bytes 491528 | tf_op jit(solution)/shard_map/ppermute | solution.py:310
  31.6 0.1 pad_add_fusion.1.refs_0_
  31.7 0.1 reshape.7.refs_1_
  31.8 1.3 %matrix_kernel.1 = (bf16[512,528]{1,0:T(8,128)(2,1)S(1)}, bf16[512,528]{1,0:T(8,128)(2,1)S(1)}, bf16[512,256]{1,0:T(8,128)(2,1)S(1)}, bf16[512,256]{1,0:T(8,128)(2,1)S(1)}) custom-call(s32[2]{0:T(128)S(1)} %pad_add_fusion.1.refs_0_, f32[36]{0:T(128)S(1)} %reshape.7.refs_1_), custom_call_target="tpu_custom_call" | custom-call | flops 5242880 | bytes 2097152 | tf_op jit(solution)/shard_map/matrix_kernel/pallas_call | solution.py:175
  33.1 0.1 pad_add_fusion.refs_0_
  33.2 0.0 collective-permute-done.3.refs_5_
  33.2 10.0 %collective-permute-done.4.refs_6_ = bf16[64,1280]{1,0:T(8,128)(2,1)S(1)} collective-permute-done((bf16[64,1280]{1,0:T(8,128)(2,1)S(1)}, bf16[64,1280]{1,0:T(8,128)(2,1)S(1)}, u32[]{:S(2)}, u32[]{:S(2)}) %collective-permute-start.4) | collective-permute-done | bytes 163872 | tf_op jit(solution)/shard_map/ppermute | solution.py:310
  43.2 0.0 collective-permute-done.5.refs_7_
  43.2 0.0 collective-permute-done.6.refs_8_
  43.2 0.6 rim_kernel.1
  43.8 0.1 collective-permute-start.7
  43.9 0.0 collective-permute-done.16
  44.0 0.1 collective-permute-start.17
  44.0 1.1 %collective-permute-done.7.refs_9_ = bf16[16,1024]{1,0:T(8,128)(2,1)S(1)} collective-permute-done((bf16[16,1024]{1,0:T(8,128)(2,1)S(1)}, bf16[16,1024]{1,0:T(8,128)(2,1)S(1)}, u32[]{:S(2)}, u32[]{:S(2)}) %collective-permute-start.7) | collective-permute-done | bytes 32800 | tf_op jit(solution)/shard_map/ppermute | solution.py:334
  45.1 2.2 %copy-done = bf16[2048,1024]{1,0:T(8,128)(2,1)S(1)} copy-done((bf16[2048,1024]{1,0:T(8,128)(2,1)S(1)}, bf16[2048,1024]{1,0:T(8,128)(2,1)}, u32[]{:S(2)}) %copy-start) | copy-done | bytes 4194328
  47.3 4.9 %tile_kernel.1 = (bf16[512,512]{1,0:T(8,128)(2,1)S(1)}, bf16[512,512]{1,0:T(8,128)(2,1)S(1)}, f32[64,1024]{1,0:T(8,128)S(1)}, bf16[64,1024]{1,0:T(8,128)(2,1)S(1...) custom-call(s32[2]{0:T(128)S(1)} %pad_add_fusion.refs_0_, ...), custom_call_target="tpu_custom_call" | custom-call | flops 3254779904 | bytes 7340032 | tf_op jit(solution)/shard_map/tile_kernel/pallas_call | solution.py:271
  52.2 0.2 collective-permute-start.18
  52.4 0.3 collective-permute-start.19
  52.8 6.6 %collective-permute-start.10 = (bf16[64,1024]{1,0:T(8,128)(2,1)S(1)}, bf16[64,1024]{1,0:T(8,128)(2,1)S(1)}, u32[]{:S(2)}, u32[]{:S(2)}) collective-permute-start(bf16[64,1024]{1,0:T(8,128)(2,1)S(1)} %get-tuple-element.32), channel_id=1, source_target_pairs={{0,10},{2,8},{4,14},{6,12},{8,2},{10,0},{12,6},{14,4},{1,11},{3,9}... | collective-permute-start | bytes 393224 | tf_op jit(solution)/shard_map/ppermute | solution.py:310
  59.4 0.0 collective-permute-start.11
  59.4 0.0 collective-permute-done.17
  59.4 6.5 %collective-permute-start.12 = (bf16[64,1024]{1,0:T(8,128)(2,1)S(1)}, bf16[64,1024]{1,0:T(8,128)(2,1)S(1)}, u32[]{:S(2)}, u32[]{:S(2)}) collective-permute-start(bf16[64,1024]{1,0:T(8,128)(2,1)S(1)} %get-tuple-element.34), channel_id=1, source_target_pairs={{0,6},{2,4},{4,2},{6,0},{8,14},{10,12},{12,10},{14,8},{1,7},{3,5},... | collective-permute-start | bytes 393224 | tf_op jit(solution)/shard_map/ppermute | solution.py:310
  65.9 0.5 fusion.6
  66.3 0.0 collective-permute-done.18
  66.3 0.1 collective-permute-start.13
  66.5 0.0 collective-permute-start.20
  66.5 0.5 fusion.4
  67.0 0.5 fusion.8
  67.4 1.9 %collective-permute-done.10 = bf16[64,1024]{1,0:T(8,128)(2,1)S(1)} collective-permute-done((bf16[64,1024]{1,0:T(8,128)(2,1)S(1)}, bf16[64,1024]{1,0:T(8,128)(2,1)S(1)}, u32[]{:S(2)}, u32[]{:S(2)}) %collective-permute-start.10) | collective-permute-done | bytes 131104 | tf_op jit(solution)/shard_map/ppermute | solution.py:310
  69.4 0.9 %collective-permute-start.14 = (bf16[64,1024]{1,0:T(8,128)(2,1)S(1)}, bf16[64,1024]{1,0:T(8,128)(2,1)S(1)}, u32[]{:S(2)}, u32[]{:S(2)}) collective-permute-start(bf16[64,1024]{1,0:T(8,128)(2,1)S(1)} %get-tuple-element.36), channel_id=1, source_target_pairs={{0,2},{2,0},{4,6},{6,4},{8,10},{10,8},{12,14},{14,12},{1,3},{3,1},... | collective-permute-start | bytes 393224 | tf_op jit(solution)/shard_map/ppermute | solution.py:310
  70.3 0.9 %collective-permute-done.11 = bf16[64,1024]{1,0:T(8,128)(2,1)S(1)} collective-permute-done((bf16[64,1024]{1,0:T(8,128)(2,1)S(1)}, bf16[64,1024]{1,0:T(8,128)(2,1)S(1)}, u32[]{:S(2)}, u32[]{:S(2)}) %collective-permute-start.11) | collective-permute-done | bytes 131104 | tf_op jit(solution)/shard_map/ppermute | solution.py:310
  71.3 1.4 %collective-permute-start.8 = (bf16[64,1024]{1,0:T(8,128)(2,1)S(1)}, bf16[64,1024]{1,0:T(8,128)(2,1)S(1)}, u32[]{:S(2)}, u32[]{:S(2)}) collective-permute-start(bf16[64,1024]{1,0:T(8,128)(2,1)S(1)} %get-tuple-element.30), channel_id=1, source_target_pairs={{0,14},{2,12},{4,10},{6,8},{8,6},{10,4},{12,2},{14,0},{1,15},{3,13... | collective-permute-start | bytes 393224 | tf_op jit(solution)/shard_map/ppermute | solution.py:310
  72.7 0.0 collective-permute-done.20
  72.7 2.9 %collective-permute-start.9 = (bf16[64,1024]{1,0:T(8,128)(2,1)S(1)}, bf16[64,1024]{1,0:T(8,128)(2,1)S(1)}, u32[]{:S(2)}, u32[]{:S(2)}) collective-permute-start(bf16[64,1024]{1,0:T(8,128)(2,1)S(1)} %get-tuple-element.31), channel_id=1, source_target_pairs={{0,12},{2,14},{4,8},{6,10},{8,4},{10,6},{12,0},{14,2},{1,13},{3,15... | collective-permute-start | bytes 393224 | tf_op jit(solution)/shard_map/ppermute | solution.py:310
  75.6 1.8 %add_multiply_fusion = f32[512,1024]{1,0:T(8,128)} fusion(f32[512,1024]{1,0:T(8,128)S(1)} %fusion.6, f32[512,1024]{1,0:T(8,128)S(1)} %fusion.8, f32[512,1024]{1,0:T(8,128)S(1)} %fusion.4, bf16[256,1024]{1,0:T(8,128)(2,1)S(1)} %collective-permute-done.20, bf16[512,512]{1,0:T(8,128)(2,1)S(1)} %collective-permute-done.18), kind=kOutput, calls=%fused_computation | convolution fusion | flops 270532608 | bytes 9175040 | tf_op jit(solution)/shard_map/dot_general | solution.py:355
  77.4 4.5 %collective-permute-done.13 = bf16[64,1024]{1,0:T(8,128)(2,1)S(1)} collective-permute-done((bf16[64,1024]{1,0:T(8,128)(2,1)S(1)}, bf16[64,1024]{1,0:T(8,128)(2,1)S(1)}, u32[]{:S(2)}, u32[]{:S(2)}) %collective-permute-start.13) | collective-permute-done | bytes 131104 | tf_op jit(solution)/shard_map/ppermute | solution.py:310
  81.9 0.9 %multiply_bitcast_fusion = f32[1,64,1024]{2,1,0:T(8,128)} fusion(bf16[64,1024]{1,0:T(8,128)(2,1)S(1)} %collective-permute-done.14, bf16[64,1024]{1,0:T(8,128)(2,1)S(1)} %collective-permute-done.13, bf16[64,1024]{1,0:T(8,128)(2,1)S(1)} %collective-permute-done.12, bf16[64,1024]{1,0:T(8,128)(2,1)S(1)} %collective-permute-done.11, ...), kind=kLoop, calls=%fused_computation.15 | loop fusion | flops 983040 | bytes 1441792 | tf_op jit(solution)/shard_map/broadcast_in_dim | solution.py:369
  (18 shorter events, 0.1 us)
Async XLA Ops:
  0.6 9.2 %copy-start.1 = (bf16[1,64,1024]{2,1,0:T(8,128)(2,1)S(1)}, bf16[1,64,1024]{2,1,0:T(8,128)(2,1)}, u32[]{:S(2)}) copy-start(bf16[1,64,1024]{2,1,0:T(8,128)(2,1)} %param.7) | copy-start | bytes 393220
  0.6 9.2 %copy-start.3 = (f32[3,3]{1,0:T(4,128)S(1)}, f32[3,3]{1,0:T(4,128)}, u32[]{:S(2)}) copy-start(f32[3,3]{1,0:T(4,128)} %param.8) | copy-start | bytes 112
  0.7 9.2 %copy-start.2 = (f32[3,3]{1,0:T(4,128)S(1)}, f32[3,3]{1,0:T(4,128)}, u32[]{:S(2)}) copy-start(f32[3,3]{1,0:T(4,128)} %param.9) | copy-start | bytes 112
  2.3 21.2 %collective-permute-start = (bf16[64,1280]{1,0:T(8,128)(2,1)S(1)}, bf16[64,1280]{1,0:T(8,128)(2,1)S(1)}, u32[]{:S(2)}, u32[]{:S(2)}) collective-permute-start(bf16[64,1280]{1,0:T(8,128)(2,1)S(1)} %get-tuple-element.51), channel_id=1, source_target_pairs={{0,2},{2,0},{4,6},{6,4},{8,10},{10,8},{12,14},{14,12},{1,3},{3,1},... | collective-permute-start | bytes 491528 | tf_op jit(solution)/shard_map/ppermute | solution.py:310
  5.3 22.4 %collective-permute-start.1 = (bf16[64,1280]{1,0:T(8,128)(2,1)S(1)}, bf16[64,1280]{1,0:T(8,128)(2,1)S(1)}, u32[]{:S(2)}, u32[]{:S(2)}) collective-permute-start(bf16[64,1280]{1,0:T(8,128)(2,1)S(1)} %get-tuple-element.52), channel_id=1, source_target_pairs={{0,4},{2,6},{4,0},{6,2},{8,12},{10,14},{12,8},{14,10},{1,5},{3,7},... | collective-permute-start | bytes 491528 | tf_op jit(solution)/shard_map/ppermute | solution.py:310
  6.8 21.3 %collective-permute-start.2 = (bf16[64,1280]{1,0:T(8,128)(2,1)S(1)}, bf16[64,1280]{1,0:T(8,128)(2,1)S(1)}, u32[]{:S(2)}, u32[]{:S(2)}) collective-permute-start(bf16[64,1280]{1,0:T(8,128)(2,1)S(1)} %get-tuple-element.53), channel_id=1, source_target_pairs={{0,6},{2,4},{4,2},{6,0},{8,14},{10,12},{12,10},{14,8},{1,7},{3,5},... | collective-permute-start | bytes 491528 | tf_op jit(solution)/shard_map/ppermute | solution.py:310
  6.8 26.3 %collective-permute-start.3 = (bf16[64,1280]{1,0:T(8,128)(2,1)S(1)}, bf16[64,1280]{1,0:T(8,128)(2,1)S(1)}, u32[]{:S(2)}, u32[]{:S(2)}) collective-permute-start(bf16[64,1280]{1,0:T(8,128)(2,1)S(1)} %get-tuple-element.54), channel_id=1, source_target_pairs={{0,8},{2,10},{4,12},{6,14},{8,0},{10,2},{12,4},{14,6},{1,9},{3,11}... | collective-permute-start | bytes 491528 | tf_op jit(solution)/shard_map/ppermute | solution.py:310
  9.9 10.0 %collective-permute-start.15 = (bf16[64,1024]{1,0:T(8,128)(2,1)S(1)}, bf16[64,1024]{1,0:T(8,128)(2,1)S(1)}, u32[]{:S(2)}, u32[]{:S(2)}) collective-permute-start(bf16[64,1024]{1,0:T(8,128)(2,1)S(1)} %bitcast.18), channel_id=1, source_target_pairs={{0,8},{2,10},{4,12},{6,14},{8,0},{10,2},{12,4},{14,6},{1,9},{3,11}... | collective-permute-start | bytes 393224 | tf_op jit(solution)/shard_map/ppermute | solution.py:310
  19.9 24.0 %collective-permute-start.16 = (bf16[128,1024]{1,0:T(8,128)(2,1)S(1)}, bf16[128,1024]{1,0:T(8,128)(2,1)S(1)}, u32[]{:S(2)}, u32[]{:S(2)}) collective-permute-start(bf16[128,1024]{1,0:T(8,128)(2,1)S(1)} %pad_maximum_fusion.1), channel_id=1, source_target_pairs={{0,4},{2,6},{4,0},{6,2},{8,12},{10,14},{12,8},{14,10},{1,5},{3,7},... | collective-permute-start | bytes 786440 | tf_op jit(solution)/shard_map/ppermute | solution.py:310
  23.4 19.8 %collective-permute-start.4 = (bf16[64,1280]{1,0:T(8,128)(2,1)S(1)}, bf16[64,1280]{1,0:T(8,128)(2,1)S(1)}, u32[]{:S(2)}, u32[]{:S(2)}) collective-permute-start(bf16[64,1280]{1,0:T(8,128)(2,1)S(1)} %get-tuple-element.55), channel_id=1, source_target_pairs={{0,10},{2,8},{4,14},{6,12},{8,2},{10,0},{12,6},{14,4},{1,11},{3,9}... | collective-permute-start | bytes 491528 | tf_op jit(solution)/shard_map/ppermute | solution.py:310
  27.7 15.5 %collective-permute-start.5 = (bf16[64,1280]{1,0:T(8,128)(2,1)S(1)}, bf16[64,1280]{1,0:T(8,128)(2,1)S(1)}, u32[]{:S(2)}, u32[]{:S(2)}) collective-permute-start(bf16[64,1280]{1,0:T(8,128)(2,1)S(1)} %get-tuple-element.56), channel_id=1, source_target_pairs={{0,12},{2,14},{4,8},{6,10},{8,4},{10,6},{12,0},{14,2},{1,13},{3,15... | collective-permute-start | bytes 491528 | tf_op jit(solution)/shard_map/ppermute | solution.py:310
  28.1 15.1 %collective-permute-start.6 = (bf16[64,1280]{1,0:T(8,128)(2,1)S(1)}, bf16[64,1280]{1,0:T(8,128)(2,1)S(1)}, u32[]{:S(2)}, u32[]{:S(2)}) collective-permute-start(bf16[64,1280]{1,0:T(8,128)(2,1)S(1)} %get-tuple-element.50), channel_id=1, source_target_pairs={{0,14},{2,12},{4,10},{6,8},{8,6},{10,4},{12,2},{14,0},{1,15},{3,13... | collective-permute-start | bytes 491528 | tf_op jit(solution)/shard_map/ppermute | solution.py:310
  43.8 1.3 %collective-permute-start.7 = (bf16[16,1024]{1,0:T(8,128)(2,1)S(1)}, bf16[16,1024]{1,0:T(8,128)(2,1)S(1)}, u32[]{:S(2)}, u32[]{:S(2)}) collective-permute-start(bf16[16,1024]{1,0:T(8,128)(2,1)S(1)} %rim_kernel.1), channel_id=1, source_target_pairs={{0,1},{1,0},{2,3},{3,2},{4,5},{5,4},{6,7},{7,6},{8,9},{9,8},{10,11... | collective-permute-start | bytes 98312 | tf_op jit(solution)/shard_map/ppermute | solution.py:334
  44.0 15.4 %collective-permute-start.17 = (bf16[256,1024]{1,0:T(8,128)(2,1)S(1)}, bf16[256,1024]{1,0:T(8,128)(2,1)S(1)}, u32[]{:S(2)}, u32[]{:S(2)}) collective-permute-start(bf16[256,1024]{1,0:T(8,128)(2,1)S(1)} %pad_maximum_fusion), channel_id=1, source_target_pairs={{0,2},{2,0},{4,6},{6,4},{8,10},{10,8},{12,14},{14,12},{1,3},{3,1},... | collective-permute-start | bytes 1572872 | tf_op jit(solution)/shard_map/ppermute | solution.py:310
  45.1 2.2 %copy-start = (bf16[2048,1024]{1,0:T(8,128)(2,1)S(1)}, bf16[2048,1024]{1,0:T(8,128)(2,1)}, u32[]{:S(2)}) copy-start(bf16[2048,1024]{1,0:T(8,128)(2,1)} %refs_14_.1) | copy-start | bytes 12582916
  52.2 14.1 %collective-permute-start.18 = (bf16[512,512]{1,0:T(8,128)(2,1)S(1)}, bf16[512,512]{1,0:T(8,128)(2,1)S(1)}, u32[]{:S(2)}, u32[]{:S(2)}) collective-permute-start(bf16[512,512]{1,0:T(8,128)(2,1)S(1)} %get-tuple-element.39), channel_id=1, source_target_pairs={{0,1},{1,0},{2,3},{3,2},{4,5},{5,4},{6,7},{7,6},{8,9},{9,8},{10,11... | collective-permute-start | bytes 1572872 | tf_op jit(solution)/shard_map/ppermute | solution.py:352
  52.4 14.1 %collective-permute-start.19 = (bf16[256,1024]{1,0:T(8,128)(2,1)S(1)}, bf16[256,1024]{1,0:T(8,128)(2,1)S(1)}, u32[]{:S(2)}, u32[]{:S(2)}) collective-permute-start(bf16[256,1024]{1,0:T(8,128)(2,1)S(1)} %pad_maximum_fusion), channel_id=1, source_target_pairs={{0,1},{1,0},{2,3},{3,2},{4,5},{5,4},{6,7},{7,6},{8,9},{9,8},{10,11... | collective-permute-start | bytes 1572872 | tf_op jit(solution)/shard_map/ppermute | solution.py:330
  52.8 16.6 %collective-permute-start.10 = (bf16[64,1024]{1,0:T(8,128)(2,1)S(1)}, bf16[64,1024]{1,0:T(8,128)(2,1)S(1)}, u32[]{:S(2)}, u32[]{:S(2)}) collective-permute-start(bf16[64,1024]{1,0:T(8,128)(2,1)S(1)} %get-tuple-element.32), channel_id=1, source_target_pairs={{0,10},{2,8},{4,14},{6,12},{8,2},{10,0},{12,6},{14,4},{1,11},{3,9}... | collective-permute-start | bytes 393224 | tf_op jit(solution)/shard_map/ppermute | solution.py:310
  59.4 11.9 %collective-permute-start.11 = (bf16[64,1024]{1,0:T(8,128)(2,1)S(1)}, bf16[64,1024]{1,0:T(8,128)(2,1)S(1)}, u32[]{:S(2)}, u32[]{:S(2)}) collective-permute-start(bf16[64,1024]{1,0:T(8,128)(2,1)S(1)} %get-tuple-element.33), channel_id=1, source_target_pairs={{0,8},{2,10},{4,12},{6,14},{8,0},{10,2},{12,4},{14,6},{1,9},{3,11}... | collective-permute-start | bytes 393224 | tf_op jit(solution)/shard_map/ppermute | solution.py:310
  59.4 18.0 %collective-permute-start.12 = (bf16[64,1024]{1,0:T(8,128)(2,1)S(1)}, bf16[64,1024]{1,0:T(8,128)(2,1)S(1)}, u32[]{:S(2)}, u32[]{:S(2)}) collective-permute-start(bf16[64,1024]{1,0:T(8,128)(2,1)S(1)} %get-tuple-element.34), channel_id=1, source_target_pairs={{0,6},{2,4},{4,2},{6,0},{8,14},{10,12},{12,10},{14,8},{1,7},{3,5},... | collective-permute-start | bytes 393224 | tf_op jit(solution)/shard_map/ppermute | solution.py:310
  66.3 15.5 %collective-permute-start.13 = (bf16[64,1024]{1,0:T(8,128)(2,1)S(1)}, bf16[64,1024]{1,0:T(8,128)(2,1)S(1)}, u32[]{:S(2)}, u32[]{:S(2)}) collective-permute-start(bf16[64,1024]{1,0:T(8,128)(2,1)S(1)} %get-tuple-element.35), channel_id=1, source_target_pairs={{0,4},{2,6},{4,0},{6,2},{8,12},{10,14},{12,8},{14,10},{1,5},{3,7},... | collective-permute-start | bytes 393224 | tf_op jit(solution)/shard_map/ppermute | solution.py:310
  66.5 6.2 %collective-permute-start.20 = (bf16[256,1024]{1,0:T(8,128)(2,1)S(1)}, bf16[256,1024]{1,0:T(8,128)(2,1)S(1)}, u32[]{:S(2)}, u32[]{:S(2)}) collective-permute-start(bf16[256,1024]{1,0:T(8,128)(2,1)S(1)} %collective-permute-done.17), channel_id=1, source_target_pairs={{0,1},{1,0},{2,3},{3,2},{4,5},{5,4},{6,7},{7,6},{8,9},{9,8},{10,11... | collective-permute-start | bytes 1572872 | tf_op jit(solution)/shard_map/ppermute | solution.py:349
  69.4 12.5 %collective-permute-start.14 = (bf16[64,1024]{1,0:T(8,128)(2,1)S(1)}, bf16[64,1024]{1,0:T(8,128)(2,1)S(1)}, u32[]{:S(2)}, u32[]{:S(2)}) collective-permute-start(bf16[64,1024]{1,0:T(8,128)(2,1)S(1)} %get-tuple-element.36), channel_id=1, source_target_pairs={{0,2},{2,0},{4,6},{6,4},{8,10},{10,8},{12,14},{14,12},{1,3},{3,1},... | collective-permute-start | bytes 393224 | tf_op jit(solution)/shard_map/ppermute | solution.py:310
  71.3 10.6 %collective-permute-start.8 = (bf16[64,1024]{1,0:T(8,128)(2,1)S(1)}, bf16[64,1024]{1,0:T(8,128)(2,1)S(1)}, u32[]{:S(2)}, u32[]{:S(2)}) collective-permute-start(bf16[64,1024]{1,0:T(8,128)(2,1)S(1)} %get-tuple-element.30), channel_id=1, source_target_pairs={{0,14},{2,12},{4,10},{6,8},{8,6},{10,4},{12,2},{14,0},{1,15},{3,13... | collective-permute-start | bytes 393224 | tf_op jit(solution)/shard_map/ppermute | solution.py:310
  72.7 9.2 %collective-permute-start.9 = (bf16[64,1024]{1,0:T(8,128)(2,1)S(1)}, bf16[64,1024]{1,0:T(8,128)(2,1)S(1)}, u32[]{:S(2)}, u32[]{:S(2)}) collective-permute-start(bf16[64,1024]{1,0:T(8,128)(2,1)S(1)} %get-tuple-element.31), channel_id=1, source_target_pairs={{0,12},{2,14},{4,8},{6,10},{8,4},{10,6},{12,0},{14,2},{1,13},{3,15... | collective-permute-start | bytes 393224 | tf_op jit(solution)/shard_map/ppermute | solution.py:310

commit v3 on v0

--- a/solution.py
+++ b/solution.py
@@ -3,6 +3,8 @@
 import jax
 import jax.numpy as jnp
 from jax import lax
+from jax.experimental import pallas as pl
+from jax.experimental.pallas import tpu as pltpu
 from jax.sharding import PartitionSpec as P
 
 QW = 128
@@ -57,7 +59,7 @@
     return total
 
 
-def shards(grad_volume, query_feats, support_feats, query_kernel, support_kernel):
+def ring_shards(grad_volume, query_feats, support_feats, query_kernel, support_kernel):
     planes, columns, queries = grad_volume.shape
     rimmed = extended(grad_volume, ((("blk", "sub"), 0), ("pair", 1)), 1)
     corr_grad = (
@@ -104,6 +106,330 @@
     return (query_grad, support_total * scale_factor)
 
 
+def split_taps(kernel):
+    high = lax.reduce_precision(kernel, 8, 7)
+    return high, kernel - high
+
+
+def banded(taps, step):
+    total = jnp.where(step == 1, taps[2], 0.0)
+    return jnp.where(step == 0, taps[1], jnp.where(step == -1, taps[0], total))
+
+
+def matrix_kernel(count, columns, place_ref, taps_ref, t_ref, rim_ref, wh_ref, wl_ref):
+    cells = count * columns
+
+    def taps(part, kernel, a, b):
+        return taps_ref[((part * 2 + kernel) * 3 + a) * 3 + b]
+
+    def span(shape, dim):
+        return lax.broadcasted_iota(jnp.int32, shape, dim)
+
+    square = (QW, QW)
+    step = span(square, 0) - span(square, 1)
+    for part, w_ref in enumerate((wh_ref, wl_ref)):
+        bands = [
+            banded([taps(part, 0, a, b) for b in range(3)], step).astype(jnp.bfloat16)
+            for a in range(3)
+        ]
+        for source in range(4):
+            for target in range(2):
+                a = source - target
+                block = bands[a] if 0 <= a <= 2 else jnp.zeros(square, jnp.bfloat16)
+                w_ref[source * QW : (source + 1) * QW, target * QW : (target + 1) * QW] = block
+    group = 4 * columns
+    shape = (2 * columns, group)
+    row_step = span(shape, 1) // columns - span(shape, 0) // columns - 1
+    col_step = lax.rem(span(shape, 1), columns) - lax.rem(span(shape, 0), columns)
+    beside = jnp.where(place_ref[1] == 0, columns, -1)
+    rim_shape = (cells, rim_ref.shape[1] // 2)
+    rim_row = span(rim_shape, 1) - span(rim_shape, 0) // columns
+    rim_col = beside - lax.rem(span(rim_shape, 0), columns)
+    for part in range(2):
+        rows = [
+            banded([taps(part, 1, a, b) for a in range(3)], row_step) for b in range(3)
+        ]
+        block = banded(rows, col_step).astype(jnp.bfloat16)
+        t_ref[part * 2 * columns : (part + 1) * 2 * columns, :] = block
+        rows = [banded([taps(part, 1, a, b) for a in range(3)], rim_row) for b in range(3)]
+        block = banded(rows, rim_col).astype(jnp.bfloat16)
+        rim_ref[:, part * rim_shape[1] : (part + 1) * rim_shape[1]] = block
+
+
+def matrix_call(place, query_kernel, support_kernel, count, columns, edge):
+    query_parts = split_taps(query_kernel)
+    support_parts = split_taps(support_kernel)
+    taps = jnp.stack(
+        [query_parts[0], support_parts[0], query_parts[1], support_parts[1]]
+    ).reshape(-1)
+    shapes = [
+        (4 * columns, 4 * columns),
+        (count * columns, 2 * edge),
+        (4 * QW, 2 * QW),
+        (4 * QW, 2 * QW),
+    ]
+    return pl.pallas_call(
+        lambda *refs: matrix_kernel(count, columns, *refs),
+        out_shape=[jax.ShapeDtypeStruct(shape, jnp.bfloat16) for shape in shapes],
+        in_specs=[pl.BlockSpec(memory_space=pltpu.SMEM)] * 2,
+        out_specs=[pl.BlockSpec(memory_space=pltpu.VMEM)] * 4,
+        cost_estimate=pl.CostEstimate(
+            flops=20 * QW * QW * count, bytes_accessed=32 * QW * QW, transcendentals=0
+        ),
+        compiler_params=pltpu.CompilerParams(vmem_limit_bytes=4 << 20),
+        name="matrix_kernel",
+    )(place, taps)
+
+
+def gather_kernel(count, columns, tile, place_ref, *refs):
+    pieces, cells_ref, rim_ref = refs[:count], refs[count], refs[count + 1]
+    own = place_ref[0]
+    first = place_ref[1] != 0
+    inner = slice(QW, QW + tile)
+    empty = jnp.zeros((columns, tile + 2 * QW), jnp.bfloat16)
+    cells_ref[:columns, :] = empty
+    cells_ref[(count + 1) * columns :, :] = empty
+    edge = rim_ref.shape[0] // 2
+    span = lax.broadcasted_iota(jnp.int32, (edge, tile), 0)
+    total = jnp.zeros(span.shape, jnp.float32)
+    for k, piece in enumerate(reversed(pieces)):
+        start = pl.multiple_of(((own ^ k) + 1) * columns, columns)
+        cells_ref[pl.ds(start, columns), :] = piece[...]
+        head = piece[:16, inner].astype(jnp.float32)[:1]
+        tail = piece[columns - 16 :, inner].astype(jnp.float32)[15:]
+        row = jnp.where(first, head, tail)
+        total = jnp.where(span == (own ^ k), row, total)
+    rim_ref[:edge, :] = total.astype(jnp.bfloat16)
+    rim_ref[edge:, :] = total.astype(jnp.bfloat16)
+
+
+def gather_call(place, pieces, tile, edge):
+    count = len(pieces)
+    columns, reach = pieces[0].shape
+    return pl.pallas_call(
+        lambda *refs: gather_kernel(count, columns, tile, *refs),
+        out_shape=[
+            jax.ShapeDtypeStruct(((count + 2) * columns, reach), jnp.bfloat16),
+            jax.ShapeDtypeStruct((2 * edge, tile), jnp.bfloat16),
+        ],
+        in_specs=[pl.BlockSpec(memory_space=pltpu.SMEM)]
+        + [pl.BlockSpec(memory_space=pltpu.VMEM)] * count,
+        out_specs=[pl.BlockSpec(memory_space=pltpu.VMEM)] * 2,
+        compiler_params=pltpu.CompilerParams(vmem_limit_bytes=4 << 20),
+        cost_estimate=pl.CostEstimate(
+            flops=count * tile, bytes_accessed=4 * count * columns * reach, transcendentals=0
+        ),
+        name="gather_kernel",
+    )(place, *reversed(pieces))
+
+
+def product(left, right):
+    return jnp.dot(left, right, preferred_element_type=jnp.float32)
+
+
+def corr_kernel(
+    group, columns, tile, place_ref, cells_ref, rim_ref, t_ref, edge_ref, wh_ref, wl_ref,
+    move_ref, stay_ref, keep_ref, send_ref, corr_ref,
+):
+    half = corr_ref.shape[0] // columns
+    own = place_ref[0]
+    core = place_ref[1]
+    base = ((own // half) ^ group) * half
+    rows = half * columns
+    pair = 2 * columns
+
+    def plane_rows(plane, size):
+        return pl.ds(pl.multiple_of(plane * columns, columns), size)
+
+    step = 2 * QW
+    for low in range(0, tile, step):
+        window = cells_ref[plane_rows(base + 1, rows), low : low + 2 * step]
+        total = product(window, wh_ref[...]) + product(window, wl_ref[...])
+        edges = edge_ref[plane_rows(base, rows), :]
+        total += product(edges, rim_ref[:, low : low + step])
+        for at in range(0, half, 2):
+            middle = cells_ref[plane_rows(base + at, 2 * pair), low + QW : low + QW + step]
+            both = product(t_ref[...], middle)
+            top = at * columns
+            block = total[top : top + pair] + both[:pair] + both[pair:]
+            corr_ref[top : top + pair, low : low + step] = block.astype(jnp.bfloat16)
+    width = tile // 2
+    for k in range(half):
+        source = plane_rows(lax.rem(own, half) ^ k, columns)
+        out_ref = move_ref if k % 2 else stay_ref
+        out_ref[k // 2 * columns : (k // 2 + 1) * columns, :] = corr_ref[source, :]
+        for half_ref, which in ((keep_ref, core), (send_ref, 1 - core)):
+            start = pl.multiple_of(which * width, width)
+            half_ref[k * columns : (k + 1) * columns, :] = corr_ref[source, pl.ds(start, width)]
+
+
+def corr_call(group, place, cells, rim, mats, count):
+    tile = rim.shape[1]
+    columns = cells.shape[0] // (count + 2)
+    half = count // 2
+    rows = half * columns
+    vmem = pl.BlockSpec(memory_space=pltpu.VMEM)
+    wide = jax.ShapeDtypeStruct((rows // 2, tile), jnp.bfloat16)
+    tall = jax.ShapeDtypeStruct((rows, tile // 2), jnp.bfloat16)
+    return pl.pallas_call(
+        lambda *refs: corr_kernel(group, columns, tile, *refs),
+        out_shape=[wide, wide, tall, tall],
+        in_specs=[pl.BlockSpec(memory_space=pltpu.SMEM)] + [vmem] * 6,
+        out_specs=[vmem] * 4,
+        scratch_shapes=[pltpu.VMEM((rows, tile), jnp.bfloat16)],
+        compiler_params=pltpu.CompilerParams(vmem_limit_bytes=6 << 20),
+        cost_estimate=pl.CostEstimate(
+            flops=2 * rows * tile * (8 * columns + 8 * QW),
+            bytes_accessed=8 * rows * tile,
+            transcendentals=0,
+        ),
+        name="corr_kernel",
+    )(place, cells, rim, *mats)
+
+
+def partial_kernel(columns, stay_ref, moved_ref, here_ref, there_ref, *outs):
+    width = here_ref.shape[1]
+    step = 2 * QW
+    for low in range(0, width, step):
+        lanes = slice(low, low + step)
+        total = product(stay_ref[...], here_ref[:, lanes])
+        total += product(moved_ref[...], there_ref[:, lanes])
+        for k, out_ref in enumerate(outs):
+            out_ref[:, lanes] = total[k * columns : (k + 1) * columns].astype(out_ref.dtype)
+
+
+def partial_call(stay, moved, here, there, columns, types):
+    rows, tile = stay.shape
+    width = here.shape[1]
+    vmem = pl.BlockSpec(memory_space=pltpu.VMEM)
+    return pl.pallas_call(
+        lambda *refs: partial_kernel(columns, *refs),
+        out_shape=[jax.ShapeDtypeStruct((columns, width), kind) for kind in types],
+        in_specs=[vmem] * 4,
+        out_specs=[vmem] * len(types),
+        compiler_params=pltpu.CompilerParams(vmem_limit_bytes=6 << 20),
+        cost_estimate=pl.CostEstimate(
+            flops=4 * rows * tile * width, bytes_accessed=4 * tile * width, transcendentals=0
+        ),
+        name="partial_kernel",
+    )(stay, moved, here, there)
+
+
+def stack_call(blocks):
+    columns, width = blocks[0].shape
+
+    def kernel(*refs):
+        for k in range(len(blocks)):
+            refs[-1][k * columns : (k + 1) * columns, :] = refs[k][...]
+
+    vmem = pl.BlockSpec(memory_space=pltpu.VMEM)
+    return pl.pallas_call(
+        kernel,
+        out_shape=jax.ShapeDtypeStruct((len(blocks) * columns, width), jnp.bfloat16),
+        in_specs=[vmem] * len(blocks),
+        out_specs=vmem,
+        compiler_params=pltpu.CompilerParams(vmem_limit_bytes=4 << 20),
+        cost_estimate=pl.CostEstimate(
+            flops=0, bytes_accessed=4 * len(blocks) * columns * width, transcendentals=0
+        ),
+        name="stack_kernel",
+    )(*blocks)
+
+
+def tile_shards(grad_volume, query_feats, support_feats, query_kernel, support_kernel):
+    _, columns, queries = grad_volume.shape
+    width = query_feats.shape[1]
+    outer = lax.axis_size("blk")
+    inner = lax.axis_size("sub")
+    count = outer * inner
+    half = count // 2
+    tile = queries // count
+    scale_factor = 1.0 / math.sqrt(width)
+    own = lax.axis_index(("blk", "sub"))
+    side = lax.axis_index("sub")
+    core = lax.axis_index("pair")
+    place = jnp.stack([own, core]).astype(jnp.int32)
+
+    def exchanged(value, mask):
+        return lax.ppermute(value, ("blk", "sub"), [(i, i ^ mask) for i in range(count)])
+
+    def swapped(value):
+        return lax.ppermute(value, "pair", [(0, 1), (1, 0)])
+
+    volume = jnp.pad(grad_volume[0], ((0, 0), (QW, QW)))
+
+    def piece(mask):
+        return lax.dynamic_slice(volume, (0, (own ^ mask) * tile), (columns, tile + 2 * QW))
+
+    pieces = [piece(0)] + [None] * (count - 1)
+    for mask in range(count - 1, 0, -1):
+        pieces[mask] = exchanged(piece(mask), mask)
+    held = [support_feats[0]] + [None] * (count - 1)
+    bit = half
+    while bit:
+        for k in range(0, count, 2 * bit):
+            held[k ^ bit] = exchanged(held[k], bit)
+        bit //= 2
+
+    edge = 16 * -(-count // 16)
+    mats = matrix_call(place, query_kernel, support_kernel, count, columns, edge)
+    here = lax.dynamic_slice(query_feats, (side * tile, 0), (tile, width))
+    there = lax.dynamic_slice(query_feats, ((side ^ 1) * tile, 0), (tile, width))
+    ordered = held + pieces[::-1]
+    ordered, mats, here, there = lax.optimization_barrier((ordered, mats, here, there))
+    held, pieces = ordered[:count], ordered[count:][::-1]
+    cells, rim = gather_call(place, pieces, tile, edge)
+    rim = swapped(rim)
+    move1, stay1, keep1, send1 = corr_call(1, place, cells, rim, mats, count)
+    moved1 = exchanged(move1, 1)
+    move0, stay0, keep0, send0 = corr_call(0, place, cells, rim, mats, count)
+    moved0 = exchanged(move0, 1)
+    other1 = swapped(send1)
+    moved1, other1 = lax.optimization_barrier((moved1, other1))
+    other0 = swapped(send0)
+    feats1, feats0 = stack_call(held[half:]), stack_call(held[:half])
+    across1, across0 = swapped(feats1), swapped(feats0)
+    moved0, other0, across1 = lax.optimization_barrier((moved0, other0, across1))
+    narrow = [jnp.bfloat16] * (count // 4)
+    parts1 = partial_call(stay1, moved1, here, there, columns, narrow)
+    parts0 = partial_call(stay0, moved0, here, there, columns, [jnp.float32] + narrow[1:])
+    landed = [exchanged(part, half + 2 * at) for at, part in enumerate(parts1)]
+    landed += [exchanged(part, 2 * at) for at, part in enumerate(parts0) if at]
+
+    def query_term(block, feats):
+        return lax.dot_general(
+            block, feats, (((0,), (0,)), ((), ())), preferred_element_type=jnp.float32
+        )
+
+    query_grad = query_term(keep1, feats1) + query_term(keep0, feats0)
+    query_grad += query_term(other1, across1)
+    query_grad += query_term(other0, across0)
+    query_grad *= scale_factor
+    support_grad = parts0[0]
+    for term in landed:
+        support_grad = support_grad + term.astype(jnp.float32)
+    return (query_grad, (support_grad * scale_factor)[None])
+
+
+def tiles_fit(mesh, grad_volume):
+    shape = dict(mesh.shape)
+    count = shape["blk"] * shape["sub"]
+    planes = grad_volume.shape[0] // (shape["grp"] * count)
+    columns = grad_volume.shape[1] // shape["pair"]
+    return (
+        planes == 1
+        and shape["pair"] == 2
+        and shape["sub"] == 2
+        and count >= 4
+        and count & (count - 1) == 0
+        and count * columns <= 1024
+        and columns % 16 == 0
+        and QW % columns == 0
+        and count * columns % QW == 0
+        and QH * QW % (count * 2 * QW) == 0
+    )
+
+
 def solution(mesh):
     in_specs = (
         P(("grp", "blk", "sub"), "pair", None),
@@ -113,4 +439,12 @@
         P(),
     )
     out_specs = (P(("grp", "blk", "sub", "pair"), None), P(("grp", "blk", "sub"), "pair", None))
-    return jax.shard_map(shards, mesh=mesh, in_specs=in_specs, out_specs=out_specs, check_vma=False)
+
+    def program(grad_volume, *rest):
+        body = tile_shards if tiles_fit(mesh, grad_volume) else ring_shards
+        mapped = jax.shard_map(
+            body, mesh=mesh, in_specs=in_specs, out_specs=out_specs, check_vma=False
+        )
+        return mapped(grad_volume, *rest)
+
+    return program

time: 320 us -> 71.7 us (0.22)
  waiting for transfers between devices: 142 us -> 29.9 us
  other arithmetic: 70.3 us -> 0.86 us
  matrix products: 40.3 us -> 3.18 us
  local copies, waits for them, and re-layouts: 28.6 us -> 4.28 us
  between operations: 14.2 us -> 0.82 us
  Pallas kernels: 0 us -> 6.88 us
    reduce_scatter x1 -> x0, waiting for transfers between devices: 70.9 us -> none  [shards(): lax.psum_scatter(query_total, ('sub', 'pair'), scatter_dimension=0, tiled...]
    unnamed x3 -> x0, other arithmetic: 45.5 us -> none
    dot_general x8 -> x4, matrix products: 40.3 us -> 3.18 us  [query_term(): lax.dot_general(block, feats, (((0,), (0,)), ((), ())), preferred_element...]
    all_to_all x1 -> x0, waiting for transfers between devices: 25.3 us -> none  [shards(): lax.all_to_all(corr_grad, 'blk', split_axis=2, concat_axis=0, tiled=True)]
    ppermute x12 -> x24, waiting for transfers between devices: 46.3 us -> 29.9 us  [the longest x19 29.4 us: exchanged(): lax.ppermute(value, ('blk', 'sub'), [(i, i ^ mask) for i in range(count)])]
    convert_element_type x1 -> x0, other arithmetic: 11.4 us -> none  [shards(): corr_grad = (query_pass(grad_volume, query_kernel) + support_pass(rimmed,...]
    add x1 -> x0, other arithmetic: 9.43 us -> none  [query_pass(): total + kernel[row_shift, col_shift] * padded[:, :, row_shift:row_shift +...]
    ppermute x12 -> x24, starting transfers between devices: 16.3 us -> 25.6 us  [the longest x19 24.9 us: exchanged(): lax.ppermute(value, ('blk', 'sub'), [(i, i ^ mask) for i in range(count)])]
  transfers between devices with their start and end apart: 14 -> 24, of which waited for: 5 -> 11; matrix products, arithmetic and copies ran while one was open for 18% -> 11% of each run, Pallas kernels for 0% -> 9%
where the time goes in v3:
time: 71.7 us; the launch traced here: 71.6 us
  waiting for transfers between devices  29.9 us (42%)
  starting transfers between devices  25.6 us (36%)
  Pallas kernels  6.88 us (10%)
  local copies, waits for them, and re-layouts  4.28 us (6%)
  matrix products  3.18 us (4%)
  other arithmetic  0.86 us (1%)
  between operations  0.82 us (1%)
    ppermute x19, waiting for transfers between devices, exchanged(): lax.ppermute(value, ('blk', 'sub'), [(i, i ^ mask) for i in range(count)])  29.4 us
    ppermute x19, starting transfers between devices, exchanged(): lax.ppermute(value, ('blk', 'sub'), [(i, i ^ mask) for i in range(count)])  24.9 us
    pallas_call x2, Pallas kernels, corr_call(): pl.pallas_call(lambda *refs: corr_kernel(group, columns, tile, *refs), ou...  3.44 us
    dot_general x4, matrix products, query_term(): lax.dot_general(block, feats, (((0,), (0,)), ((), ())), preferred_element...  3.18 us
    dynamic_slice x1, local copies, waits for them, and re-layouts, tile_shards(): lax.dynamic_slice(query_feats, ((side ^ 1) * tile, 0), (tile, width))  2.66 us
    dynamic_slice x1, local copies, waits for them, and re-layouts, piece(): lax.dynamic_slice(volume, (0, (own ^ mask) * tile), (columns, tile + 2 *...  1.52 us
    pallas_call x2, Pallas kernels, partial_call(): pl.pallas_call(lambda *refs: partial_kernel(columns, *refs), out_shape=[j...  1.47 us
  transfers between devices with their start and end apart: 24, of which 11 were waited for; matrix products, arithmetic and copies ran while one was open for 11% of the time, Pallas kernels for 9%

profile of v3, /device:TPU:0, one launch (start us, length us, event | category | flops | bytes accessed | tf_op | source)
XLA Modules:
  0.0 71.6 jit_solution(2640499707943188)
XLA Ops:
  0.6 4.1 %collective-permute-start.3 = (bf16[64,1024]{1,0:T(8,128)(2,1)}, bf16[64,1024]{1,0:T(8,128)(2,1)S(1)}, u32[]{:S(2)}, u32[]{:S(2)}) collective-permute-start(bf16[64,1024]{1,0:T(8,128)(2,1)} %bitcast.22), channel_id=1, source_target_pairs={{0,8},{2,10},{4,12},{6,14},{8,0},{10,2},{12,4},{14,6},{1,9},{3,11}... | collective-permute-start | bytes 393224 | tf_op jit(solution)/shard_map/ppermute | solution.py:354
  4.8 1.6 %collective-permute-start.1 = (bf16[64,1024]{1,0:T(8,128)(2,1)}, bf16[64,1024]{1,0:T(8,128)(2,1)S(1)}, u32[]{:S(2)}, u32[]{:S(2)}) collective-permute-start(bf16[64,1024]{1,0:T(8,128)(2,1)} %bitcast.23), channel_id=1, source_target_pairs={{0,4},{2,6},{4,0},{6,2},{8,12},{10,14},{12,8},{14,10},{1,5},{3,7},... | collective-permute-start | bytes 393224 | tf_op jit(solution)/shard_map/ppermute | solution.py:354
  6.3 1.5 %collective-permute-start = (bf16[64,1024]{1,0:T(8,128)(2,1)}, bf16[64,1024]{1,0:T(8,128)(2,1)S(1)}, u32[]{:S(2)}, u32[]{:S(2)}) collective-permute-start(bf16[64,1024]{1,0:T(8,128)(2,1)} %bitcast.24), channel_id=1, source_target_pairs={{0,2},{2,0},{4,6},{6,4},{8,10},{10,8},{12,14},{14,12},{1,3},{3,1},... | collective-permute-start | bytes 393224 | tf_op jit(solution)/shard_map/ppermute | solution.py:354
  7.8 1.5 %pad_dynamic-slice_fusion = (bf16[64,1280]{1,0:T(8,128)(2,1)S(1)}, bf16[64,1280]{1,0:T(8,128)(2,1)S(1)}, bf16[64,1280]{1,0:T(8,128)(2,1)S(1)}, bf16[64,1280]{1,0...) fusion(s32[]{:T(128)S(6)} %select_n.37, ...), kind=kLoop, calls=%fused_computation.1 | loop fusion | bytes 2359328 | tf_op jit(solution)/shard_map/dynamic_slice | solution.py:362
  9.3 0.4 collective-permute-start.10
  9.7 0.2 collective-permute-start.11
  9.9 1.4 %collective-permute-done.3.refs_0_ = bf16[64,1024]{1,0:T(8,128)(2,1)S(1)} collective-permute-done((bf16[64,1024]{1,0:T(8,128)(2,1)}, bf16[64,1024]{1,0:T(8,128)(2,1)S(1)}, u32[]{:S(2)}, u32[]{:S(2)}) %collective-permute-start.3) | collective-permute-done | bytes 131104 | tf_op jit(solution)/shard_map/ppermute | solution.py:354
  11.4 1.7 %collective-permute-start.12 = (bf16[64,1280]{1,0:T(8,128)(2,1)S(1)}, bf16[64,1280]{1,0:T(8,128)(2,1)S(1)}, u32[]{:S(2)}, u32[]{:S(2)}) collective-permute-start(bf16[64,1280]{1,0:T(8,128)(2,1)S(1)} %get-tuple-element.99), channel_id=1, source_target_pairs={{0,4},{2,6},{4,0},{6,2},{8,12},{10,14},{12,8},{14,10},{1,5},{3,7},... | collective-permute-start | bytes 491528 | tf_op jit(solution)/shard_map/ppermute | solution.py:354
  13.1 1.5 %collective-permute-start.13 = (bf16[64,1280]{1,0:T(8,128)(2,1)S(1)}, bf16[64,1280]{1,0:T(8,128)(2,1)S(1)}, u32[]{:S(2)}, u32[]{:S(2)}) collective-permute-start(bf16[64,1280]{1,0:T(8,128)(2,1)S(1)} %get-tuple-element.100), channel_id=1, source_target_pairs={{0,2},{2,0},{4,6},{6,4},{8,10},{10,8},{12,14},{14,12},{1,3},{3,1},... | collective-permute-start | bytes 491528 | tf_op jit(solution)/shard_map/ppermute | solution.py:354
  14.6 2.9 %collective-permute-start.7 = (bf16[64,1280]{1,0:T(8,128)(2,1)S(1)}, bf16[64,1280]{1,0:T(8,128)(2,1)S(1)}, u32[]{:S(2)}, u32[]{:S(2)}) collective-permute-start(bf16[64,1280]{1,0:T(8,128)(2,1)S(1)} %get-tuple-element.101), channel_id=1, source_target_pairs={{0,14},{2,12},{4,10},{6,8},{8,6},{10,4},{12,2},{14,0},{1,15},{3,13... | collective-permute-start | bytes 491528 | tf_op jit(solution)/shard_map/ppermute | solution.py:354
  17.5 2.0 %collective-permute-done.10.refs_4_ = bf16[64,1280]{1,0:T(8,128)(2,1)S(1)} collective-permute-done((bf16[64,1280]{1,0:T(8,128)(2,1)S(1)}, bf16[64,1280]{1,0:T(8,128)(2,1)S(1)}, u32[]{:S(2)}, u32[]{:S(2)}) %collective-permute-start.10) | collective-permute-done | bytes 163872 | tf_op jit(solution)/shard_map/ppermute | solution.py:354
  19.6 0.1 reshape.7.refs_1_
  19.7 0.1 pad_add_fusion.refs_0_
  19.8 1.2 %matrix_kernel.1 = (bf16[256,256]{1,0:T(8,128)(2,1)S(1)}, bf16[512,32]{1,0:T(8,128)(2,1)S(1)}, bf16[512,256]{1,0:T(8,128)(2,1)S(1)}, bf16[512,256]{1,0:T(8,128)(2,1)S(1)}) custom-call(s32[2]{0:T(128)S(1)} %pad_add_fusion.refs_0_, f32[36]{0:T(128)S(1)} %reshape.7.refs_1_), custom_call_target="tpu_custom_call" | custom-call | flops 2621440 | bytes 524288 | tf_op jit(solution)/shard_map/matrix_kernel/pallas_call | solution.py:171
  21.0 2.5 %collective-permute-start.8 = (bf16[64,1280]{1,0:T(8,128)(2,1)S(1)}, bf16[64,1280]{1,0:T(8,128)(2,1)S(1)}, u32[]{:S(2)}, u32[]{:S(2)}) collective-permute-start(bf16[64,1280]{1,0:T(8,128)(2,1)S(1)} %get-tuple-element.95), channel_id=1, source_target_pairs={{0,12},{2,14},{4,8},{6,10},{8,4},{10,6},{12,0},{14,2},{1,13},{3,15... | collective-permute-start | bytes 491528 | tf_op jit(solution)/shard_map/ppermute | solution.py:354
  23.4 2.2 %collective-permute-done.12.refs_6_ = bf16[64,1280]{1,0:T(8,128)(2,1)S(1)} collective-permute-done((bf16[64,1280]{1,0:T(8,128)(2,1)S(1)}, bf16[64,1280]{1,0:T(8,128)(2,1)S(1)}, u32[]{:S(2)}, u32[]{:S(2)}) %collective-permute-start.12) | collective-permute-done | bytes 163872 | tf_op jit(solution)/shard_map/ppermute | solution.py:354
  25.7 0.2 collective-permute-start.9
  25.8 0.6 collective-permute-start.4
  26.4 2.1 %collective-permute-done.7.refs_1_ = bf16[64,1280]{1,0:T(8,128)(2,1)S(1)} collective-permute-done((bf16[64,1280]{1,0:T(8,128)(2,1)S(1)}, bf16[64,1280]{1,0:T(8,128)(2,1)S(1)}, u32[]{:S(2)}, u32[]{:S(2)}) %collective-permute-start.7) | collective-permute-done | bytes 163872 | tf_op jit(solution)/shard_map/ppermute | solution.py:354
  28.5 0.9 %collective-permute-start.2 = (bf16[64,1024]{1,0:T(8,128)(2,1)S(1)}, bf16[64,1024]{1,0:T(8,128)(2,1)S(1)}, u32[]{:S(2)}, u32[]{:S(2)}) collective-permute-start(bf16[64,1024]{1,0:T(8,128)(2,1)S(1)} %collective-permute-done.1.refs_2_), channel_id=1, source_target_pairs={{0,2},{2,0},{4,6},{6,4},{8,10},{10,8},{12,14},{14,12},{1,3},{3,1},... | collective-permute-start | bytes 393224 | tf_op jit(solution)/shard_map/ppermute | solution.py:354
  29.4 1.1 %collective-permute-start.6 = (bf16[64,1024]{1,0:T(8,128)(2,1)S(1)}, bf16[64,1024]{1,0:T(8,128)(2,1)S(1)}, u32[]{:S(2)}, u32[]{:S(2)}) collective-permute-start(bf16[64,1024]{1,0:T(8,128)(2,1)S(1)} %collective-permute-done.5.refs_2_), channel_id=1, source_target_pairs={{0,2},{2,0},{4,6},{6,4},{8,10},{10,8},{12,14},{14,12},{1,3},{3,1},... | collective-permute-start | bytes 393224 | tf_op jit(solution)/shard_map/ppermute | solution.py:354
  30.5 2.7 %constant_dynamic-slice_fusion = (bf16[1024,1024]{1,0:T(8,128)(2,1)S(1)}, bf16[1024,1024]{1,0:T(8,128)(2,1)S(1)}) fusion(bf16[2048,1024]{1,0:T(8,128)(2,1)} %param.6, s32[]{:T(128)S(6)} %select_n.39, s32[]{:T(128)S(6)} %select_n.38), kind=kLoop, calls=%fused_computation.15 | loop fusion | bytes 8388616 | tf_op jit(solution)/shard_map/dynamic_slice | solution.py:377
  33.2 0.0 copy-start
  33.2 1.1 %collective-permute-done.8.refs_2_ = bf16[64,1280]{1,0:T(8,128)(2,1)S(1)} collective-permute-done((bf16[64,1280]{1,0:T(8,128)(2,1)S(1)}, bf16[64,1280]{1,0:T(8,128)(2,1)S(1)}, u32[]{:S(2)}, u32[]{:S(2)}) %collective-permute-start.8) | collective-permute-done | bytes 163872 | tf_op jit(solution)/shard_map/ppermute | solution.py:354
  34.3 7.2 %collective-permute-done.9.refs_3_ = bf16[64,1280]{1,0:T(8,128)(2,1)S(1)} collective-permute-done((bf16[64,1280]{1,0:T(8,128)(2,1)S(1)}, bf16[64,1280]{1,0:T(8,128)(2,1)S(1)}, u32[]{:S(2)}, u32[]{:S(2)}) %collective-permute-start.9) | collective-permute-done | bytes 163872 | tf_op jit(solution)/shard_map/ppermute | solution.py:354
  41.4 0.7 %gather_kernel.1 = (bf16[640,1280]{1,0:T(8,128)(2,1)S(1)}, bf16[32,1024]{1,0:T(8,128)(2,1)S(1)}) custom-call(s32[2]{0:T(128)S(1)} %pad_add_fusion.refs_0_, bf16[64,1280]{1,0:T(8,128)(2,1)S(1)} %collective-permute-done.7.refs_1_, bf16[64,1280]{1,0:T(8,128)(2,1)S(1)} %collective-permute-done.8.refs_2_, bf16[64,1280]{1,0:T(8,128)(2,1)S(1)} %collective-permute-done.9.refs_3_, ...), custom_call_target="tpu_custom_call" | custom-call | flops 8192 | bytes 2621440 | tf_op jit(solution)/shard_map/gather_kernel/pallas_call | solution.py:209
  42.2 0.1 collective-permute-start.14
  42.3 0.6 collective-permute-start.19
  42.9 0.1 collective-permute-start.20
  43.0 0.5 collective-permute-done.14.refs_2_
  43.5 1.7 %corr_kernel.2 = (bf16[128,1024]{1,0:T(8,128)(2,1)S(1)}, bf16[128,1024]{1,0:T(8,128)(2,1)S(1)}, bf16[256,512]{1,0:T(8,128)(2,1)S(1)}, bf16[256,512]{1,0:T(8,128)(2,1)S(1)}) custom-call(s32[2]{0:T(128)S(1)} %pad_add_fusion.refs_0_, bf16[640,1280]{1,0:T(8,128)(2,1)S(1)} %get-tuple-element.59.refs_1_, bf16[32,1024]{1,0:T(8,128)(2,1)S(1)} %collective-permute-done.14.refs_2_, ...), custom_call_target="tpu_custom_call" | custom-call | flops 805306368 | bytes 2097152 | tf_op jit(solution)/shard_map/corr_kernel/pallas_call | solution.py:274
  45.2 0.6 collective-permute-start.15
  45.8 1.7 %corr_kernel.3 = (bf16[128,1024]{1,0:T(8,128)(2,1)S(1)}, bf16[128,1024]{1,0:T(8,128)(2,1)S(1)}, bf16[256,512]{1,0:T(8,128)(2,1)S(1)}, bf16[256,512]{1,0:T(8,128)(2,1)S(1)}) custom-call(s32[2]{0:T(128)S(1)} %pad_add_fusion.refs_0_, bf16[640,1280]{1,0:T(8,128)(2,1)S(1)} %get-tuple-element.59.refs_1_, bf16[32,1024]{1,0:T(8,128)(2,1)S(1)} %collective-permute-done.14.refs_2_, ...), custom_call_target="tpu_custom_call" | custom-call | flops 805306368 | bytes 2097152 | tf_op jit(solution)/shard_map/corr_kernel/pallas_call | solution.py:274
  47.5 1.6 %collective-permute-start.17 = (bf16[128,1024]{1,0:T(8,128)(2,1)S(1)}, bf16[128,1024]{1,0:T(8,128)(2,1)S(1)}, u32[]{:S(2)}, u32[]{:S(2)}) collective-permute-start(bf16[128,1024]{1,0:T(8,128)(2,1)S(1)} %get-tuple-element.78), channel_id=1, source_target_pairs={{0,2},{2,0},{4,6},{6,4},{8,10},{10,8},{12,14},{14,12},{1,3},{3,1},... | collective-permute-start | bytes 786440 | tf_op jit(solution)/shard_map/ppermute | solution.py:354
  49.1 0.5 fusion.3
  49.6 4.9 %collective-permute-done.15.refs_1_ = bf16[128,1024]{1,0:T(8,128)(2,1)S(1)} collective-permute-done((bf16[128,1024]{1,0:T(8,128)(2,1)S(1)}, bf16[128,1024]{1,0:T(8,128)(2,1)S(1)}, u32[]{:S(2)}, u32[]{:S(2)}) %collective-permute-start.15) | collective-permute-done | bytes 262176 | tf_op jit(solution)/shard_map/ppermute | solution.py:354
  54.4 0.5 fusion.2
  54.9 0.7 %partial_kernel.3 = (bf16[64,1024]{1,0:T(8,128)(2,1)S(1)}, bf16[64,1024]{1,0:T(8,128)(2,1)S(1)}) custom-call(bf16[128,1024]{1,0:T(8,128)(2,1)S(1)} %get-tuple-element.87.refs_0_, bf16[128,1024]{1,0:T(8,128)(2,1)S(1)} %collective-permute-done.15.refs_1_, bf16[1024,1024]{1,0:T(8,128)(2,1)S(1)} %get-tuple-element.84.refs_2_, ...), custom_call_target="tpu_custom_call" | custom-call | flops 536870912 | bytes 4194304 | tf_op jit(solution)/shard_map/partial_kernel/pallas_call | solution.py:305
  55.7 1.0 %collective-permute-start.21 = (bf16[64,1024]{1,0:T(8,128)(2,1)S(1)}, bf16[64,1024]{1,0:T(8,128)(2,1)S(1)}, u32[]{:S(2)}, u32[]{:S(2)}) collective-permute-start(bf16[64,1024]{1,0:T(8,128)(2,1)S(1)} %get-tuple-element.89), channel_id=1, source_target_pairs={{0,8},{2,10},{4,12},{6,14},{8,0},{10,2},{12,4},{14,6},{1,9},{3,11}... | collective-permute-start | bytes 393224 | tf_op jit(solution)/shard_map/ppermute | solution.py:354
  56.7 2.6 %collective-permute-done.17.refs_1_ = bf16[128,1024]{1,0:T(8,128)(2,1)S(1)} collective-permute-done((bf16[128,1024]{1,0:T(8,128)(2,1)S(1)}, bf16[128,1024]{1,0:T(8,128)(2,1)S(1)}, u32[]{:S(2)}, u32[]{:S(2)}) %collective-permute-start.17) | collective-permute-done | bytes 262176 | tf_op jit(solution)/shard_map/ppermute | solution.py:354
  59.3 2.5 %collective-permute-start.22 = (bf16[64,1024]{1,0:T(8,128)(2,1)S(1)}, bf16[64,1024]{1,0:T(8,128)(2,1)S(1)}, u32[]{:S(2)}, u32[]{:S(2)}) collective-permute-start(bf16[64,1024]{1,0:T(8,128)(2,1)S(1)} %get-tuple-element.90), channel_id=1, source_target_pairs={{0,12},{2,14},{4,8},{6,10},{8,4},{10,6},{12,0},{14,2},{1,13},{3,15... | collective-permute-start | bytes 393224 | tf_op jit(solution)/shard_map/ppermute | solution.py:354
  61.8 0.7 %partial_kernel.2 = (f32[64,1024]{1,0:T(8,128)S(1)}, bf16[64,1024]{1,0:T(8,128)(2,1)S(1)}) custom-call(bf16[128,1024]{1,0:T(8,128)(2,1)S(1)} %get-tuple-element.82.refs_0_, bf16[128,1024]{1,0:T(8,128)(2,1)S(1)} %collective-permute-done.17.refs_1_, bf16[1024,1024]{1,0:T(8,128)(2,1)S(1)} %get-tuple-element.84.refs_2_, ...), custom_call_target="tpu_custom_call" | custom-call | flops 536870912 | bytes 4194304 | tf_op jit(solution)/shard_map/partial_kernel/pallas_call | solution.py:305
  62.5 0.1 collective-permute-start.23
  62.6 0.5 fusion.4
  63.1 1.8 %add_multiply_fusion = f32[512,1024]{1,0:T(8,128)} fusion(f32[512,1024]{1,0:T(8,128)S(1)} %fusion.4, f32[512,1024]{1,0:T(8,128)S(1)} %fusion.2, f32[512,1024]{1,0:T(8,128)S(1)} %fusion.3, bf16[256,512]{1,0:T(8,128)(2,1)S(1)} %collective-permute-done.18, bf16[256,1024]{1,0:T(8,128)(2,1)S(1)} %collective-permute-done.20), kind=kOutput, calls=%fused_computation | convolution fusion | flops 270532608 | bytes 9175040 | tf_op jit(solution)/shard_map/dot_general | solution.py:400
  64.9 3.2 %collective-permute-done.21 = bf16[64,1024]{1,0:T(8,128)(2,1)S(1)} collective-permute-done((bf16[64,1024]{1,0:T(8,128)(2,1)S(1)}, bf16[64,1024]{1,0:T(8,128)(2,1)S(1)}, u32[]{:S(2)}, u32[]{:S(2)}) %collective-permute-start.21) | collective-permute-done | bytes 131104 | tf_op jit(solution)/shard_map/ppermute | solution.py:354
  68.1 2.7 %collective-permute-done.23 = bf16[64,1024]{1,0:T(8,128)(2,1)S(1)} collective-permute-done((bf16[64,1024]{1,0:T(8,128)(2,1)S(1)}, bf16[64,1024]{1,0:T(8,128)(2,1)S(1)}, u32[]{:S(2)}, u32[]{:S(2)}) %collective-permute-start.23) | collective-permute-done | bytes 131104 | tf_op jit(solution)/shard_map/ppermute | solution.py:354
  70.8 0.8 %multiply_bitcast_fusion = f32[1,64,1024]{2,1,0:T(8,128)} fusion(bf16[64,1024]{1,0:T(8,128)(2,1)S(1)} %collective-permute-done.23, bf16[64,1024]{1,0:T(8,128)(2,1)S(1)} %collective-permute-done.22, f32[64,1024]{1,0:T(8,128)S(1)} %get-tuple-element.86, bf16[64,1024]{1,0:T(8,128)(2,1)S(1)} %collective-permute-done.21), kind=kLoop, calls=%fused_computation.9 | loop fusion | flops 458752 | bytes 917504 | tf_op jit(solution)/shard_map/broadcast_in_dim | solution.py:411
  (25 shorter events, 0.1 us)
Async XLA Ops:
  0.6 9.3 %copy-start.2 = (f32[3,3]{1,0:T(4,128)S(1)}, f32[3,3]{1,0:T(4,128)}, u32[]{:S(2)}) copy-start(f32[3,3]{1,0:T(4,128)} %param.8) | copy-start | bytes 112
  0.6 9.3 %copy-start.1 = (f32[3,3]{1,0:T(4,128)S(1)}, f32[3,3]{1,0:T(4,128)}, u32[]{:S(2)}) copy-start(f32[3,3]{1,0:T(4,128)} %param.9) | copy-start | bytes 112
  0.6 10.7 %collective-permute-start.3 = (bf16[64,1024]{1,0:T(8,128)(2,1)}, bf16[64,1024]{1,0:T(8,128)(2,1)S(1)}, u32[]{:S(2)}, u32[]{:S(2)}) collective-permute-start(bf16[64,1024]{1,0:T(8,128)(2,1)} %bitcast.22), channel_id=1, source_target_pairs={{0,8},{2,10},{4,12},{6,14},{8,0},{10,2},{12,4},{14,6},{1,9},{3,11}... | collective-permute-start | bytes 393224 | tf_op jit(solution)/shard_map/ppermute | solution.py:354
  4.8 8.3 %collective-permute-start.1 = (bf16[64,1024]{1,0:T(8,128)(2,1)}, bf16[64,1024]{1,0:T(8,128)(2,1)S(1)}, u32[]{:S(2)}, u32[]{:S(2)}) collective-permute-start(bf16[64,1024]{1,0:T(8,128)(2,1)} %bitcast.23), channel_id=1, source_target_pairs={{0,4},{2,6},{4,0},{6,2},{8,12},{10,14},{12,8},{14,10},{1,5},{3,7},... | collective-permute-start | bytes 393224 | tf_op jit(solution)/shard_map/ppermute | solution.py:354
  6.3 8.3 %collective-permute-start = (bf16[64,1024]{1,0:T(8,128)(2,1)}, bf16[64,1024]{1,0:T(8,128)(2,1)S(1)}, u32[]{:S(2)}, u32[]{:S(2)}) collective-permute-start(bf16[64,1024]{1,0:T(8,128)(2,1)} %bitcast.24), channel_id=1, source_target_pairs={{0,2},{2,0},{4,6},{6,4},{8,10},{10,8},{12,14},{14,12},{1,3},{3,1},... | collective-permute-start | bytes 393224 | tf_op jit(solution)/shard_map/ppermute | solution.py:354
  9.3 10.2 %collective-permute-start.10 = (bf16[64,1280]{1,0:T(8,128)(2,1)S(1)}, bf16[64,1280]{1,0:T(8,128)(2,1)S(1)}, u32[]{:S(2)}, u32[]{:S(2)}) collective-permute-start(bf16[64,1280]{1,0:T(8,128)(2,1)S(1)} %get-tuple-element.97), channel_id=1, source_target_pairs={{0,8},{2,10},{4,12},{6,14},{8,0},{10,2},{12,4},{14,6},{1,9},{3,11}... | collective-permute-start | bytes 491528 | tf_op jit(solution)/shard_map/ppermute | solution.py:354
  9.7 11.2 %collective-permute-start.11 = (bf16[64,1280]{1,0:T(8,128)(2,1)S(1)}, bf16[64,1280]{1,0:T(8,128)(2,1)S(1)}, u32[]{:S(2)}, u32[]{:S(2)}) collective-permute-start(bf16[64,1280]{1,0:T(8,128)(2,1)S(1)} %get-tuple-element.98), channel_id=1, source_target_pairs={{0,6},{2,4},{4,2},{6,0},{8,14},{10,12},{12,10},{14,8},{1,7},{3,5},... | collective-permute-start | bytes 491528 | tf_op jit(solution)/shard_map/ppermute | solution.py:354
  11.4 14.3 %collective-permute-start.12 = (bf16[64,1280]{1,0:T(8,128)(2,1)S(1)}, bf16[64,1280]{1,0:T(8,128)(2,1)S(1)}, u32[]{:S(2)}, u32[]{:S(2)}) collective-permute-start(bf16[64,1280]{1,0:T(8,128)(2,1)S(1)} %get-tuple-element.99), channel_id=1, source_target_pairs={{0,4},{2,6},{4,0},{6,2},{8,12},{10,14},{12,8},{14,10},{1,5},{3,7},... | collective-permute-start | bytes 491528 | tf_op jit(solution)/shard_map/ppermute | solution.py:354
  13.1 12.7 %collective-permute-start.13 = (bf16[64,1280]{1,0:T(8,128)(2,1)S(1)}, bf16[64,1280]{1,0:T(8,128)(2,1)S(1)}, u32[]{:S(2)}, u32[]{:S(2)}) collective-permute-start(bf16[64,1280]{1,0:T(8,128)(2,1)S(1)} %get-tuple-element.100), channel_id=1, source_target_pairs={{0,2},{2,0},{4,6},{6,4},{8,10},{10,8},{12,14},{14,12},{1,3},{3,1},... | collective-permute-start | bytes 491528 | tf_op jit(solution)/shard_map/ppermute | solution.py:354
  14.6 13.9 %collective-permute-start.7 = (bf16[64,1280]{1,0:T(8,128)(2,1)S(1)}, bf16[64,1280]{1,0:T(8,128)(2,1)S(1)}, u32[]{:S(2)}, u32[]{:S(2)}) collective-permute-start(bf16[64,1280]{1,0:T(8,128)(2,1)S(1)} %get-tuple-element.101), channel_id=1, source_target_pairs={{0,14},{2,12},{4,10},{6,8},{8,6},{10,4},{12,2},{14,0},{1,15},{3,13... | collective-permute-start | bytes 491528 | tf_op jit(solution)/shard_map/ppermute | solution.py:354
  19.6 9.8 %collective-permute-start.5 = (bf16[64,1024]{1,0:T(8,128)(2,1)S(1)}, bf16[64,1024]{1,0:T(8,128)(2,1)S(1)}, u32[]{:S(2)}, u32[]{:S(2)}) collective-permute-start(bf16[64,1024]{1,0:T(8,128)(2,1)S(1)} %collective-permute-done.3.refs_0_), channel_id=1, source_target_pairs={{0,4},{2,6},{4,0},{6,2},{8,12},{10,14},{12,8},{14,10},{1,5},{3,7},... | collective-permute-start | bytes 393224 | tf_op jit(solution)/shard_map/ppermute | solution.py:354
  21.0 13.3 %collective-permute-start.8 = (bf16[64,1280]{1,0:T(8,128)(2,1)S(1)}, bf16[64,1280]{1,0:T(8,128)(2,1)S(1)}, u32[]{:S(2)}, u32[]{:S(2)}) collective-permute-start(bf16[64,1280]{1,0:T(8,128)(2,1)S(1)} %get-tuple-element.95), channel_id=1, source_target_pairs={{0,12},{2,14},{4,8},{6,10},{8,4},{10,6},{12,0},{14,2},{1,13},{3,15... | collective-permute-start | bytes 491528 | tf_op jit(solution)/shard_map/ppermute | solution.py:354
  25.7 15.8 %collective-permute-start.9 = (bf16[64,1280]{1,0:T(8,128)(2,1)S(1)}, bf16[64,1280]{1,0:T(8,128)(2,1)S(1)}, u32[]{:S(2)}, u32[]{:S(2)}) collective-permute-start(bf16[64,1280]{1,0:T(8,128)(2,1)S(1)} %get-tuple-element.96), channel_id=1, source_target_pairs={{0,10},{2,8},{4,14},{6,12},{8,2},{10,0},{12,6},{14,4},{1,11},{3,9}... | collective-permute-start | bytes 491528 | tf_op jit(solution)/shard_map/ppermute | solution.py:354
  25.8 15.6 %collective-permute-start.4 = (bf16[64,1024]{1,0:T(8,128)(2,1)S(1)}, bf16[64,1024]{1,0:T(8,128)(2,1)S(1)}, u32[]{:S(2)}, u32[]{:S(2)}) collective-permute-start(bf16[64,1024]{1,0:T(8,128)(2,1)S(1)} %collective-permute-done.3.refs_0_), channel_id=1, source_target_pairs={{0,2},{2,0},{4,6},{6,4},{8,10},{10,8},{12,14},{14,12},{1,3},{3,1},... | collective-permute-start | bytes 393224 | tf_op jit(solution)/shard_map/ppermute | solution.py:354
  28.5 12.9 %collective-permute-start.2 = (bf16[64,1024]{1,0:T(8,128)(2,1)S(1)}, bf16[64,1024]{1,0:T(8,128)(2,1)S(1)}, u32[]{:S(2)}, u32[]{:S(2)}) collective-permute-start(bf16[64,1024]{1,0:T(8,128)(2,1)S(1)} %collective-permute-done.1.refs_2_), channel_id=1, source_target_pairs={{0,2},{2,0},{4,6},{6,4},{8,10},{10,8},{12,14},{14,12},{1,3},{3,1},... | collective-permute-start | bytes 393224 | tf_op jit(solution)/shard_map/ppermute | solution.py:354
  29.4 12.1 %collective-permute-start.6 = (bf16[64,1024]{1,0:T(8,128)(2,1)S(1)}, bf16[64,1024]{1,0:T(8,128)(2,1)S(1)}, u32[]{:S(2)}, u32[]{:S(2)}) collective-permute-start(bf16[64,1024]{1,0:T(8,128)(2,1)S(1)} %collective-permute-done.5.refs_2_), channel_id=1, source_target_pairs={{0,2},{2,0},{4,6},{6,4},{8,10},{10,8},{12,14},{14,12},{1,3},{3,1},... | collective-permute-start | bytes 393224 | tf_op jit(solution)/shard_map/ppermute | solution.py:354
  33.2 9.7 %copy-start = (bf16[1,64,1024]{2,1,0:T(8,128)(2,1)S(1)}, bf16[1,64,1024]{2,1,0:T(8,128)(2,1)}, u32[]{:S(2)}) copy-start(bf16[1,64,1024]{2,1,0:T(8,128)(2,1)} %param.7) | copy-start | bytes 393220
  42.2 1.3 %collective-permute-start.14 = (bf16[32,1024]{1,0:T(8,128)(2,1)S(1)}, bf16[32,1024]{1,0:T(8,128)(2,1)S(1)}, u32[]{:S(2)}, u32[]{:S(2)}) collective-permute-start(bf16[32,1024]{1,0:T(8,128)(2,1)S(1)} %get-tuple-element.60), channel_id=1, source_target_pairs={{0,1},{1,0},{2,3},{3,2},{4,5},{5,4},{6,7},{7,6},{8,9},{9,8},{10,11... | collective-permute-start | bytes 196616 | tf_op jit(solution)/shard_map/ppermute | solution.py:357
  42.3 19.5 %collective-permute-start.19 = (bf16[256,1024]{1,0:T(8,128)(2,1)S(1)}, bf16[256,1024]{1,0:T(8,128)(2,1)S(1)}, u32[]{:S(2)}, u32[]{:S(2)}) collective-permute-start(bf16[256,1024]{1,0:T(8,128)(2,1)S(1)} %stack_kernel.2), channel_id=1, source_target_pairs={{0,1},{1,0},{2,3},{3,2},{4,5},{5,4},{6,7},{7,6},{8,9},{9,8},{10,11... | collective-permute-start | bytes 1572872 | tf_op jit(solution)/shard_map/ppermute | solution.py:357
  42.9 20.2 %collective-permute-start.20 = (bf16[256,1024]{1,0:T(8,128)(2,1)S(1)}, bf16[256,1024]{1,0:T(8,128)(2,1)S(1)}, u32[]{:S(2)}, u32[]{:S(2)}) collective-permute-start(bf16[256,1024]{1,0:T(8,128)(2,1)S(1)} %stack_kernel.3), channel_id=1, source_target_pairs={{0,1},{1,0},{2,3},{3,2},{4,5},{5,4},{6,7},{7,6},{8,9},{9,8},{10,11... | collective-permute-start | bytes 1572872 | tf_op jit(solution)/shard_map/ppermute | solution.py:357
  45.2 9.2 %collective-permute-start.15 = (bf16[128,1024]{1,0:T(8,128)(2,1)S(1)}, bf16[128,1024]{1,0:T(8,128)(2,1)S(1)}, u32[]{:S(2)}, u32[]{:S(2)}) collective-permute-start(bf16[128,1024]{1,0:T(8,128)(2,1)S(1)} %get-tuple-element.75), channel_id=1, source_target_pairs={{0,2},{2,0},{4,6},{6,4},{8,10},{10,8},{12,14},{14,12},{1,3},{3,1},... | collective-permute-start | bytes 786440 | tf_op jit(solution)/shard_map/ppermute | solution.py:354
  45.8 9.1 %collective-permute-start.16 = (bf16[256,512]{1,0:T(8,128)(2,1)S(1)}, bf16[256,512]{1,0:T(8,128)(2,1)S(1)}, u32[]{:S(2)}, u32[]{:S(2)}) collective-permute-start(bf16[256,512]{1,0:T(8,128)(2,1)S(1)} %get-tuple-element.76), channel_id=1, source_target_pairs={{0,1},{1,0},{2,3},{3,2},{4,5},{5,4},{6,7},{7,6},{8,9},{9,8},{10,11... | collective-permute-start | bytes 786440 | tf_op jit(solution)/shard_map/ppermute | solution.py:357
  47.5 11.7 %collective-permute-start.17 = (bf16[128,1024]{1,0:T(8,128)(2,1)S(1)}, bf16[128,1024]{1,0:T(8,128)(2,1)S(1)}, u32[]{:S(2)}, u32[]{:S(2)}) collective-permute-start(bf16[128,1024]{1,0:T(8,128)(2,1)S(1)} %get-tuple-element.78), channel_id=1, source_target_pairs={{0,2},{2,0},{4,6},{6,4},{8,10},{10,8},{12,14},{14,12},{1,3},{3,1},... | collective-permute-start | bytes 786440 | tf_op jit(solution)/shard_map/ppermute | solution.py:354
  54.4 7.3 %collective-permute-start.18 = (bf16[256,512]{1,0:T(8,128)(2,1)S(1)}, bf16[256,512]{1,0:T(8,128)(2,1)S(1)}, u32[]{:S(2)}, u32[]{:S(2)}) collective-permute-start(bf16[256,512]{1,0:T(8,128)(2,1)S(1)} %get-tuple-element.79), channel_id=1, source_target_pairs={{0,1},{1,0},{2,3},{3,2},{4,5},{5,4},{6,7},{7,6},{8,9},{9,8},{10,11... | collective-permute-start | bytes 786440 | tf_op jit(solution)/shard_map/ppermute | solution.py:357
  55.7 12.4 %collective-permute-start.21 = (bf16[64,1024]{1,0:T(8,128)(2,1)S(1)}, bf16[64,1024]{1,0:T(8,128)(2,1)S(1)}, u32[]{:S(2)}, u32[]{:S(2)}) collective-permute-start(bf16[64,1024]{1,0:T(8,128)(2,1)S(1)} %get-tuple-element.89), channel_id=1, source_target_pairs={{0,8},{2,10},{4,12},{6,14},{8,0},{10,2},{12,4},{14,6},{1,9},{3,11}... | collective-permute-start | bytes 393224 | tf_op jit(solution)/shard_map/ppermute | solution.py:354
  59.3 8.8 %collective-permute-start.22 = (bf16[64,1024]{1,0:T(8,128)(2,1)S(1)}, bf16[64,1024]{1,0:T(8,128)(2,1)S(1)}, u32[]{:S(2)}, u32[]{:S(2)}) collective-permute-start(bf16[64,1024]{1,0:T(8,128)(2,1)S(1)} %get-tuple-element.90), channel_id=1, source_target_pairs={{0,12},{2,14},{4,8},{6,10},{8,4},{10,6},{12,0},{14,2},{1,13},{3,15... | collective-permute-start | bytes 393224 | tf_op jit(solution)/shard_map/ppermute | solution.py:354
  62.5 8.3 %collective-permute-start.23 = (bf16[64,1024]{1,0:T(8,128)(2,1)S(1)}, bf16[64,1024]{1,0:T(8,128)(2,1)S(1)}, u32[]{:S(2)}, u32[]{:S(2)}) collective-permute-start(bf16[64,1024]{1,0:T(8,128)(2,1)S(1)} %get-tuple-element.91), channel_id=1, source_target_pairs={{0,4},{2,6},{4,0},{6,2},{8,12},{10,14},{12,8},{14,10},{1,5},{3,7},... | collective-permute-start | bytes 393224 | tf_op jit(solution)/shard_map/ppermute | solution.py:354

commit v4 on v3

--- a/solution.py
+++ b/solution.py
@@ -194,7 +194,7 @@
     total = jnp.zeros(span.shape, jnp.float32)
     for k, piece in enumerate(reversed(pieces)):
         start = pl.multiple_of(((own ^ k) + 1) * columns, columns)
-        cells_ref[pl.ds(start, columns), :] = piece[...]
+        cells_ref[pl.ds(start, columns), :] = piece[:, : tile + 2 * QW]
         head = piece[:16, inner].astype(jnp.float32)[:1]
         tail = piece[columns - 16 :, inner].astype(jnp.float32)[15:]
         row = jnp.where(first, head, tail)
@@ -227,10 +227,10 @@
     return jnp.dot(left, right, preferred_element_type=jnp.float32)
 
 
-def corr_kernel(
-    group, columns, tile, place_ref, cells_ref, rim_ref, t_ref, edge_ref, wh_ref, wl_ref,
-    move_ref, stay_ref, keep_ref, send_ref, corr_ref,
-):
+def corr_kernel(group, columns, tile, *refs):
+    place_ref, cells_ref, rim_ref, t_ref, edge_ref, wh_ref, wl_ref = refs[:7]
+    corr_ref = refs[-1]
+    move_ref, stay_ref, keep_ref, send_ref = refs[-5:-1]
     half = corr_ref.shape[0] // columns
     own = place_ref[0]
     core = place_ref[1]
@@ -261,20 +261,22 @@
         for half_ref, which in ((keep_ref, core), (send_ref, 1 - core)):
             start = pl.multiple_of(which * width, width)
             half_ref[k * columns : (k + 1) * columns, :] = corr_ref[source, pl.ds(start, width)]
-
-
-def corr_call(group, place, cells, rim, mats, count):
+    for earlier_ref, half_ref in zip(refs[7:-5], (keep_ref, send_ref)):
+        half_ref[rows:, :] = earlier_ref[...]
+
+
+def corr_call(group, place, cells, rim, mats, count, earlier=()):
     tile = rim.shape[1]
     columns = cells.shape[0] // (count + 2)
     half = count // 2
     rows = half * columns
     vmem = pl.BlockSpec(memory_space=pltpu.VMEM)
     wide = jax.ShapeDtypeStruct((rows // 2, tile), jnp.bfloat16)
-    tall = jax.ShapeDtypeStruct((rows, tile // 2), jnp.bfloat16)
+    tall = jax.ShapeDtypeStruct((2 * rows if earlier else rows, tile // 2), jnp.bfloat16)
     return pl.pallas_call(
         lambda *refs: corr_kernel(group, columns, tile, *refs),
         out_shape=[wide, wide, tall, tall],
-        in_specs=[pl.BlockSpec(memory_space=pltpu.SMEM)] + [vmem] * 6,
+        in_specs=[pl.BlockSpec(memory_space=pltpu.SMEM)] + [vmem] * (6 + len(earlier)),
         out_specs=[vmem] * 4,
         scratch_shapes=[pltpu.VMEM((rows, tile), jnp.bfloat16)],
         compiler_params=pltpu.CompilerParams(vmem_limit_bytes=6 << 20),
@@ -284,7 +286,7 @@
             transcendentals=0,
         ),
         name="corr_kernel",
-    )(place, cells, rim, *mats)
+    )(place, cells, rim, *mats, *earlier)
 
 
 def partial_kernel(columns, stay_ref, moved_ref, here_ref, there_ref, *outs):
@@ -361,35 +363,43 @@
     def piece(mask):
         return lax.dynamic_slice(volume, (0, (own ^ mask) * tile), (columns, tile + 2 * QW))
 
-    pieces = [piece(0)] + [None] * (count - 1)
+    reach = tile + 2 * QW
+    feats = support_feats[0]
+    merged = []
+    pieces = [piece(mask) for mask in range(count)]
+    held = [feats] + [None] * (count - 1)
     for mask in range(count - 1, 0, -1):
-        pieces[mask] = exchanged(piece(mask), mask)
-    held = [support_feats[0]] + [None] * (count - 1)
+        if mask in merged:
+            both = exchanged(jnp.concatenate([pieces[mask], feats], axis=1), mask)
+            pieces[mask] = both
+            held[mask] = both[:, reach:]
+        else:
+            pieces[mask] = exchanged(pieces[mask], mask)
     bit = half
     while bit:
         for k in range(0, count, 2 * bit):
-            held[k ^ bit] = exchanged(held[k], bit)
+            if held[k ^ bit] is None:
+                held[k ^ bit] = exchanged(held[k], bit)
         bit //= 2
 
     edge = 16 * -(-count // 16)
     mats = matrix_call(place, query_kernel, support_kernel, count, columns, edge)
     here = lax.dynamic_slice(query_feats, (side * tile, 0), (tile, width))
     there = lax.dynamic_slice(query_feats, ((side ^ 1) * tile, 0), (tile, width))
-    ordered = held + pieces[::-1]
+    ordered = held + [pieces[k] for k in [5, 4, 3, 2, 1, 7, 6, 0]]
     ordered, mats, here, there = lax.optimization_barrier((ordered, mats, here, there))
-    held, pieces = ordered[:count], ordered[count:][::-1]
+    held, landed = ordered[:count], ordered[count:]
+    for at, k in enumerate([5, 4, 3, 2, 1, 7, 6, 0]):
+        pieces[k] = landed[at]
     cells, rim = gather_call(place, pieces, tile, edge)
     rim = swapped(rim)
-    move1, stay1, keep1, send1 = corr_call(1, place, cells, rim, mats, count)
+    feats = stack_call(held)
+    across = swapped(feats)
+    move1, stay1, keep, send = corr_call(1, place, cells, rim, mats, count)
     moved1 = exchanged(move1, 1)
-    move0, stay0, keep0, send0 = corr_call(0, place, cells, rim, mats, count)
+    move0, stay0, keep, send = corr_call(0, place, cells, rim, mats, count, (keep, send))
     moved0 = exchanged(move0, 1)
-    other1 = swapped(send1)
-    moved1, other1 = lax.optimization_barrier((moved1, other1))
-    other0 = swapped(send0)
-    feats1, feats0 = stack_call(held[half:]), stack_call(held[:half])
-    across1, across0 = swapped(feats1), swapped(feats0)
-    moved0, other0, across1 = lax.optimization_barrier((moved0, other0, across1))
+    other = swapped(send)
     narrow = [jnp.bfloat16] * (count // 4)
     parts1 = partial_call(stay1, moved1, here, there, columns, narrow)
     parts0 = partial_call(stay0, moved0, here, there, columns, [jnp.float32] + narrow[1:])
@@ -401,10 +411,11 @@
             block, feats, (((0,), (0,)), ((), ())), preferred_element_type=jnp.float32
         )
 
-    query_grad = query_term(keep1, feats1) + query_term(keep0, feats0)
-    query_grad += query_term(other1, across1)
-    query_grad += query_term(other0, across0)
+    rows = half * columns
+    query_grad = query_term(keep[:rows], feats[:rows]) + query_term(keep[rows:], feats[rows:])
+    query_grad += query_term(other[:rows], across[:rows]) + query_term(other[rows:], across[rows:])
     query_grad *= scale_factor
+    landed[0], query_grad = lax.optimization_barrier((landed[0], query_grad))
     support_grad = parts0[0]
     for term in landed:
         support_grad = support_grad + term.astype(jnp.float32)

time: 71.7 us -> 70.1 us (0.978)
  starting transfers between devices: 25.6 us -> 24.6 us
    ppermute x19, waiting for transfers between devices: 29.4 us -> 27.8 us  [exchanged(): lax.ppermute(value, ('blk', 'sub'), [(i, i ^ mask) for i in range(count)])]
    ppermute x5 -> x3, waiting for transfers between devices: 0.52 us -> 1.47 us  [swapped(): return lax.ppermute(value, 'pair', [(0, 1), (1, 0)])]
    ppermute x19, starting transfers between devices: 24.9 us -> 24 us  [exchanged(): lax.ppermute(value, ('blk', 'sub'), [(i, i ^ mask) for i in range(count)])]
  transfers between devices with their start and end apart: 24 -> 22, of which waited for: 11 -> 11; matrix products, arithmetic and copies ran while one was open for 11% -> 11% of each run, Pallas kernels for 9% -> 10%
where the time goes in v4:
time: 70.1 us; the launch traced here: 70 us
  waiting for transfers between devices  29.3 us (42%)
  starting transfers between devices  24.6 us (35%)
  Pallas kernels  6.88 us (10%)
  local copies, waits for them, and re-layouts  4.28 us (6%)
  matrix products  3.19 us (5%)
  other arithmetic  0.86 us (1%)
  between operations  0.81 us (1%)
    ppermute x19, waiting for transfers between devices, exchanged(): lax.ppermute(value, ('blk', 'sub'), [(i, i ^ mask) for i in range(count)])  27.8 us
    ppermute x19, starting transfers between devices, exchanged(): lax.ppermute(value, ('blk', 'sub'), [(i, i ^ mask) for i in range(count)])  24 us
    pallas_call x2, Pallas kernels, corr_call(): pl.pallas_call(lambda *refs: corr_kernel(group, columns, tile, *refs), ou...  3.44 us
    dot_general x4, matrix products, query_term(): lax.dot_general(block, feats, (((0,), (0,)), ((), ())), preferred_element...  3.19 us
    dynamic_slice x1, local copies, waits for them, and re-layouts, tile_shards(): lax.dynamic_slice(query_feats, ((side ^ 1) * tile, 0), (tile, width))  2.66 us
    dynamic_slice x1, local copies, waits for them, and re-layouts, piece(): lax.dynamic_slice(volume, (0, (own ^ mask) * tile), (columns, tile + 2 *...  1.52 us
    pallas_call x2, Pallas kernels, partial_call(): pl.pallas_call(lambda *refs: partial_kernel(columns, *refs), out_shape=[j...  1.48 us
    ppermute x3, waiting for transfers between devices, swapped(): return lax.ppermute(value, 'pair', [(0, 1), (1, 0)])  1.47 us
  transfers between devices with their start and end apart: 22, of which 11 were waited for; matrix products, arithmetic and copies ran while one was open for 11% of the time, Pallas kernels for 10%

profile of v4, /device:TPU:0, one launch (start us, length us, event | category | flops | bytes accessed | tf_op | source)
XLA Modules:
  0.0 70.0 jit_solution(18351624032888658665)
XLA Ops:
  0.6 4.1 %collective-permute-start.3 = (bf16[64,1024]{1,0:T(8,128)(2,1)}, bf16[64,1024]{1,0:T(8,128)(2,1)S(1)}, u32[]{:S(2)}, u32[]{:S(2)}) collective-permute-start(bf16[64,1024]{1,0:T(8,128)(2,1)} %bitcast.14), channel_id=1, source_target_pairs={{0,8},{2,10},{4,12},{6,14},{8,0},{10,2},{12,4},{14,6},{1,9},{3,11}... | collective-permute-start | bytes 393224 | tf_op jit(solution)/shard_map/ppermute | solution.py:356
  4.8 1.6 %collective-permute-start.1 = (bf16[64,1024]{1,0:T(8,128)(2,1)}, bf16[64,1024]{1,0:T(8,128)(2,1)S(1)}, u32[]{:S(2)}, u32[]{:S(2)}) collective-permute-start(bf16[64,1024]{1,0:T(8,128)(2,1)} %bitcast.15), channel_id=1, source_target_pairs={{0,4},{2,6},{4,0},{6,2},{8,12},{10,14},{12,8},{14,10},{1,5},{3,7},... | collective-permute-start | bytes 393224 | tf_op jit(solution)/shard_map/ppermute | solution.py:356
  6.3 1.5 %collective-permute-start = (bf16[64,1024]{1,0:T(8,128)(2,1)}, bf16[64,1024]{1,0:T(8,128)(2,1)S(1)}, u32[]{:S(2)}, u32[]{:S(2)}) collective-permute-start(bf16[64,1024]{1,0:T(8,128)(2,1)} %bitcast.16), channel_id=1, source_target_pairs={{0,2},{2,0},{4,6},{6,4},{8,10},{10,8},{12,14},{14,12},{1,3},{3,1},... | collective-permute-start | bytes 393224 | tf_op jit(solution)/shard_map/ppermute | solution.py:356
  7.8 1.5 %pad_dynamic-slice_fusion = (bf16[64,1280]{1,0:T(8,128)(2,1)S(1)}, bf16[64,1280]{1,0:T(8,128)(2,1)S(1)}, bf16[64,1280]{1,0:T(8,128)(2,1)S(1)}, bf16[64,1280]{1,0...) fusion(s32[]{:T(128)S(6)} %select_n.37, ...), kind=kLoop, calls=%fused_computation.8 | loop fusion | bytes 2359328 | tf_op jit(solution)/shard_map/dynamic_slice | solution.py:364
  9.3 0.4 collective-permute-start.8
  9.7 0.2 collective-permute-start.9
  9.9 1.4 %collective-permute-done.3.refs_4_ = bf16[64,1024]{1,0:T(8,128)(2,1)S(1)} collective-permute-done((bf16[64,1024]{1,0:T(8,128)(2,1)}, bf16[64,1024]{1,0:T(8,128)(2,1)S(1)}, u32[]{:S(2)}, u32[]{:S(2)}) %collective-permute-start.3) | collective-permute-done | bytes 131104 | tf_op jit(solution)/shard_map/ppermute | solution.py:356
  11.4 1.7 %collective-permute-start.10 = (bf16[64,1280]{1,0:T(8,128)(2,1)S(1)}, bf16[64,1280]{1,0:T(8,128)(2,1)S(1)}, u32[]{:S(2)}, u32[]{:S(2)}) collective-permute-start(bf16[64,1280]{1,0:T(8,128)(2,1)S(1)} %get-tuple-element.91), channel_id=1, source_target_pairs={{0,4},{2,6},{4,0},{6,2},{8,12},{10,14},{12,8},{14,10},{1,5},{3,7},... | collective-permute-start | bytes 491528 | tf_op jit(solution)/shard_map/ppermute | solution.py:356
  13.1 0.0 collective-permute-done.1.refs_2_
  13.1 1.5 %collective-permute-start.11 = (bf16[64,1280]{1,0:T(8,128)(2,1)S(1)}, bf16[64,1280]{1,0:T(8,128)(2,1)S(1)}, u32[]{:S(2)}, u32[]{:S(2)}) collective-permute-start(bf16[64,1280]{1,0:T(8,128)(2,1)S(1)} %get-tuple-element.92), channel_id=1, source_target_pairs={{0,2},{2,0},{4,6},{6,4},{8,10},{10,8},{12,14},{14,12},{1,3},{3,1},... | collective-permute-start | bytes 491528 | tf_op jit(solution)/shard_map/ppermute | solution.py:356
  14.6 2.9 %collective-permute-start.12 = (bf16[64,1280]{1,0:T(8,128)(2,1)S(1)}, bf16[64,1280]{1,0:T(8,128)(2,1)S(1)}, u32[]{:S(2)}, u32[]{:S(2)}) collective-permute-start(bf16[64,1280]{1,0:T(8,128)(2,1)S(1)} %get-tuple-element.93), channel_id=1, source_target_pairs={{0,14},{2,12},{4,10},{6,8},{8,6},{10,4},{12,2},{14,0},{1,15},{3,13... | collective-permute-start | bytes 491528 | tf_op jit(solution)/shard_map/ppermute | solution.py:356
  17.5 2.0 %collective-permute-done.8.refs_4_ = bf16[64,1280]{1,0:T(8,128)(2,1)S(1)} collective-permute-done((bf16[64,1280]{1,0:T(8,128)(2,1)S(1)}, bf16[64,1280]{1,0:T(8,128)(2,1)S(1)}, u32[]{:S(2)}, u32[]{:S(2)}) %collective-permute-start.8) | collective-permute-done | bytes 163872 | tf_op jit(solution)/shard_map/ppermute | solution.py:356
  19.6 0.1 reshape.7.refs_1_
  19.7 0.1 pad_add_fusion.refs_0_
  19.8 1.2 %matrix_kernel.1 = (bf16[256,256]{1,0:T(8,128)(2,1)S(1)}, bf16[512,32]{1,0:T(8,128)(2,1)S(1)}, bf16[512,256]{1,0:T(8,128)(2,1)S(1)}, bf16[512,256]{1,0:T(8,128)(2,1)S(1)}) custom-call(s32[2]{0:T(128)S(1)} %pad_add_fusion.refs_0_, f32[36]{0:T(128)S(1)} %reshape.7.refs_1_), custom_call_target="tpu_custom_call" | custom-call | flops 2621440 | bytes 524288 | tf_op jit(solution)/shard_map/matrix_kernel/pallas_call | solution.py:171
  21.0 2.5 %collective-permute-start.13 = (bf16[64,1280]{1,0:T(8,128)(2,1)S(1)}, bf16[64,1280]{1,0:T(8,128)(2,1)S(1)}, u32[]{:S(2)}, u32[]{:S(2)}) collective-permute-start(bf16[64,1280]{1,0:T(8,128)(2,1)S(1)} %get-tuple-element.94), channel_id=1, source_target_pairs={{0,12},{2,14},{4,8},{6,10},{8,4},{10,6},{12,0},{14,2},{1,13},{3,15... | collective-permute-start | bytes 491528 | tf_op jit(solution)/shard_map/ppermute | solution.py:356
  23.4 2.2 %collective-permute-done.10.refs_6_ = bf16[64,1280]{1,0:T(8,128)(2,1)S(1)} collective-permute-done((bf16[64,1280]{1,0:T(8,128)(2,1)S(1)}, bf16[64,1280]{1,0:T(8,128)(2,1)S(1)}, u32[]{:S(2)}, u32[]{:S(2)}) %collective-permute-start.10) | collective-permute-done | bytes 163872 | tf_op jit(solution)/shard_map/ppermute | solution.py:356
  25.7 0.2 collective-permute-start.7
  25.8 0.6 collective-permute-start.4
  26.4 2.1 %collective-permute-done.12.refs_1_ = bf16[64,1280]{1,0:T(8,128)(2,1)S(1)} collective-permute-done((bf16[64,1280]{1,0:T(8,128)(2,1)S(1)}, bf16[64,1280]{1,0:T(8,128)(2,1)S(1)}, u32[]{:S(2)}, u32[]{:S(2)}) %collective-permute-start.12) | collective-permute-done | bytes 163872 | tf_op jit(solution)/shard_map/ppermute | solution.py:356
  28.5 0.9 %collective-permute-start.2 = (bf16[64,1024]{1,0:T(8,128)(2,1)S(1)}, bf16[64,1024]{1,0:T(8,128)(2,1)S(1)}, u32[]{:S(2)}, u32[]{:S(2)}) collective-permute-start(bf16[64,1024]{1,0:T(8,128)(2,1)S(1)} %collective-permute-done.1.refs_2_), channel_id=1, source_target_pairs={{0,2},{2,0},{4,6},{6,4},{8,10},{10,8},{12,14},{14,12},{1,3},{3,1},... | collective-permute-start | bytes 393224 | tf_op jit(solution)/shard_map/ppermute | solution.py:356
  29.4 1.1 %collective-permute-start.6 = (bf16[64,1024]{1,0:T(8,128)(2,1)S(1)}, bf16[64,1024]{1,0:T(8,128)(2,1)S(1)}, u32[]{:S(2)}, u32[]{:S(2)}) collective-permute-start(bf16[64,1024]{1,0:T(8,128)(2,1)S(1)} %collective-permute-done.5.refs_6_), channel_id=1, source_target_pairs={{0,2},{2,0},{4,6},{6,4},{8,10},{10,8},{12,14},{14,12},{1,3},{3,1},... | collective-permute-start | bytes 393224 | tf_op jit(solution)/shard_map/ppermute | solution.py:356
  30.5 2.7 %constant_dynamic-slice_fusion = (bf16[1024,1024]{1,0:T(8,128)(2,1)S(1)}, bf16[1024,1024]{1,0:T(8,128)(2,1)S(1)}) fusion(bf16[2048,1024]{1,0:T(8,128)(2,1)} %param.6, s32[]{:T(128)S(6)} %select_n.39, s32[]{:T(128)S(6)} %select_n.38), kind=kLoop, calls=%fused_computation.26 | loop fusion | bytes 8388616 | tf_op jit(solution)/shard_map/dynamic_slice | solution.py:388
  33.2 1.1 %collective-permute-done.13.refs_2_ = bf16[64,1280]{1,0:T(8,128)(2,1)S(1)} collective-permute-done((bf16[64,1280]{1,0:T(8,128)(2,1)S(1)}, bf16[64,1280]{1,0:T(8,128)(2,1)S(1)}, u32[]{:S(2)}, u32[]{:S(2)}) %collective-permute-start.13) | collective-permute-done | bytes 163872 | tf_op jit(solution)/shard_map/ppermute | solution.py:356
  34.3 7.2 %collective-permute-done.7.refs_3_ = bf16[64,1280]{1,0:T(8,128)(2,1)S(1)} collective-permute-done((bf16[64,1280]{1,0:T(8,128)(2,1)S(1)}, bf16[64,1280]{1,0:T(8,128)(2,1)S(1)}, u32[]{:S(2)}, u32[]{:S(2)}) %collective-permute-start.7) | collective-permute-done | bytes 163872 | tf_op jit(solution)/shard_map/ppermute | solution.py:356
  41.5 0.1 stack_kernel.1
  41.5 0.1 collective-permute-start.18
  41.6 0.7 %gather_kernel.1 = (bf16[640,1280]{1,0:T(8,128)(2,1)S(1)}, bf16[32,1024]{1,0:T(8,128)(2,1)S(1)}) custom-call(s32[2]{0:T(128)S(1)} %pad_add_fusion.refs_0_, bf16[64,1280]{1,0:T(8,128)(2,1)S(1)} %collective-permute-done.12.refs_1_, bf16[64,1280]{1,0:T(8,128)(2,1)S(1)} %collective-permute-done.13.refs_2_, bf16[64,1280]{1,0:T(8,128)(2,1)S(1)} %collective-permute-done.7.refs_3_, ...), custom_call_target="tpu_custom_call" | custom-call | flops 8192 | bytes 2621440 | tf_op jit(solution)/shard_map/gather_kernel/pallas_call | solution.py:209
  42.3 0.6 collective-permute-start.14
  42.9 1.5 %collective-permute-done.14.refs_2_ = bf16[32,1024]{1,0:T(8,128)(2,1)S(1)} collective-permute-done((bf16[32,1024]{1,0:T(8,128)(2,1)S(1)}, bf16[32,1024]{1,0:T(8,128)(2,1)S(1)}, u32[]{:S(2)}, u32[]{:S(2)}) %collective-permute-start.14) | collective-permute-done | bytes 65568 | tf_op jit(solution)/shard_map/ppermute | solution.py:359
  44.4 1.7 %corr_kernel.2 = (bf16[128,1024]{1,0:T(8,128)(2,1)S(1)}, bf16[128,1024]{1,0:T(8,128)(2,1)S(1)}, bf16[256,512]{1,0:T(8,128)(2,1)S(1)}, bf16[256,512]{1,0:T(8,128)(2,1)S(1)}) custom-call(s32[2]{0:T(128)S(1)} %pad_add_fusion.refs_0_, bf16[640,1280]{1,0:T(8,128)(2,1)S(1)} %get-tuple-element.56.refs_1_, bf16[32,1024]{1,0:T(8,128)(2,1)S(1)} %collective-permute-done.14.refs_2_, ...), custom_call_target="tpu_custom_call" | custom-call | flops 805306368 | bytes 2097152 | tf_op jit(solution)/shard_map/corr_kernel/pallas_call | solution.py:276
  46.1 0.6 collective-permute-start.15
  46.7 1.7 %corr_kernel.3 = (bf16[128,1024]{1,0:T(8,128)(2,1)S(1)}, bf16[128,1024]{1,0:T(8,128)(2,1)S(1)}, bf16[512,512]{1,0:T(8,128)(2,1)S(1)}, bf16[512,512]{1,0:T(8,128)(2,1)S(1)}) custom-call(s32[2]{0:T(128)S(1)} %pad_add_fusion.refs_0_, bf16[640,1280]{1,0:T(8,128)(2,1)S(1)} %get-tuple-element.56.refs_1_, bf16[32,1024]{1,0:T(8,128)(2,1)S(1)} %collective-permute-done.14.refs_2_, ...), custom_call_target="tpu_custom_call" | custom-call | flops 805306368 | bytes 2097152 | tf_op jit(solution)/shard_map/corr_kernel/pallas_call | solution.py:276
  48.4 1.6 %collective-permute-start.19 = (bf16[128,1024]{1,0:T(8,128)(2,1)S(1)}, bf16[128,1024]{1,0:T(8,128)(2,1)S(1)}, u32[]{:S(2)}, u32[]{:S(2)}) collective-permute-start(bf16[128,1024]{1,0:T(8,128)(2,1)S(1)} %get-tuple-element.81), channel_id=1, source_target_pairs={{0,2},{2,0},{4,6},{6,4},{8,10},{10,8},{12,14},{14,12},{1,3},{3,1},... | collective-permute-start | bytes 786440 | tf_op jit(solution)/shard_map/ppermute | solution.py:356
  50.0 0.5 fusion.3
  50.4 0.5 fusion.5
  50.9 4.4 %collective-permute-done.15.refs_1_ = bf16[128,1024]{1,0:T(8,128)(2,1)S(1)} collective-permute-done((bf16[128,1024]{1,0:T(8,128)(2,1)S(1)}, bf16[128,1024]{1,0:T(8,128)(2,1)S(1)}, u32[]{:S(2)}, u32[]{:S(2)}) %collective-permute-start.15) | collective-permute-done | bytes 262176 | tf_op jit(solution)/shard_map/ppermute | solution.py:356
  55.3 0.7 %partial_kernel.2 = (bf16[64,1024]{1,0:T(8,128)(2,1)S(1)}, bf16[64,1024]{1,0:T(8,128)(2,1)S(1)}) custom-call(bf16[128,1024]{1,0:T(8,128)(2,1)S(1)} %get-tuple-element.62.refs_0_, bf16[128,1024]{1,0:T(8,128)(2,1)S(1)} %collective-permute-done.15.refs_1_, bf16[1024,1024]{1,0:T(8,128)(2,1)S(1)} %get-tuple-element.64.refs_2_, ...), custom_call_target="tpu_custom_call" | custom-call | flops 536870912 | bytes 4194304 | tf_op jit(solution)/shard_map/partial_kernel/pallas_call | solution.py:307
  56.0 1.0 %collective-permute-start.16 = (bf16[64,1024]{1,0:T(8,128)(2,1)S(1)}, bf16[64,1024]{1,0:T(8,128)(2,1)S(1)}, u32[]{:S(2)}, u32[]{:S(2)}) collective-permute-start(bf16[64,1024]{1,0:T(8,128)(2,1)S(1)} %get-tuple-element.66), channel_id=1, source_target_pairs={{0,8},{2,10},{4,12},{6,14},{8,0},{10,2},{12,4},{14,6},{1,9},{3,11}... | collective-permute-start | bytes 393224 | tf_op jit(solution)/shard_map/ppermute | solution.py:356
  57.1 1.6 %collective-permute-start.20 = (bf16[64,1024]{1,0:T(8,128)(2,1)S(1)}, bf16[64,1024]{1,0:T(8,128)(2,1)S(1)}, u32[]{:S(2)}, u32[]{:S(2)}) collective-permute-start(bf16[64,1024]{1,0:T(8,128)(2,1)S(1)} %get-tuple-element.84), channel_id=1, source_target_pairs={{0,12},{2,14},{4,8},{6,10},{8,4},{10,6},{12,0},{14,2},{1,13},{3,15... | collective-permute-start | bytes 393224 | tf_op jit(solution)/shard_map/ppermute | solution.py:356
  58.7 1.4 %collective-permute-done.19.refs_1_ = bf16[128,1024]{1,0:T(8,128)(2,1)S(1)} collective-permute-done((bf16[128,1024]{1,0:T(8,128)(2,1)S(1)}, bf16[128,1024]{1,0:T(8,128)(2,1)S(1)}, u32[]{:S(2)}, u32[]{:S(2)}) %collective-permute-start.19) | collective-permute-done | bytes 262176 | tf_op jit(solution)/shard_map/ppermute | solution.py:356
  60.1 0.7 %partial_kernel.3 = (f32[64,1024]{1,0:T(8,128)S(1)}, bf16[64,1024]{1,0:T(8,128)(2,1)S(1)}) custom-call(bf16[128,1024]{1,0:T(8,128)(2,1)S(1)} %get-tuple-element.80.refs_0_, bf16[128,1024]{1,0:T(8,128)(2,1)S(1)} %collective-permute-done.19.refs_1_, bf16[1024,1024]{1,0:T(8,128)(2,1)S(1)} %get-tuple-element.64.refs_2_, ...), custom_call_target="tpu_custom_call" | custom-call | flops 536870912 | bytes 4194304 | tf_op jit(solution)/shard_map/partial_kernel/pallas_call | solution.py:307
  60.9 0.1 collective-permute-start.21
  61.0 0.5 fusion
  61.4 1.8 %add_multiply_fusion = f32[512,1024]{1,0:T(8,128)} fusion(f32[512,1024]{1,0:T(8,128)S(1)} %fusion, f32[512,1024]{1,0:T(8,128)S(1)} %fusion.5, f32[512,1024]{1,0:T(8,128)S(1)} %fusion.3, bf16[512,1024]{1,0:T(8,128)(2,1)S(1)} %collective-permute-done.18, bf16[512,512]{1,0:T(8,128)(2,1)S(1)} %collective-permute-done.17), kind=kOutput, calls=%fused_computation | convolution fusion | flops 270532608 | bytes 9175040 | tf_op jit(solution)/shard_map/dot_general | solution.py:410
  63.2 3.5 %collective-permute-done.16 = bf16[64,1024]{1,0:T(8,128)(2,1)S(1)} collective-permute-done((bf16[64,1024]{1,0:T(8,128)(2,1)S(1)}, bf16[64,1024]{1,0:T(8,128)(2,1)S(1)}, u32[]{:S(2)}, u32[]{:S(2)}) %collective-permute-start.16) | collective-permute-done | bytes 131104 | tf_op jit(solution)/shard_map/ppermute | solution.py:356
  66.8 2.4 %collective-permute-done.21 = bf16[64,1024]{1,0:T(8,128)(2,1)S(1)} collective-permute-done((bf16[64,1024]{1,0:T(8,128)(2,1)S(1)}, bf16[64,1024]{1,0:T(8,128)(2,1)S(1)}, u32[]{:S(2)}, u32[]{:S(2)}) %collective-permute-start.21) | collective-permute-done | bytes 131104 | tf_op jit(solution)/shard_map/ppermute | solution.py:356
  69.2 0.8 %multiply_bitcast_fusion = f32[1,64,1024]{2,1,0:T(8,128)} fusion(bf16[64,1024]{1,0:T(8,128)(2,1)S(1)} %collective-permute-done.21, bf16[64,1024]{1,0:T(8,128)(2,1)S(1)} %collective-permute-done.20, f32[64,1024]{1,0:T(8,128)S(1)} %get-tuple-element.82, bf16[64,1024]{1,0:T(8,128)(2,1)S(1)} %collective-permute-done.16), kind=kLoop, calls=%fused_computation.18 | loop fusion | flops 458752 | bytes 917504 | tf_op jit(solution)/shard_map/broadcast_in_dim | solution.py:422
  (20 shorter events, 0.1 us)
Async XLA Ops:
  0.6 9.3 %copy-start.1 = (f32[3,3]{1,0:T(4,128)S(1)}, f32[3,3]{1,0:T(4,128)}, u32[]{:S(2)}) copy-start(f32[3,3]{1,0:T(4,128)} %param.9) | copy-start | bytes 112
  0.6 9.3 %copy-start.2 = (f32[3,3]{1,0:T(4,128)S(1)}, f32[3,3]{1,0:T(4,128)}, u32[]{:S(2)}) copy-start(f32[3,3]{1,0:T(4,128)} %param.8) | copy-start | bytes 112
  0.6 10.7 %collective-permute-start.3 = (bf16[64,1024]{1,0:T(8,128)(2,1)}, bf16[64,1024]{1,0:T(8,128)(2,1)S(1)}, u32[]{:S(2)}, u32[]{:S(2)}) collective-permute-start(bf16[64,1024]{1,0:T(8,128)(2,1)} %bitcast.14), channel_id=1, source_target_pairs={{0,8},{2,10},{4,12},{6,14},{8,0},{10,2},{12,4},{14,6},{1,9},{3,11}... | collective-permute-start | bytes 393224 | tf_op jit(solution)/shard_map/ppermute | solution.py:356
  4.8 8.3 %collective-permute-start.1 = (bf16[64,1024]{1,0:T(8,128)(2,1)}, bf16[64,1024]{1,0:T(8,128)(2,1)S(1)}, u32[]{:S(2)}, u32[]{:S(2)}) collective-permute-start(bf16[64,1024]{1,0:T(8,128)(2,1)} %bitcast.15), channel_id=1, source_target_pairs={{0,4},{2,6},{4,0},{6,2},{8,12},{10,14},{12,8},{14,10},{1,5},{3,7},... | collective-permute-start | bytes 393224 | tf_op jit(solution)/shard_map/ppermute | solution.py:356
  6.3 8.3 %collective-permute-start = (bf16[64,1024]{1,0:T(8,128)(2,1)}, bf16[64,1024]{1,0:T(8,128)(2,1)S(1)}, u32[]{:S(2)}, u32[]{:S(2)}) collective-permute-start(bf16[64,1024]{1,0:T(8,128)(2,1)} %bitcast.16), channel_id=1, source_target_pairs={{0,2},{2,0},{4,6},{6,4},{8,10},{10,8},{12,14},{14,12},{1,3},{3,1},... | collective-permute-start | bytes 393224 | tf_op jit(solution)/shard_map/ppermute | solution.py:356
  9.3 10.2 %collective-permute-start.8 = (bf16[64,1280]{1,0:T(8,128)(2,1)S(1)}, bf16[64,1280]{1,0:T(8,128)(2,1)S(1)}, u32[]{:S(2)}, u32[]{:S(2)}) collective-permute-start(bf16[64,1280]{1,0:T(8,128)(2,1)S(1)} %get-tuple-element.89), channel_id=1, source_target_pairs={{0,8},{2,10},{4,12},{6,14},{8,0},{10,2},{12,4},{14,6},{1,9},{3,11}... | collective-permute-start | bytes 491528 | tf_op jit(solution)/shard_map/ppermute | solution.py:356
  9.7 11.2 %collective-permute-start.9 = (bf16[64,1280]{1,0:T(8,128)(2,1)S(1)}, bf16[64,1280]{1,0:T(8,128)(2,1)S(1)}, u32[]{:S(2)}, u32[]{:S(2)}) collective-permute-start(bf16[64,1280]{1,0:T(8,128)(2,1)S(1)} %get-tuple-element.90), channel_id=1, source_target_pairs={{0,6},{2,4},{4,2},{6,0},{8,14},{10,12},{12,10},{14,8},{1,7},{3,5},... | collective-permute-start | bytes 491528 | tf_op jit(solution)/shard_map/ppermute | solution.py:356
  11.4 14.3 %collective-permute-start.10 = (bf16[64,1280]{1,0:T(8,128)(2,1)S(1)}, bf16[64,1280]{1,0:T(8,128)(2,1)S(1)}, u32[]{:S(2)}, u32[]{:S(2)}) collective-permute-start(bf16[64,1280]{1,0:T(8,128)(2,1)S(1)} %get-tuple-element.91), channel_id=1, source_target_pairs={{0,4},{2,6},{4,0},{6,2},{8,12},{10,14},{12,8},{14,10},{1,5},{3,7},... | collective-permute-start | bytes 491528 | tf_op jit(solution)/shard_map/ppermute | solution.py:356
  13.1 12.7 %collective-permute-start.11 = (bf16[64,1280]{1,0:T(8,128)(2,1)S(1)}, bf16[64,1280]{1,0:T(8,128)(2,1)S(1)}, u32[]{:S(2)}, u32[]{:S(2)}) collective-permute-start(bf16[64,1280]{1,0:T(8,128)(2,1)S(1)} %get-tuple-element.92), channel_id=1, source_target_pairs={{0,2},{2,0},{4,6},{6,4},{8,10},{10,8},{12,14},{14,12},{1,3},{3,1},... | collective-permute-start | bytes 491528 | tf_op jit(solution)/shard_map/ppermute | solution.py:356
  14.6 13.9 %collective-permute-start.12 = (bf16[64,1280]{1,0:T(8,128)(2,1)S(1)}, bf16[64,1280]{1,0:T(8,128)(2,1)S(1)}, u32[]{:S(2)}, u32[]{:S(2)}) collective-permute-start(bf16[64,1280]{1,0:T(8,128)(2,1)S(1)} %get-tuple-element.93), channel_id=1, source_target_pairs={{0,14},{2,12},{4,10},{6,8},{8,6},{10,4},{12,2},{14,0},{1,15},{3,13... | collective-permute-start | bytes 491528 | tf_op jit(solution)/shard_map/ppermute | solution.py:356
  19.6 9.8 %collective-permute-start.5 = (bf16[64,1024]{1,0:T(8,128)(2,1)S(1)}, bf16[64,1024]{1,0:T(8,128)(2,1)S(1)}, u32[]{:S(2)}, u32[]{:S(2)}) collective-permute-start(bf16[64,1024]{1,0:T(8,128)(2,1)S(1)} %collective-permute-done.3.refs_4_), channel_id=1, source_target_pairs={{0,4},{2,6},{4,0},{6,2},{8,12},{10,14},{12,8},{14,10},{1,5},{3,7},... | collective-permute-start | bytes 393224 | tf_op jit(solution)/shard_map/ppermute | solution.py:356
  21.0 13.3 %collective-permute-start.13 = (bf16[64,1280]{1,0:T(8,128)(2,1)S(1)}, bf16[64,1280]{1,0:T(8,128)(2,1)S(1)}, u32[]{:S(2)}, u32[]{:S(2)}) collective-permute-start(bf16[64,1280]{1,0:T(8,128)(2,1)S(1)} %get-tuple-element.94), channel_id=1, source_target_pairs={{0,12},{2,14},{4,8},{6,10},{8,4},{10,6},{12,0},{14,2},{1,13},{3,15... | collective-permute-start | bytes 491528 | tf_op jit(solution)/shard_map/ppermute | solution.py:356
  25.7 15.8 %copy-start = (bf16[1,64,1024]{2,1,0:T(8,128)(2,1)S(1)}, bf16[1,64,1024]{2,1,0:T(8,128)(2,1)}, u32[]{:S(2)}) copy-start(bf16[1,64,1024]{2,1,0:T(8,128)(2,1)} %param.7) | copy-start | bytes 393220
  25.7 15.8 %collective-permute-start.7 = (bf16[64,1280]{1,0:T(8,128)(2,1)S(1)}, bf16[64,1280]{1,0:T(8,128)(2,1)S(1)}, u32[]{:S(2)}, u32[]{:S(2)}) collective-permute-start(bf16[64,1280]{1,0:T(8,128)(2,1)S(1)} %get-tuple-element.95), channel_id=1, source_target_pairs={{0,10},{2,8},{4,14},{6,12},{8,2},{10,0},{12,6},{14,4},{1,11},{3,9}... | collective-permute-start | bytes 491528 | tf_op jit(solution)/shard_map/ppermute | solution.py:356
  25.8 15.6 %collective-permute-start.4 = (bf16[64,1024]{1,0:T(8,128)(2,1)S(1)}, bf16[64,1024]{1,0:T(8,128)(2,1)S(1)}, u32[]{:S(2)}, u32[]{:S(2)}) collective-permute-start(bf16[64,1024]{1,0:T(8,128)(2,1)S(1)} %collective-permute-done.3.refs_4_), channel_id=1, source_target_pairs={{0,2},{2,0},{4,6},{6,4},{8,10},{10,8},{12,14},{14,12},{1,3},{3,1},... | collective-permute-start | bytes 393224 | tf_op jit(solution)/shard_map/ppermute | solution.py:356
  28.5 12.9 %collective-permute-start.2 = (bf16[64,1024]{1,0:T(8,128)(2,1)S(1)}, bf16[64,1024]{1,0:T(8,128)(2,1)S(1)}, u32[]{:S(2)}, u32[]{:S(2)}) collective-permute-start(bf16[64,1024]{1,0:T(8,128)(2,1)S(1)} %collective-permute-done.1.refs_2_), channel_id=1, source_target_pairs={{0,2},{2,0},{4,6},{6,4},{8,10},{10,8},{12,14},{14,12},{1,3},{3,1},... | collective-permute-start | bytes 393224 | tf_op jit(solution)/shard_map/ppermute | solution.py:356
  29.4 12.1 %collective-permute-start.6 = (bf16[64,1024]{1,0:T(8,128)(2,1)S(1)}, bf16[64,1024]{1,0:T(8,128)(2,1)S(1)}, u32[]{:S(2)}, u32[]{:S(2)}) collective-permute-start(bf16[64,1024]{1,0:T(8,128)(2,1)S(1)} %collective-permute-done.5.refs_6_), channel_id=1, source_target_pairs={{0,2},{2,0},{4,6},{6,4},{8,10},{10,8},{12,14},{14,12},{1,3},{3,1},... | collective-permute-start | bytes 393224 | tf_op jit(solution)/shard_map/ppermute | solution.py:356
  41.5 19.4 %collective-permute-start.18 = (bf16[512,1024]{1,0:T(8,128)(2,1)S(1)}, bf16[512,1024]{1,0:T(8,128)(2,1)S(1)}, u32[]{:S(2)}, u32[]{:S(2)}) collective-permute-start(bf16[512,1024]{1,0:T(8,128)(2,1)S(1)} %stack_kernel.1), channel_id=1, source_target_pairs={{0,1},{1,0},{2,3},{3,2},{4,5},{5,4},{6,7},{7,6},{8,9},{9,8},{10,11... | collective-permute-start | bytes 3145736 | tf_op jit(solution)/shard_map/ppermute | solution.py:359
  42.3 2.0 %collective-permute-start.14 = (bf16[32,1024]{1,0:T(8,128)(2,1)S(1)}, bf16[32,1024]{1,0:T(8,128)(2,1)S(1)}, u32[]{:S(2)}, u32[]{:S(2)}) collective-permute-start(bf16[32,1024]{1,0:T(8,128)(2,1)S(1)} %get-tuple-element.57), channel_id=1, source_target_pairs={{0,1},{1,0},{2,3},{3,2},{4,5},{5,4},{6,7},{7,6},{8,9},{9,8},{10,11... | collective-permute-start | bytes 196616 | tf_op jit(solution)/shard_map/ppermute | solution.py:359
  46.1 9.2 %collective-permute-start.15 = (bf16[128,1024]{1,0:T(8,128)(2,1)S(1)}, bf16[128,1024]{1,0:T(8,128)(2,1)S(1)}, u32[]{:S(2)}, u32[]{:S(2)}) collective-permute-start(bf16[128,1024]{1,0:T(8,128)(2,1)S(1)} %get-tuple-element.63), channel_id=1, source_target_pairs={{0,2},{2,0},{4,6},{6,4},{8,10},{10,8},{12,14},{14,12},{1,3},{3,1},... | collective-permute-start | bytes 786440 | tf_op jit(solution)/shard_map/ppermute | solution.py:356
  48.4 11.7 %collective-permute-start.19 = (bf16[128,1024]{1,0:T(8,128)(2,1)S(1)}, bf16[128,1024]{1,0:T(8,128)(2,1)S(1)}, u32[]{:S(2)}, u32[]{:S(2)}) collective-permute-start(bf16[128,1024]{1,0:T(8,128)(2,1)S(1)} %get-tuple-element.81), channel_id=1, source_target_pairs={{0,2},{2,0},{4,6},{6,4},{8,10},{10,8},{12,14},{14,12},{1,3},{3,1},... | collective-permute-start | bytes 786440 | tf_op jit(solution)/shard_map/ppermute | solution.py:356
  50.0 11.0 %collective-permute-start.17 = (bf16[512,512]{1,0:T(8,128)(2,1)S(1)}, bf16[512,512]{1,0:T(8,128)(2,1)S(1)}, u32[]{:S(2)}, u32[]{:S(2)}) collective-permute-start(bf16[512,512]{1,0:T(8,128)(2,1)S(1)} %get-tuple-element.78), channel_id=1, source_target_pairs={{0,1},{1,0},{2,3},{3,2},{4,5},{5,4},{6,7},{7,6},{8,9},{9,8},{10,11... | collective-permute-start | bytes 1572872 | tf_op jit(solution)/shard_map/ppermute | solution.py:359
  56.0 10.7 %collective-permute-start.16 = (bf16[64,1024]{1,0:T(8,128)(2,1)S(1)}, bf16[64,1024]{1,0:T(8,128)(2,1)S(1)}, u32[]{:S(2)}, u32[]{:S(2)}) collective-permute-start(bf16[64,1024]{1,0:T(8,128)(2,1)S(1)} %get-tuple-element.66), channel_id=1, source_target_pairs={{0,8},{2,10},{4,12},{6,14},{8,0},{10,2},{12,4},{14,6},{1,9},{3,11}... | collective-permute-start | bytes 393224 | tf_op jit(solution)/shard_map/ppermute | solution.py:356
  57.1 9.7 %collective-permute-start.20 = (bf16[64,1024]{1,0:T(8,128)(2,1)S(1)}, bf16[64,1024]{1,0:T(8,128)(2,1)S(1)}, u32[]{:S(2)}, u32[]{:S(2)}) collective-permute-start(bf16[64,1024]{1,0:T(8,128)(2,1)S(1)} %get-tuple-element.84), channel_id=1, source_target_pairs={{0,12},{2,14},{4,8},{6,10},{8,4},{10,6},{12,0},{14,2},{1,13},{3,15... | collective-permute-start | bytes 393224 | tf_op jit(solution)/shard_map/ppermute | solution.py:356
  60.9 8.3 %collective-permute-start.21 = (bf16[64,1024]{1,0:T(8,128)(2,1)S(1)}, bf16[64,1024]{1,0:T(8,128)(2,1)S(1)}, u32[]{:S(2)}, u32[]{:S(2)}) collective-permute-start(bf16[64,1024]{1,0:T(8,128)(2,1)S(1)} %get-tuple-element.85), channel_id=1, source_target_pairs={{0,4},{2,6},{4,0},{6,2},{8,12},{10,14},{12,8},{14,10},{1,5},{3,7},... | collective-permute-start | bytes 393224 | tf_op jit(solution)/shard_map/ppermute | solution.py:356

commit v5 on v4

--- a/solution.py
+++ b/solution.py
@@ -227,8 +227,32 @@
     return jnp.dot(left, right, preferred_element_type=jnp.float32)
 
 
+def query_kernel(columns, tile, cells_ref, wh_ref, wl_ref, out_ref):
+    rows = out_ref.shape[0]
+    step = 2 * QW
+    for low in range(0, tile, step):
+        window = cells_ref[columns : columns + rows, low : low + 2 * step]
+        total = product(window, wh_ref[...]) + product(window, wl_ref[...])
+        out_ref[:, low : low + step] = total
+
+
+def query_call(cells, high, low, columns, tile):
+    rows = cells.shape[0] - 2 * columns
+    return pl.pallas_call(
+        lambda *refs: query_kernel(columns, tile, *refs),
+        out_shape=jax.ShapeDtypeStruct((rows, tile), jnp.float32),
+        in_specs=[pl.BlockSpec(memory_space=pltpu.VMEM)] * 3,
+        out_specs=pl.BlockSpec(memory_space=pltpu.VMEM),
+        compiler_params=pltpu.CompilerParams(vmem_limit_bytes=6 << 20),
+        cost_estimate=pl.CostEstimate(
+            flops=16 * rows * tile * QW, bytes_accessed=8 * rows * tile, transcendentals=0
+        ),
+        name="query_kernel",
+    )(cells, high, low)
+
+
 def corr_kernel(group, columns, tile, *refs):
-    place_ref, cells_ref, rim_ref, t_ref, edge_ref, wh_ref, wl_ref = refs[:7]
+    place_ref, cells_ref, rim_ref, t_ref, edge_ref, query_ref = refs[:6]
     corr_ref = refs[-1]
     move_ref, stay_ref, keep_ref, send_ref = refs[-5:-1]
     half = corr_ref.shape[0] // columns
@@ -243,8 +267,7 @@
 
     step = 2 * QW
     for low in range(0, tile, step):
-        window = cells_ref[plane_rows(base + 1, rows), low : low + 2 * step]
-        total = product(window, wh_ref[...]) + product(window, wl_ref[...])
+        total = query_ref[plane_rows(base, rows), low : low + step]
         edges = edge_ref[plane_rows(base, rows), :]
         total += product(edges, rim_ref[:, low : low + step])
         for at in range(0, half, 2):
@@ -261,7 +284,7 @@
         for half_ref, which in ((keep_ref, core), (send_ref, 1 - core)):
             start = pl.multiple_of(which * width, width)
             half_ref[k * columns : (k + 1) * columns, :] = corr_ref[source, pl.ds(start, width)]
-    for earlier_ref, half_ref in zip(refs[7:-5], (keep_ref, send_ref)):
+    for earlier_ref, half_ref in zip(refs[6:-5], (keep_ref, send_ref)):
         half_ref[rows:, :] = earlier_ref[...]
 
 
@@ -276,12 +299,12 @@
     return pl.pallas_call(
         lambda *refs: corr_kernel(group, columns, tile, *refs),
         out_shape=[wide, wide, tall, tall],
-        in_specs=[pl.BlockSpec(memory_space=pltpu.SMEM)] + [vmem] * (6 + len(earlier)),
+        in_specs=[pl.BlockSpec(memory_space=pltpu.SMEM)] + [vmem] * (5 + len(earlier)),
         out_specs=[vmem] * 4,
         scratch_shapes=[pltpu.VMEM((rows, tile), jnp.bfloat16)],
         compiler_params=pltpu.CompilerParams(vmem_limit_bytes=6 << 20),
         cost_estimate=pl.CostEstimate(
-            flops=2 * rows * tile * (8 * columns + 8 * QW),
+            flops=2 * rows * tile * 8 * columns,
             bytes_accessed=8 * rows * tile,
             transcendentals=0,
         ),
@@ -386,13 +409,14 @@
     mats = matrix_call(place, query_kernel, support_kernel, count, columns, edge)
     here = lax.dynamic_slice(query_feats, (side * tile, 0), (tile, width))
     there = lax.dynamic_slice(query_feats, ((side ^ 1) * tile, 0), (tile, width))
-    ordered = held + [pieces[k] for k in [5, 4, 3, 2, 1, 7, 6, 0]]
+    ordered = held + [pieces[k] for k in [7, 6, 5, 4, 3, 2, 1, 0]]
     ordered, mats, here, there = lax.optimization_barrier((ordered, mats, here, there))
     held, landed = ordered[:count], ordered[count:]
-    for at, k in enumerate([5, 4, 3, 2, 1, 7, 6, 0]):
+    for at, k in enumerate([7, 6, 5, 4, 3, 2, 1, 0]):
         pieces[k] = landed[at]
     cells, rim = gather_call(place, pieces, tile, edge)
     rim = swapped(rim)
+    mats = [mats[0], mats[1], query_call(cells, mats[2], mats[3], columns, tile)]
     feats = stack_call(held)
     across = swapped(feats)
     move1, stay1, keep, send = corr_call(1, place, cells, rim, mats, count)
@@ -415,7 +439,7 @@
     query_grad = query_term(keep[:rows], feats[:rows]) + query_term(keep[rows:], feats[rows:])
     query_grad += query_term(other[:rows], across[:rows]) + query_term(other[rows:], across[rows:])
     query_grad *= scale_factor
-    landed[0], query_grad = lax.optimization_barrier((landed[0], query_grad))
+    landed[-1], query_grad = lax.optimization_barrier((landed[-1], query_grad))
     support_grad = parts0[0]
     for term in landed:
         support_grad = support_grad + term.astype(jnp.float32)

time: 70.1 us -> 69.6 us (level)
  waiting for transfers between devices: 29.3 us -> 28.5 us
    ppermute x3, waiting for transfers between devices: 1.47 us -> 0.21 us  [swapped(): return lax.ppermute(value, 'pair', [(0, 1), (1, 0)])]
    pallas_call x0 -> x1, Pallas kernels: none -> 1.25 us  [query_call(): pl.pallas_call(lambda *refs: query_kernel(columns, tile, *refs), out_shap...]
    pallas_call x2, Pallas kernels: 3.44 us -> 2.37 us  [corr_call(): pl.pallas_call(lambda *refs: corr_kernel(group, columns, tile, *refs), ou...]
  transfers between devices with their start and end apart: 22 -> 22, of which waited for: 11 -> 10; matrix products, arithmetic and copies ran while one was open for 11% -> 11% of each run, Pallas kernels for 10% -> 10%
where the time goes in v5:
time: 69.6 us; the launch traced here: 69.4 us
  waiting for transfers between devices  28.5 us (41%)
  starting transfers between devices  24.7 us (35%)
  Pallas kernels  7.05 us (10%)
  local copies, waits for them, and re-layouts  4.28 us (6%)
  matrix products  3.19 us (5%)
  other arithmetic  0.86 us (1%)
  between operations  0.82 us (1%)
    ppermute x19, waiting for transfers between devices, exchanged(): lax.ppermute(value, ('blk', 'sub'), [(i, i ^ mask) for i in range(count)])  28.3 us
    ppermute x19, starting transfers between devices, exchanged(): lax.ppermute(value, ('blk', 'sub'), [(i, i ^ mask) for i in range(count)])  24 us
    dot_general x4, matrix products, query_term(): lax.dot_general(block, feats, (((0,), (0,)), ((), ())), preferred_element...  3.19 us
    dynamic_slice x1, local copies, waits for them, and re-layouts, tile_shards(): lax.dynamic_slice(query_feats, ((side ^ 1) * tile, 0), (tile, width))  2.66 us
    pallas_call x2, Pallas kernels, corr_call(): pl.pallas_call(lambda *refs: corr_kernel(group, columns, tile, *refs), ou...  2.37 us
    dynamic_slice x1, local copies, waits for them, and re-layouts, piece(): lax.dynamic_slice(volume, (0, (own ^ mask) * tile), (columns, tile + 2 *...  1.52 us
    pallas_call x2, Pallas kernels, partial_call(): pl.pallas_call(lambda *refs: partial_kernel(columns, *refs), out_shape=[j...  1.46 us
  transfers between devices with their start and end apart: 22, of which 10 were waited for; matrix products, arithmetic and copies ran while one was open for 11% of the time, Pallas kernels for 10%

profile of v5, /device:TPU:0, one launch (start us, length us, event | category | flops | bytes accessed | tf_op | source)
XLA Modules:
  0.0 69.4 jit_solution(13192260639264610895)
XLA Ops:
  0.6 4.1 %collective-permute-start.3 = (bf16[64,1024]{1,0:T(8,128)(2,1)}, bf16[64,1024]{1,0:T(8,128)(2,1)S(1)}, u32[]{:S(2)}, u32[]{:S(2)}) collective-permute-start(bf16[64,1024]{1,0:T(8,128)(2,1)} %bitcast.14), channel_id=1, source_target_pairs={{0,8},{2,10},{4,12},{6,14},{8,0},{10,2},{12,4},{14,6},{1,9},{3,11}... | collective-permute-start | bytes 393224 | tf_op jit(solution)/shard_map/ppermute | solution.py:379
  4.8 1.6 %collective-permute-start.1 = (bf16[64,1024]{1,0:T(8,128)(2,1)}, bf16[64,1024]{1,0:T(8,128)(2,1)S(1)}, u32[]{:S(2)}, u32[]{:S(2)}) collective-permute-start(bf16[64,1024]{1,0:T(8,128)(2,1)} %bitcast.15), channel_id=1, source_target_pairs={{0,4},{2,6},{4,0},{6,2},{8,12},{10,14},{12,8},{14,10},{1,5},{3,7},... | collective-permute-start | bytes 393224 | tf_op jit(solution)/shard_map/ppermute | solution.py:379
  6.3 1.5 %collective-permute-start = (bf16[64,1024]{1,0:T(8,128)(2,1)}, bf16[64,1024]{1,0:T(8,128)(2,1)S(1)}, u32[]{:S(2)}, u32[]{:S(2)}) collective-permute-start(bf16[64,1024]{1,0:T(8,128)(2,1)} %bitcast.16), channel_id=1, source_target_pairs={{0,2},{2,0},{4,6},{6,4},{8,10},{10,8},{12,14},{14,12},{1,3},{3,1},... | collective-permute-start | bytes 393224 | tf_op jit(solution)/shard_map/ppermute | solution.py:379
  7.8 1.5 %pad_dynamic-slice_fusion = (bf16[64,1280]{1,0:T(8,128)(2,1)S(1)}, bf16[64,1280]{1,0:T(8,128)(2,1)S(1)}, bf16[64,1280]{1,0:T(8,128)(2,1)S(1)}, bf16[64,1280]{1,0...) fusion(s32[]{:T(128)S(6)} %select_n.37, ...), kind=kLoop, calls=%fused_computation.8 | loop fusion | bytes 2359328 | tf_op jit(solution)/shard_map/dynamic_slice | solution.py:387
  9.3 0.4 collective-permute-start.10
  9.7 0.2 collective-permute-start.11
  9.9 1.4 %collective-permute-done.3.refs_4_ = bf16[64,1024]{1,0:T(8,128)(2,1)S(1)} collective-permute-done((bf16[64,1024]{1,0:T(8,128)(2,1)}, bf16[64,1024]{1,0:T(8,128)(2,1)S(1)}, u32[]{:S(2)}, u32[]{:S(2)}) %collective-permute-start.3) | collective-permute-done | bytes 131104 | tf_op jit(solution)/shard_map/ppermute | solution.py:379
  11.4 1.7 %collective-permute-start.12 = (bf16[64,1280]{1,0:T(8,128)(2,1)S(1)}, bf16[64,1280]{1,0:T(8,128)(2,1)S(1)}, u32[]{:S(2)}, u32[]{:S(2)}) collective-permute-start(bf16[64,1280]{1,0:T(8,128)(2,1)S(1)} %get-tuple-element.93), channel_id=1, source_target_pairs={{0,4},{2,6},{4,0},{6,2},{8,12},{10,14},{12,8},{14,10},{1,5},{3,7},... | collective-permute-start | bytes 491528 | tf_op jit(solution)/shard_map/ppermute | solution.py:379
  13.1 1.5 %collective-permute-start.13 = (bf16[64,1280]{1,0:T(8,128)(2,1)S(1)}, bf16[64,1280]{1,0:T(8,128)(2,1)S(1)}, u32[]{:S(2)}, u32[]{:S(2)}) collective-permute-start(bf16[64,1280]{1,0:T(8,128)(2,1)S(1)} %get-tuple-element.94), channel_id=1, source_target_pairs={{0,2},{2,0},{4,6},{6,4},{8,10},{10,8},{12,14},{14,12},{1,3},{3,1},... | collective-permute-start | bytes 491528 | tf_op jit(solution)/shard_map/ppermute | solution.py:379
  14.6 2.9 %collective-permute-start.7 = (bf16[64,1280]{1,0:T(8,128)(2,1)S(1)}, bf16[64,1280]{1,0:T(8,128)(2,1)S(1)}, u32[]{:S(2)}, u32[]{:S(2)}) collective-permute-start(bf16[64,1280]{1,0:T(8,128)(2,1)S(1)} %get-tuple-element.95), channel_id=1, source_target_pairs={{0,14},{2,12},{4,10},{6,8},{8,6},{10,4},{12,2},{14,0},{1,15},{3,13... | collective-permute-start | bytes 491528 | tf_op jit(solution)/shard_map/ppermute | solution.py:379
  17.5 2.0 %collective-permute-done.10.refs_4_ = bf16[64,1280]{1,0:T(8,128)(2,1)S(1)} collective-permute-done((bf16[64,1280]{1,0:T(8,128)(2,1)S(1)}, bf16[64,1280]{1,0:T(8,128)(2,1)S(1)}, u32[]{:S(2)}, u32[]{:S(2)}) %collective-permute-start.10) | collective-permute-done | bytes 163872 | tf_op jit(solution)/shard_map/ppermute | solution.py:379
  19.6 0.1 reshape.7.refs_1_
  19.7 0.1 pad_add_fusion.refs_0_
  19.8 1.2 %matrix_kernel.1 = (bf16[256,256]{1,0:T(8,128)(2,1)S(1)}, bf16[512,32]{1,0:T(8,128)(2,1)S(1)}, bf16[512,256]{1,0:T(8,128)(2,1)S(1)}, bf16[512,256]{1,0:T(8,128)(2,1)S(1)}) custom-call(s32[2]{0:T(128)S(1)} %pad_add_fusion.refs_0_, f32[36]{0:T(128)S(1)} %reshape.7.refs_1_), custom_call_target="tpu_custom_call" | custom-call | flops 2621440 | bytes 524288 | tf_op jit(solution)/shard_map/matrix_kernel/pallas_call | solution.py:171
  21.0 2.5 %collective-permute-start.8 = (bf16[64,1280]{1,0:T(8,128)(2,1)S(1)}, bf16[64,1280]{1,0:T(8,128)(2,1)S(1)}, u32[]{:S(2)}, u32[]{:S(2)}) collective-permute-start(bf16[64,1280]{1,0:T(8,128)(2,1)S(1)} %get-tuple-element.89), channel_id=1, source_target_pairs={{0,12},{2,14},{4,8},{6,10},{8,4},{10,6},{12,0},{14,2},{1,13},{3,15... | collective-permute-start | bytes 491528 | tf_op jit(solution)/shard_map/ppermute | solution.py:379
  23.4 2.2 %collective-permute-done.12.refs_6_ = bf16[64,1280]{1,0:T(8,128)(2,1)S(1)} collective-permute-done((bf16[64,1280]{1,0:T(8,128)(2,1)S(1)}, bf16[64,1280]{1,0:T(8,128)(2,1)S(1)}, u32[]{:S(2)}, u32[]{:S(2)}) %collective-permute-start.12) | collective-permute-done | bytes 163872 | tf_op jit(solution)/shard_map/ppermute | solution.py:379
  25.7 0.2 collective-permute-start.9
  25.8 0.6 collective-permute-start.4
  26.4 2.1 %collective-permute-done.7.refs_1_ = bf16[64,1280]{1,0:T(8,128)(2,1)S(1)} collective-permute-done((bf16[64,1280]{1,0:T(8,128)(2,1)S(1)}, bf16[64,1280]{1,0:T(8,128)(2,1)S(1)}, u32[]{:S(2)}, u32[]{:S(2)}) %collective-permute-start.7) | collective-permute-done | bytes 163872 | tf_op jit(solution)/shard_map/ppermute | solution.py:379
  28.5 0.9 %collective-permute-start.2 = (bf16[64,1024]{1,0:T(8,128)(2,1)S(1)}, bf16[64,1024]{1,0:T(8,128)(2,1)S(1)}, u32[]{:S(2)}, u32[]{:S(2)}) collective-permute-start(bf16[64,1024]{1,0:T(8,128)(2,1)S(1)} %collective-permute-done.1.refs_2_), channel_id=1, source_target_pairs={{0,2},{2,0},{4,6},{6,4},{8,10},{10,8},{12,14},{14,12},{1,3},{3,1},... | collective-permute-start | bytes 393224 | tf_op jit(solution)/shard_map/ppermute | solution.py:379
  29.4 1.1 %collective-permute-start.6 = (bf16[64,1024]{1,0:T(8,128)(2,1)S(1)}, bf16[64,1024]{1,0:T(8,128)(2,1)S(1)}, u32[]{:S(2)}, u32[]{:S(2)}) collective-permute-start(bf16[64,1024]{1,0:T(8,128)(2,1)S(1)} %collective-permute-done.5.refs_6_), channel_id=1, source_target_pairs={{0,2},{2,0},{4,6},{6,4},{8,10},{10,8},{12,14},{14,12},{1,3},{3,1},... | collective-permute-start | bytes 393224 | tf_op jit(solution)/shard_map/ppermute | solution.py:379
  30.5 2.7 %constant_dynamic-slice_fusion = (bf16[1024,1024]{1,0:T(8,128)(2,1)S(1)}, bf16[1024,1024]{1,0:T(8,128)(2,1)S(1)}) fusion(bf16[2048,1024]{1,0:T(8,128)(2,1)} %param.6, s32[]{:T(128)S(6)} %select_n.39, s32[]{:T(128)S(6)} %select_n.38), kind=kLoop, calls=%fused_computation.26 | loop fusion | bytes 8388616 | tf_op jit(solution)/shard_map/dynamic_slice | solution.py:411
  33.2 1.1 %collective-permute-done.8.refs_2_ = bf16[64,1280]{1,0:T(8,128)(2,1)S(1)} collective-permute-done((bf16[64,1280]{1,0:T(8,128)(2,1)S(1)}, bf16[64,1280]{1,0:T(8,128)(2,1)S(1)}, u32[]{:S(2)}, u32[]{:S(2)}) %collective-permute-start.8) | collective-permute-done | bytes 163872 | tf_op jit(solution)/shard_map/ppermute | solution.py:379
  34.3 7.2 %collective-permute-done.9.refs_3_ = bf16[64,1280]{1,0:T(8,128)(2,1)S(1)} collective-permute-done((bf16[64,1280]{1,0:T(8,128)(2,1)S(1)}, bf16[64,1280]{1,0:T(8,128)(2,1)S(1)}, u32[]{:S(2)}, u32[]{:S(2)}) %collective-permute-start.9) | collective-permute-done | bytes 163872 | tf_op jit(solution)/shard_map/ppermute | solution.py:379
  41.5 0.1 stack_kernel.1
  41.5 0.1 collective-permute-start.18
  41.6 0.7 %gather_kernel.1 = (bf16[640,1280]{1,0:T(8,128)(2,1)S(1)}, bf16[32,1024]{1,0:T(8,128)(2,1)S(1)}) custom-call(s32[2]{0:T(128)S(1)} %pad_add_fusion.refs_0_, bf16[64,1280]{1,0:T(8,128)(2,1)S(1)} %collective-permute-done.7.refs_1_, bf16[64,1280]{1,0:T(8,128)(2,1)S(1)} %collective-permute-done.8.refs_2_, bf16[64,1280]{1,0:T(8,128)(2,1)S(1)} %collective-permute-done.9.refs_3_, ...), custom_call_target="tpu_custom_call" | custom-call | flops 8192 | bytes 2621440 | tf_op jit(solution)/shard_map/gather_kernel/pallas_call | solution.py:209
  42.3 0.6 collective-permute-start.14
  42.9 1.2 %query_kernel.1.refs_5_ = f32[512,1024]{1,0:T(8,128)S(1)} custom-call(bf16[640,1280]{1,0:T(8,128)(2,1)S(1)} %get-tuple-element.56.refs_0_.refs_1_, bf16[512,256]{1,0:T(8,128)(2,1)S(1)} %get-tuple-element.60.refs_1_, bf16[512,256]{1,0:T(8,128)(2,1)S(1)} %get-tuple-element.61.refs_2_), custom_call_target="tpu_custom_call" | custom-call | flops 1073741824 | bytes 4194304 | tf_op jit(solution)/shard_map/query_kernel/pallas_call | solution.py:241
  44.1 0.2 collective-permute-done.14.refs_2_
  44.4 1.2 %corr_kernel.2 = (bf16[128,1024]{1,0:T(8,128)(2,1)S(1)}, bf16[128,1024]{1,0:T(8,128)(2,1)S(1)}, bf16[256,512]{1,0:T(8,128)(2,1)S(1)}, bf16[256,512]{1,0:T(8,128)(2,1)S(1)}) custom-call(s32[2]{0:T(128)S(1)} %pad_add_fusion.refs_0_, bf16[640,1280]{1,0:T(8,128)(2,1)S(1)} %get-tuple-element.56.refs_0_.refs_1_, ...), custom_call_target="tpu_custom_call" | custom-call | flops 268435456 | bytes 2097152 | tf_op jit(solution)/shard_map/corr_kernel/pallas_call | solution.py:299
  45.6 0.6 collective-permute-start.19
  46.1 1.2 %corr_kernel.3 = (bf16[128,1024]{1,0:T(8,128)(2,1)S(1)}, bf16[128,1024]{1,0:T(8,128)(2,1)S(1)}, bf16[512,512]{1,0:T(8,128)(2,1)S(1)}, bf16[512,512]{1,0:T(8,128)(2,1)S(1)}) custom-call(s32[2]{0:T(128)S(1)} %pad_add_fusion.refs_0_, bf16[640,1280]{1,0:T(8,128)(2,1)S(1)} %get-tuple-element.56.refs_0_.refs_1_, ...), custom_call_target="tpu_custom_call" | custom-call | flops 268435456 | bytes 2097152 | tf_op jit(solution)/shard_map/corr_kernel/pallas_call | solution.py:299
  47.3 0.1 collective-permute-start.17
  47.4 0.5 fusion.3
  47.9 1.6 %collective-permute-start.15 = (bf16[128,1024]{1,0:T(8,128)(2,1)S(1)}, bf16[128,1024]{1,0:T(8,128)(2,1)S(1)}, u32[]{:S(2)}, u32[]{:S(2)}) collective-permute-start(bf16[128,1024]{1,0:T(8,128)(2,1)S(1)} %get-tuple-element.65), channel_id=1, source_target_pairs={{0,2},{2,0},{4,6},{6,4},{8,10},{10,8},{12,14},{14,12},{1,3},{3,1},... | collective-permute-start | bytes 786440 | tf_op jit(solution)/shard_map/ppermute | solution.py:379
  49.4 0.5 fusion.5
  49.9 4.9 %collective-permute-done.19.refs_1_ = bf16[128,1024]{1,0:T(8,128)(2,1)S(1)} collective-permute-done((bf16[128,1024]{1,0:T(8,128)(2,1)S(1)}, bf16[128,1024]{1,0:T(8,128)(2,1)S(1)}, u32[]{:S(2)}, u32[]{:S(2)}) %collective-permute-start.19) | collective-permute-done | bytes 262176 | tf_op jit(solution)/shard_map/ppermute | solution.py:379
  54.8 0.7 %partial_kernel.3 = (bf16[64,1024]{1,0:T(8,128)(2,1)S(1)}, bf16[64,1024]{1,0:T(8,128)(2,1)S(1)}) custom-call(bf16[128,1024]{1,0:T(8,128)(2,1)S(1)} %get-tuple-element.81.refs_0_, bf16[128,1024]{1,0:T(8,128)(2,1)S(1)} %collective-permute-done.19.refs_1_, bf16[1024,1024]{1,0:T(8,128)(2,1)S(1)} %get-tuple-element.66.refs_2_, ...), custom_call_target="tpu_custom_call" | custom-call | flops 536870912 | bytes 4194304 | tf_op jit(solution)/shard_map/partial_kernel/pallas_call | solution.py:330
  55.5 1.0 %collective-permute-start.20 = (bf16[64,1024]{1,0:T(8,128)(2,1)S(1)}, bf16[64,1024]{1,0:T(8,128)(2,1)S(1)}, u32[]{:S(2)}, u32[]{:S(2)}) collective-permute-start(bf16[64,1024]{1,0:T(8,128)(2,1)S(1)} %get-tuple-element.83), channel_id=1, source_target_pairs={{0,8},{2,10},{4,12},{6,14},{8,0},{10,2},{12,4},{14,6},{1,9},{3,11}... | collective-permute-start | bytes 393224 | tf_op jit(solution)/shard_map/ppermute | solution.py:379
  56.5 1.6 %collective-permute-start.21 = (bf16[64,1024]{1,0:T(8,128)(2,1)S(1)}, bf16[64,1024]{1,0:T(8,128)(2,1)S(1)}, u32[]{:S(2)}, u32[]{:S(2)}) collective-permute-start(bf16[64,1024]{1,0:T(8,128)(2,1)S(1)} %get-tuple-element.84), channel_id=1, source_target_pairs={{0,12},{2,14},{4,8},{6,10},{8,4},{10,6},{12,0},{14,2},{1,13},{3,15... | collective-permute-start | bytes 393224 | tf_op jit(solution)/shard_map/ppermute | solution.py:379
  58.1 1.4 %collective-permute-done.15.refs_1_ = bf16[128,1024]{1,0:T(8,128)(2,1)S(1)} collective-permute-done((bf16[128,1024]{1,0:T(8,128)(2,1)S(1)}, bf16[128,1024]{1,0:T(8,128)(2,1)S(1)}, u32[]{:S(2)}, u32[]{:S(2)}) %collective-permute-start.15) | collective-permute-done | bytes 262176 | tf_op jit(solution)/shard_map/ppermute | solution.py:379
  59.6 0.7 %partial_kernel.2 = (f32[64,1024]{1,0:T(8,128)S(1)}, bf16[64,1024]{1,0:T(8,128)(2,1)S(1)}) custom-call(bf16[128,1024]{1,0:T(8,128)(2,1)S(1)} %get-tuple-element.64.refs_0_, bf16[128,1024]{1,0:T(8,128)(2,1)S(1)} %collective-permute-done.15.refs_1_, bf16[1024,1024]{1,0:T(8,128)(2,1)S(1)} %get-tuple-element.66.refs_2_, ...), custom_call_target="tpu_custom_call" | custom-call | flops 536870912 | bytes 4194304 | tf_op jit(solution)/shard_map/partial_kernel/pallas_call | solution.py:330
  60.3 0.1 collective-permute-start.16
  60.4 0.5 fusion
  60.9 1.8 %add_multiply_fusion = f32[512,1024]{1,0:T(8,128)} fusion(f32[512,1024]{1,0:T(8,128)S(1)} %fusion, f32[512,1024]{1,0:T(8,128)S(1)} %fusion.5, f32[512,1024]{1,0:T(8,128)S(1)} %fusion.3, bf16[512,1024]{1,0:T(8,128)(2,1)S(1)} %collective-permute-done.18, bf16[512,512]{1,0:T(8,128)(2,1)S(1)} %collective-permute-done.17), kind=kOutput, calls=%fused_computation | convolution fusion | flops 270532608 | bytes 9175040 | tf_op jit(solution)/shard_map/dot_general | solution.py:434
  62.7 5.9 %collective-permute-done.16 = bf16[64,1024]{1,0:T(8,128)(2,1)S(1)} collective-permute-done((bf16[64,1024]{1,0:T(8,128)(2,1)S(1)}, bf16[64,1024]{1,0:T(8,128)(2,1)S(1)}, u32[]{:S(2)}, u32[]{:S(2)}) %collective-permute-start.16) | collective-permute-done | bytes 131104 | tf_op jit(solution)/shard_map/ppermute | solution.py:379
  68.6 0.8 %multiply_bitcast_fusion = f32[1,64,1024]{2,1,0:T(8,128)} fusion(bf16[64,1024]{1,0:T(8,128)(2,1)S(1)} %collective-permute-done.16, bf16[64,1024]{1,0:T(8,128)(2,1)S(1)} %collective-permute-done.21, f32[64,1024]{1,0:T(8,128)S(1)} %get-tuple-element.80, bf16[64,1024]{1,0:T(8,128)(2,1)S(1)} %collective-permute-done.20), kind=kLoop, calls=%fused_computation.18 | loop fusion | flops 458752 | bytes 917504 | tf_op jit(solution)/shard_map/broadcast_in_dim | solution.py:446
  (21 shorter events, 0.1 us)
Async XLA Ops:
  0.6 9.3 %copy-start.2 = (f32[3,3]{1,0:T(4,128)S(1)}, f32[3,3]{1,0:T(4,128)}, u32[]{:S(2)}) copy-start(f32[3,3]{1,0:T(4,128)} %param.8) | copy-start | bytes 112
  0.6 9.3 %copy-start.1 = (f32[3,3]{1,0:T(4,128)S(1)}, f32[3,3]{1,0:T(4,128)}, u32[]{:S(2)}) copy-start(f32[3,3]{1,0:T(4,128)} %param.9) | copy-start | bytes 112
  0.6 10.7 %collective-permute-start.3 = (bf16[64,1024]{1,0:T(8,128)(2,1)}, bf16[64,1024]{1,0:T(8,128)(2,1)S(1)}, u32[]{:S(2)}, u32[]{:S(2)}) collective-permute-start(bf16[64,1024]{1,0:T(8,128)(2,1)} %bitcast.14), channel_id=1, source_target_pairs={{0,8},{2,10},{4,12},{6,14},{8,0},{10,2},{12,4},{14,6},{1,9},{3,11}... | collective-permute-start | bytes 393224 | tf_op jit(solution)/shard_map/ppermute | solution.py:379
  4.8 8.3 %collective-permute-start.1 = (bf16[64,1024]{1,0:T(8,128)(2,1)}, bf16[64,1024]{1,0:T(8,128)(2,1)S(1)}, u32[]{:S(2)}, u32[]{:S(2)}) collective-permute-start(bf16[64,1024]{1,0:T(8,128)(2,1)} %bitcast.15), channel_id=1, source_target_pairs={{0,4},{2,6},{4,0},{6,2},{8,12},{10,14},{12,8},{14,10},{1,5},{3,7},... | collective-permute-start | bytes 393224 | tf_op jit(solution)/shard_map/ppermute | solution.py:379
  6.3 8.3 %collective-permute-start = (bf16[64,1024]{1,0:T(8,128)(2,1)}, bf16[64,1024]{1,0:T(8,128)(2,1)S(1)}, u32[]{:S(2)}, u32[]{:S(2)}) collective-permute-start(bf16[64,1024]{1,0:T(8,128)(2,1)} %bitcast.16), channel_id=1, source_target_pairs={{0,2},{2,0},{4,6},{6,4},{8,10},{10,8},{12,14},{14,12},{1,3},{3,1},... | collective-permute-start | bytes 393224 | tf_op jit(solution)/shard_map/ppermute | solution.py:379
  9.3 10.2 %collective-permute-start.10 = (bf16[64,1280]{1,0:T(8,128)(2,1)S(1)}, bf16[64,1280]{1,0:T(8,128)(2,1)S(1)}, u32[]{:S(2)}, u32[]{:S(2)}) collective-permute-start(bf16[64,1280]{1,0:T(8,128)(2,1)S(1)} %get-tuple-element.91), channel_id=1, source_target_pairs={{0,8},{2,10},{4,12},{6,14},{8,0},{10,2},{12,4},{14,6},{1,9},{3,11}... | collective-permute-start | bytes 491528 | tf_op jit(solution)/shard_map/ppermute | solution.py:379
  9.7 11.2 %collective-permute-start.11 = (bf16[64,1280]{1,0:T(8,128)(2,1)S(1)}, bf16[64,1280]{1,0:T(8,128)(2,1)S(1)}, u32[]{:S(2)}, u32[]{:S(2)}) collective-permute-start(bf16[64,1280]{1,0:T(8,128)(2,1)S(1)} %get-tuple-element.92), channel_id=1, source_target_pairs={{0,6},{2,4},{4,2},{6,0},{8,14},{10,12},{12,10},{14,8},{1,7},{3,5},... | collective-permute-start | bytes 491528 | tf_op jit(solution)/shard_map/ppermute | solution.py:379
  11.4 14.3 %collective-permute-start.12 = (bf16[64,1280]{1,0:T(8,128)(2,1)S(1)}, bf16[64,1280]{1,0:T(8,128)(2,1)S(1)}, u32[]{:S(2)}, u32[]{:S(2)}) collective-permute-start(bf16[64,1280]{1,0:T(8,128)(2,1)S(1)} %get-tuple-element.93), channel_id=1, source_target_pairs={{0,4},{2,6},{4,0},{6,2},{8,12},{10,14},{12,8},{14,10},{1,5},{3,7},... | collective-permute-start | bytes 491528 | tf_op jit(solution)/shard_map/ppermute | solution.py:379
  13.1 12.7 %collective-permute-start.13 = (bf16[64,1280]{1,0:T(8,128)(2,1)S(1)}, bf16[64,1280]{1,0:T(8,128)(2,1)S(1)}, u32[]{:S(2)}, u32[]{:S(2)}) collective-permute-start(bf16[64,1280]{1,0:T(8,128)(2,1)S(1)} %get-tuple-element.94), channel_id=1, source_target_pairs={{0,2},{2,0},{4,6},{6,4},{8,10},{10,8},{12,14},{14,12},{1,3},{3,1},... | collective-permute-start | bytes 491528 | tf_op jit(solution)/shard_map/ppermute | solution.py:379
  14.6 13.9 %collective-permute-start.7 = (bf16[64,1280]{1,0:T(8,128)(2,1)S(1)}, bf16[64,1280]{1,0:T(8,128)(2,1)S(1)}, u32[]{:S(2)}, u32[]{:S(2)}) collective-permute-start(bf16[64,1280]{1,0:T(8,128)(2,1)S(1)} %get-tuple-element.95), channel_id=1, source_target_pairs={{0,14},{2,12},{4,10},{6,8},{8,6},{10,4},{12,2},{14,0},{1,15},{3,13... | collective-permute-start | bytes 491528 | tf_op jit(solution)/shard_map/ppermute | solution.py:379
  19.6 9.8 %collective-permute-start.5 = (bf16[64,1024]{1,0:T(8,128)(2,1)S(1)}, bf16[64,1024]{1,0:T(8,128)(2,1)S(1)}, u32[]{:S(2)}, u32[]{:S(2)}) collective-permute-start(bf16[64,1024]{1,0:T(8,128)(2,1)S(1)} %collective-permute-done.3.refs_4_), channel_id=1, source_target_pairs={{0,4},{2,6},{4,0},{6,2},{8,12},{10,14},{12,8},{14,10},{1,5},{3,7},... | collective-permute-start | bytes 393224 | tf_op jit(solution)/shard_map/ppermute | solution.py:379
  21.0 13.3 %collective-permute-start.8 = (bf16[64,1280]{1,0:T(8,128)(2,1)S(1)}, bf16[64,1280]{1,0:T(8,128)(2,1)S(1)}, u32[]{:S(2)}, u32[]{:S(2)}) collective-permute-start(bf16[64,1280]{1,0:T(8,128)(2,1)S(1)} %get-tuple-element.89), channel_id=1, source_target_pairs={{0,12},{2,14},{4,8},{6,10},{8,4},{10,6},{12,0},{14,2},{1,13},{3,15... | collective-permute-start | bytes 491528 | tf_op jit(solution)/shard_map/ppermute | solution.py:379
  25.7 15.8 %copy-start = (bf16[1,64,1024]{2,1,0:T(8,128)(2,1)S(1)}, bf16[1,64,1024]{2,1,0:T(8,128)(2,1)}, u32[]{:S(2)}) copy-start(bf16[1,64,1024]{2,1,0:T(8,128)(2,1)} %param.7) | copy-start | bytes 393220
  25.7 15.8 %collective-permute-start.9 = (bf16[64,1280]{1,0:T(8,128)(2,1)S(1)}, bf16[64,1280]{1,0:T(8,128)(2,1)S(1)}, u32[]{:S(2)}, u32[]{:S(2)}) collective-permute-start(bf16[64,1280]{1,0:T(8,128)(2,1)S(1)} %get-tuple-element.90), channel_id=1, source_target_pairs={{0,10},{2,8},{4,14},{6,12},{8,2},{10,0},{12,6},{14,4},{1,11},{3,9}... | collective-permute-start | bytes 491528 | tf_op jit(solution)/shard_map/ppermute | solution.py:379
  25.8 15.6 %collective-permute-start.4 = (bf16[64,1024]{1,0:T(8,128)(2,1)S(1)}, bf16[64,1024]{1,0:T(8,128)(2,1)S(1)}, u32[]{:S(2)}, u32[]{:S(2)}) collective-permute-start(bf16[64,1024]{1,0:T(8,128)(2,1)S(1)} %collective-permute-done.3.refs_4_), channel_id=1, source_target_pairs={{0,2},{2,0},{4,6},{6,4},{8,10},{10,8},{12,14},{14,12},{1,3},{3,1},... | collective-permute-start | bytes 393224 | tf_op jit(solution)/shard_map/ppermute | solution.py:379
  28.5 12.9 %collective-permute-start.2 = (bf16[64,1024]{1,0:T(8,128)(2,1)S(1)}, bf16[64,1024]{1,0:T(8,128)(2,1)S(1)}, u32[]{:S(2)}, u32[]{:S(2)}) collective-permute-start(bf16[64,1024]{1,0:T(8,128)(2,1)S(1)} %collective-permute-done.1.refs_2_), channel_id=1, source_target_pairs={{0,2},{2,0},{4,6},{6,4},{8,10},{10,8},{12,14},{14,12},{1,3},{3,1},... | collective-permute-start | bytes 393224 | tf_op jit(solution)/shard_map/ppermute | solution.py:379
  29.4 12.1 %collective-permute-start.6 = (bf16[64,1024]{1,0:T(8,128)(2,1)S(1)}, bf16[64,1024]{1,0:T(8,128)(2,1)S(1)}, u32[]{:S(2)}, u32[]{:S(2)}) collective-permute-start(bf16[64,1024]{1,0:T(8,128)(2,1)S(1)} %collective-permute-done.5.refs_6_), channel_id=1, source_target_pairs={{0,2},{2,0},{4,6},{6,4},{8,10},{10,8},{12,14},{14,12},{1,3},{3,1},... | collective-permute-start | bytes 393224 | tf_op jit(solution)/shard_map/ppermute | solution.py:379
  41.5 18.9 %collective-permute-start.18 = (bf16[512,1024]{1,0:T(8,128)(2,1)S(1)}, bf16[512,1024]{1,0:T(8,128)(2,1)S(1)}, u32[]{:S(2)}, u32[]{:S(2)}) collective-permute-start(bf16[512,1024]{1,0:T(8,128)(2,1)S(1)} %stack_kernel.1), channel_id=1, source_target_pairs={{0,1},{1,0},{2,3},{3,2},{4,5},{5,4},{6,7},{7,6},{8,9},{9,8},{10,11... | collective-permute-start | bytes 3145736 | tf_op jit(solution)/shard_map/ppermute | solution.py:382
  42.3 2.0 %collective-permute-start.14 = (bf16[32,1024]{1,0:T(8,128)(2,1)S(1)}, bf16[32,1024]{1,0:T(8,128)(2,1)S(1)}, u32[]{:S(2)}, u32[]{:S(2)}) collective-permute-start(bf16[32,1024]{1,0:T(8,128)(2,1)S(1)} %get-tuple-element.57), channel_id=1, source_target_pairs={{0,1},{1,0},{2,3},{3,2},{4,5},{5,4},{6,7},{7,6},{8,9},{9,8},{10,11... | collective-permute-start | bytes 196616 | tf_op jit(solution)/shard_map/ppermute | solution.py:382
  45.6 9.2 %collective-permute-start.19 = (bf16[128,1024]{1,0:T(8,128)(2,1)S(1)}, bf16[128,1024]{1,0:T(8,128)(2,1)S(1)}, u32[]{:S(2)}, u32[]{:S(2)}) collective-permute-start(bf16[128,1024]{1,0:T(8,128)(2,1)S(1)} %get-tuple-element.82), channel_id=1, source_target_pairs={{0,2},{2,0},{4,6},{6,4},{8,10},{10,8},{12,14},{14,12},{1,3},{3,1},... | collective-permute-start | bytes 786440 | tf_op jit(solution)/shard_map/ppermute | solution.py:379
  47.3 13.1 %collective-permute-start.17 = (bf16[512,512]{1,0:T(8,128)(2,1)S(1)}, bf16[512,512]{1,0:T(8,128)(2,1)S(1)}, u32[]{:S(2)}, u32[]{:S(2)}) collective-permute-start(bf16[512,512]{1,0:T(8,128)(2,1)S(1)} %get-tuple-element.78), channel_id=1, source_target_pairs={{0,1},{1,0},{2,3},{3,2},{4,5},{5,4},{6,7},{7,6},{8,9},{9,8},{10,11... | collective-permute-start | bytes 1572872 | tf_op jit(solution)/shard_map/ppermute | solution.py:382
  47.9 11.7 %collective-permute-start.15 = (bf16[128,1024]{1,0:T(8,128)(2,1)S(1)}, bf16[128,1024]{1,0:T(8,128)(2,1)S(1)}, u32[]{:S(2)}, u32[]{:S(2)}) collective-permute-start(bf16[128,1024]{1,0:T(8,128)(2,1)S(1)} %get-tuple-element.65), channel_id=1, source_target_pairs={{0,2},{2,0},{4,6},{6,4},{8,10},{10,8},{12,14},{14,12},{1,3},{3,1},... | collective-permute-start | bytes 786440 | tf_op jit(solution)/shard_map/ppermute | solution.py:379
  55.5 13.1 %collective-permute-start.20 = (bf16[64,1024]{1,0:T(8,128)(2,1)S(1)}, bf16[64,1024]{1,0:T(8,128)(2,1)S(1)}, u32[]{:S(2)}, u32[]{:S(2)}) collective-permute-start(bf16[64,1024]{1,0:T(8,128)(2,1)S(1)} %get-tuple-element.83), channel_id=1, source_target_pairs={{0,8},{2,10},{4,12},{6,14},{8,0},{10,2},{12,4},{14,6},{1,9},{3,11}... | collective-permute-start | bytes 393224 | tf_op jit(solution)/shard_map/ppermute | solution.py:379
  56.5 12.1 %collective-permute-start.21 = (bf16[64,1024]{1,0:T(8,128)(2,1)S(1)}, bf16[64,1024]{1,0:T(8,128)(2,1)S(1)}, u32[]{:S(2)}, u32[]{:S(2)}) collective-permute-start(bf16[64,1024]{1,0:T(8,128)(2,1)S(1)} %get-tuple-element.84), channel_id=1, source_target_pairs={{0,12},{2,14},{4,8},{6,10},{8,4},{10,6},{12,0},{14,2},{1,13},{3,15... | collective-permute-start | bytes 393224 | tf_op jit(solution)/shard_map/ppermute | solution.py:379
  60.3 8.3 %collective-permute-start.16 = (bf16[64,1024]{1,0:T(8,128)(2,1)S(1)}, bf16[64,1024]{1,0:T(8,128)(2,1)S(1)}, u32[]{:S(2)}, u32[]{:S(2)}) collective-permute-start(bf16[64,1024]{1,0:T(8,128)(2,1)S(1)} %get-tuple-element.68), channel_id=1, source_target_pairs={{0,4},{2,6},{4,0},{6,2},{8,12},{10,14},{12,8},{14,10},{1,5},{3,7},... | collective-permute-start | bytes 393224 | tf_op jit(solution)/shard_map/ppermute | solution.py:379

commit v6 on v5

--- a/solution.py
+++ b/solution.py
@@ -409,10 +409,10 @@
     mats = matrix_call(place, query_kernel, support_kernel, count, columns, edge)
     here = lax.dynamic_slice(query_feats, (side * tile, 0), (tile, width))
     there = lax.dynamic_slice(query_feats, ((side ^ 1) * tile, 0), (tile, width))
-    ordered = held + [pieces[k] for k in [7, 6, 5, 4, 3, 2, 1, 0]]
+    ordered = held + [pieces[k] for k in [7, 5, 6, 4, 3, 2, 1, 0]]
     ordered, mats, here, there = lax.optimization_barrier((ordered, mats, here, there))
     held, landed = ordered[:count], ordered[count:]
-    for at, k in enumerate([7, 6, 5, 4, 3, 2, 1, 0]):
+    for at, k in enumerate([7, 5, 6, 4, 3, 2, 1, 0]):
         pieces[k] = landed[at]
     cells, rim = gather_call(place, pieces, tile, edge)
     rim = swapped(rim)

time: 69.6 us -> 67.5 us (0.970)
  waiting for transfers between devices: 28.5 us -> 19 us
  starting transfers between devices: 24.7 us -> 32.1 us
    ppermute x19, waiting for transfers between devices: 28.3 us -> 18.8 us  [exchanged(): lax.ppermute(value, ('blk', 'sub'), [(i, i ^ mask) for i in range(count)])]
    ppermute x19, starting transfers between devices: 24 us -> 31.4 us  [exchanged(): lax.ppermute(value, ('blk', 'sub'), [(i, i ^ mask) for i in range(count)])]
where the time goes in v6:
time: 67.5 us; the launch traced here: 67.3 us
  starting transfers between devices  32.1 us (48%)
  waiting for transfers between devices  19 us (28%)
  Pallas kernels  7.05 us (10%)
  local copies, waits for them, and re-layouts  4.28 us (6%)
  matrix products  3.19 us (5%)
  other arithmetic  0.86 us (1%)
  between operations  0.79 us (1%)
    ppermute x19, starting transfers between devices, exchanged(): lax.ppermute(value, ('blk', 'sub'), [(i, i ^ mask) for i in range(count)])  31.4 us
    ppermute x19, waiting for transfers between devices, exchanged(): lax.ppermute(value, ('blk', 'sub'), [(i, i ^ mask) for i in range(count)])  18.8 us
    dot_general x4, matrix products, query_term(): lax.dot_general(block, feats, (((0,), (0,)), ((), ())), preferred_element...  3.19 us
    dynamic_slice x1, local copies, waits for them, and re-layouts, tile_shards(): lax.dynamic_slice(query_feats, ((side ^ 1) * tile, 0), (tile, width))  2.66 us
    pallas_call x2, Pallas kernels, corr_call(): pl.pallas_call(lambda *refs: corr_kernel(group, columns, tile, *refs), ou...  2.38 us
    dynamic_slice x1, local copies, waits for them, and re-layouts, piece(): lax.dynamic_slice(volume, (0, (own ^ mask) * tile), (columns, tile + 2 *...  1.52 us
    pallas_call x2, Pallas kernels, partial_call(): pl.pallas_call(lambda *refs: partial_kernel(columns, *refs), out_shape=[j...  1.46 us
  transfers between devices with their start and end apart: 22, of which 10 were waited for; matrix products, arithmetic and copies ran while one was open for 11% of the time, Pallas kernels for 10%

profile of v6, /device:TPU:0, one launch (start us, length us, event | category | flops | bytes accessed | tf_op | source)
XLA Modules:
  0.0 67.3 jit_solution(8723032233841402838)
XLA Ops:
  0.6 4.1 %collective-permute-start.3 = (bf16[64,1024]{1,0:T(8,128)(2,1)}, bf16[64,1024]{1,0:T(8,128)(2,1)S(1)}, u32[]{:S(2)}, u32[]{:S(2)}) collective-permute-start(bf16[64,1024]{1,0:T(8,128)(2,1)} %bitcast.14), channel_id=1, source_target_pairs={{0,8},{2,10},{4,12},{6,14},{8,0},{10,2},{12,4},{14,6},{1,9},{3,11}... | collective-permute-start | bytes 393224 | tf_op jit(solution)/shard_map/ppermute | solution.py:379
  4.8 1.6 %collective-permute-start.1 = (bf16[64,1024]{1,0:T(8,128)(2,1)}, bf16[64,1024]{1,0:T(8,128)(2,1)S(1)}, u32[]{:S(2)}, u32[]{:S(2)}) collective-permute-start(bf16[64,1024]{1,0:T(8,128)(2,1)} %bitcast.15), channel_id=1, source_target_pairs={{0,4},{2,6},{4,0},{6,2},{8,12},{10,14},{12,8},{14,10},{1,5},{3,7},... | collective-permute-start | bytes 393224 | tf_op jit(solution)/shard_map/ppermute | solution.py:379
  6.3 1.5 %collective-permute-start = (bf16[64,1024]{1,0:T(8,128)(2,1)}, bf16[64,1024]{1,0:T(8,128)(2,1)S(1)}, u32[]{:S(2)}, u32[]{:S(2)}) collective-permute-start(bf16[64,1024]{1,0:T(8,128)(2,1)} %bitcast.16), channel_id=1, source_target_pairs={{0,2},{2,0},{4,6},{6,4},{8,10},{10,8},{12,14},{14,12},{1,3},{3,1},... | collective-permute-start | bytes 393224 | tf_op jit(solution)/shard_map/ppermute | solution.py:379
  7.8 1.5 %pad_dynamic-slice_fusion = (bf16[64,1280]{1,0:T(8,128)(2,1)S(1)}, bf16[64,1280]{1,0:T(8,128)(2,1)S(1)}, bf16[64,1280]{1,0:T(8,128)(2,1)S(1)}, bf16[64,1280]{1,0...) fusion(s32[]{:T(128)S(6)} %select_n.37, ...), kind=kLoop, calls=%fused_computation.8 | loop fusion | bytes 2359328 | tf_op jit(solution)/shard_map/dynamic_slice | solution.py:387
  9.3 0.4 collective-permute-start.10
  9.7 0.2 collective-permute-start.11
  9.9 1.4 %collective-permute-done.3.refs_4_ = bf16[64,1024]{1,0:T(8,128)(2,1)S(1)} collective-permute-done((bf16[64,1024]{1,0:T(8,128)(2,1)}, bf16[64,1024]{1,0:T(8,128)(2,1)S(1)}, u32[]{:S(2)}, u32[]{:S(2)}) %collective-permute-start.3) | collective-permute-done | bytes 131104 | tf_op jit(solution)/shard_map/ppermute | solution.py:379
  11.4 1.7 %collective-permute-start.12 = (bf16[64,1280]{1,0:T(8,128)(2,1)S(1)}, bf16[64,1280]{1,0:T(8,128)(2,1)S(1)}, u32[]{:S(2)}, u32[]{:S(2)}) collective-permute-start(bf16[64,1280]{1,0:T(8,128)(2,1)S(1)} %get-tuple-element.93), channel_id=1, source_target_pairs={{0,4},{2,6},{4,0},{6,2},{8,12},{10,14},{12,8},{14,10},{1,5},{3,7},... | collective-permute-start | bytes 491528 | tf_op jit(solution)/shard_map/ppermute | solution.py:379
  13.1 1.5 %collective-permute-start.13 = (bf16[64,1280]{1,0:T(8,128)(2,1)S(1)}, bf16[64,1280]{1,0:T(8,128)(2,1)S(1)}, u32[]{:S(2)}, u32[]{:S(2)}) collective-permute-start(bf16[64,1280]{1,0:T(8,128)(2,1)S(1)} %get-tuple-element.94), channel_id=1, source_target_pairs={{0,2},{2,0},{4,6},{6,4},{8,10},{10,8},{12,14},{14,12},{1,3},{3,1},... | collective-permute-start | bytes 491528 | tf_op jit(solution)/shard_map/ppermute | solution.py:379
  14.6 2.9 %collective-permute-start.7 = (bf16[64,1280]{1,0:T(8,128)(2,1)S(1)}, bf16[64,1280]{1,0:T(8,128)(2,1)S(1)}, u32[]{:S(2)}, u32[]{:S(2)}) collective-permute-start(bf16[64,1280]{1,0:T(8,128)(2,1)S(1)} %get-tuple-element.95), channel_id=1, source_target_pairs={{0,14},{2,12},{4,10},{6,8},{8,6},{10,4},{12,2},{14,0},{1,15},{3,13... | collective-permute-start | bytes 491528 | tf_op jit(solution)/shard_map/ppermute | solution.py:379
  17.5 2.0 %collective-permute-done.10.refs_4_ = bf16[64,1280]{1,0:T(8,128)(2,1)S(1)} collective-permute-done((bf16[64,1280]{1,0:T(8,128)(2,1)S(1)}, bf16[64,1280]{1,0:T(8,128)(2,1)S(1)}, u32[]{:S(2)}, u32[]{:S(2)}) %collective-permute-start.10) | collective-permute-done | bytes 163872 | tf_op jit(solution)/shard_map/ppermute | solution.py:379
  19.6 0.1 reshape.7.refs_1_
  19.7 0.1 pad_add_fusion.refs_0_
  19.8 1.2 %matrix_kernel.1 = (bf16[256,256]{1,0:T(8,128)(2,1)S(1)}, bf16[512,32]{1,0:T(8,128)(2,1)S(1)}, bf16[512,256]{1,0:T(8,128)(2,1)S(1)}, bf16[512,256]{1,0:T(8,128)(2,1)S(1)}) custom-call(s32[2]{0:T(128)S(1)} %pad_add_fusion.refs_0_, f32[36]{0:T(128)S(1)} %reshape.7.refs_1_), custom_call_target="tpu_custom_call" | custom-call | flops 2621440 | bytes 524288 | tf_op jit(solution)/shard_map/matrix_kernel/pallas_call | solution.py:171
  21.0 3.9 %collective-permute-start.8 = (bf16[64,1280]{1,0:T(8,128)(2,1)S(1)}, bf16[64,1280]{1,0:T(8,128)(2,1)S(1)}, u32[]{:S(2)}, u32[]{:S(2)}) collective-permute-start(bf16[64,1280]{1,0:T(8,128)(2,1)S(1)} %get-tuple-element.89), channel_id=1, source_target_pairs={{0,10},{2,8},{4,14},{6,12},{8,2},{10,0},{12,6},{14,4},{1,11},{3,9}... | collective-permute-start | bytes 491528 | tf_op jit(solution)/shard_map/ppermute | solution.py:379
  24.9 3.6 %collective-permute-done.12.refs_6_ = bf16[64,1280]{1,0:T(8,128)(2,1)S(1)} collective-permute-done((bf16[64,1280]{1,0:T(8,128)(2,1)S(1)}, bf16[64,1280]{1,0:T(8,128)(2,1)S(1)}, u32[]{:S(2)}, u32[]{:S(2)}) %collective-permute-start.12) | collective-permute-done | bytes 163872 | tf_op jit(solution)/shard_map/ppermute | solution.py:379
  28.5 2.5 %collective-permute-start.9 = (bf16[64,1280]{1,0:T(8,128)(2,1)S(1)}, bf16[64,1280]{1,0:T(8,128)(2,1)S(1)}, u32[]{:S(2)}, u32[]{:S(2)}) collective-permute-start(bf16[64,1280]{1,0:T(8,128)(2,1)S(1)} %get-tuple-element.90), channel_id=1, source_target_pairs={{0,12},{2,14},{4,8},{6,10},{8,4},{10,6},{12,0},{14,2},{1,13},{3,15... | collective-permute-start | bytes 491528 | tf_op jit(solution)/shard_map/ppermute | solution.py:379
  31.0 1.7 %collective-permute-start.4 = (bf16[64,1024]{1,0:T(8,128)(2,1)S(1)}, bf16[64,1024]{1,0:T(8,128)(2,1)S(1)}, u32[]{:S(2)}, u32[]{:S(2)}) collective-permute-start(bf16[64,1024]{1,0:T(8,128)(2,1)S(1)} %collective-permute-done.3.refs_4_), channel_id=1, source_target_pairs={{0,2},{2,0},{4,6},{6,4},{8,10},{10,8},{12,14},{14,12},{1,3},{3,1},... | collective-permute-start | bytes 393224 | tf_op jit(solution)/shard_map/ppermute | solution.py:379
  32.7 0.3 collective-permute-start.2
  33.0 1.7 %collective-permute-start.6 = (bf16[64,1024]{1,0:T(8,128)(2,1)S(1)}, bf16[64,1024]{1,0:T(8,128)(2,1)S(1)}, u32[]{:S(2)}, u32[]{:S(2)}) collective-permute-start(bf16[64,1024]{1,0:T(8,128)(2,1)S(1)} %collective-permute-done.5.refs_6_), channel_id=1, source_target_pairs={{0,2},{2,0},{4,6},{6,4},{8,10},{10,8},{12,14},{14,12},{1,3},{3,1},... | collective-permute-start | bytes 393224 | tf_op jit(solution)/shard_map/ppermute | solution.py:379
  34.8 2.7 %constant_dynamic-slice_fusion = (bf16[1024,1024]{1,0:T(8,128)(2,1)S(1)}, bf16[1024,1024]{1,0:T(8,128)(2,1)S(1)}) fusion(bf16[2048,1024]{1,0:T(8,128)(2,1)} %param.6, s32[]{:T(128)S(6)} %select_n.39, s32[]{:T(128)S(6)} %select_n.38), kind=kLoop, calls=%fused_computation.26 | loop fusion | bytes 8388616 | tf_op jit(solution)/shard_map/dynamic_slice | solution.py:411
  37.4 0.6 collective-permute-done.8.refs_3_
  38.1 0.3 collective-permute-done.2.refs_3_
  38.4 1.4 %collective-permute-done.6.refs_7_ = bf16[64,1024]{1,0:T(8,128)(2,1)S(1)} collective-permute-done((bf16[64,1024]{1,0:T(8,128)(2,1)S(1)}, bf16[64,1024]{1,0:T(8,128)(2,1)S(1)}, u32[]{:S(2)}, u32[]{:S(2)}) %collective-permute-start.6) | collective-permute-done | bytes 131104 | tf_op jit(solution)/shard_map/ppermute | solution.py:379
  39.8 0.1 stack_kernel.1
  39.8 0.1 collective-permute-start.18
  39.9 0.7 %gather_kernel.1 = (bf16[640,1280]{1,0:T(8,128)(2,1)S(1)}, bf16[32,1024]{1,0:T(8,128)(2,1)S(1)}) custom-call(s32[2]{0:T(128)S(1)} %pad_add_fusion.refs_0_, bf16[64,1280]{1,0:T(8,128)(2,1)S(1)} %collective-permute-done.7.refs_1_, bf16[64,1280]{1,0:T(8,128)(2,1)S(1)} %collective-permute-done.9.refs_2_, bf16[64,1280]{1,0:T(8,128)(2,1)S(1)} %collective-permute-done.8.refs_3_, ...), custom_call_target="tpu_custom_call" | custom-call | flops 8192 | bytes 2621440 | tf_op jit(solution)/shard_map/gather_kernel/pallas_call | solution.py:209
  40.6 0.6 collective-permute-start.14
  41.2 1.2 %query_kernel.1.refs_5_ = f32[512,1024]{1,0:T(8,128)S(1)} custom-call(bf16[640,1280]{1,0:T(8,128)(2,1)S(1)} %get-tuple-element.56.refs_0_.refs_1_, bf16[512,256]{1,0:T(8,128)(2,1)S(1)} %get-tuple-element.60.refs_1_, bf16[512,256]{1,0:T(8,128)(2,1)S(1)} %get-tuple-element.61.refs_2_), custom_call_target="tpu_custom_call" | custom-call | flops 1073741824 | bytes 4194304 | tf_op jit(solution)/shard_map/query_kernel/pallas_call | solution.py:241
  42.5 0.2 collective-permute-done.14.refs_2_
  42.7 1.2 %corr_kernel.2 = (bf16[128,1024]{1,0:T(8,128)(2,1)S(1)}, bf16[128,1024]{1,0:T(8,128)(2,1)S(1)}, bf16[256,512]{1,0:T(8,128)(2,1)S(1)}, bf16[256,512]{1,0:T(8,128)(2,1)S(1)}) custom-call(s32[2]{0:T(128)S(1)} %pad_add_fusion.refs_0_, bf16[640,1280]{1,0:T(8,128)(2,1)S(1)} %get-tuple-element.56.refs_0_.refs_1_, ...), custom_call_target="tpu_custom_call" | custom-call | flops 268435456 | bytes 2097152 | tf_op jit(solution)/shard_map/corr_kernel/pallas_call | solution.py:299
  43.9 1.5 %collective-permute-start.19 = (bf16[128,1024]{1,0:T(8,128)(2,1)S(1)}, bf16[128,1024]{1,0:T(8,128)(2,1)S(1)}, u32[]{:S(2)}, u32[]{:S(2)}) collective-permute-start(bf16[128,1024]{1,0:T(8,128)(2,1)S(1)} %get-tuple-element.82), channel_id=1, source_target_pairs={{0,2},{2,0},{4,6},{6,4},{8,10},{10,8},{12,14},{14,12},{1,3},{3,1},... | collective-permute-start | bytes 786440 | tf_op jit(solution)/shard_map/ppermute | solution.py:379
  45.4 1.2 %corr_kernel.3 = (bf16[128,1024]{1,0:T(8,128)(2,1)S(1)}, bf16[128,1024]{1,0:T(8,128)(2,1)S(1)}, bf16[512,512]{1,0:T(8,128)(2,1)S(1)}, bf16[512,512]{1,0:T(8,128)(2,1)S(1)}) custom-call(s32[2]{0:T(128)S(1)} %pad_add_fusion.refs_0_, bf16[640,1280]{1,0:T(8,128)(2,1)S(1)} %get-tuple-element.56.refs_0_.refs_1_, ...), custom_call_target="tpu_custom_call" | custom-call | flops 268435456 | bytes 2097152 | tf_op jit(solution)/shard_map/corr_kernel/pallas_call | solution.py:299
  46.6 0.1 collective-permute-start.17
  46.7 0.5 fusion.3
  47.1 0.6 collective-permute-start.15
  47.8 0.5 fusion.5
  48.2 4.9 %collective-permute-done.19.refs_1_ = bf16[128,1024]{1,0:T(8,128)(2,1)S(1)} collective-permute-done((bf16[128,1024]{1,0:T(8,128)(2,1)S(1)}, bf16[128,1024]{1,0:T(8,128)(2,1)S(1)}, u32[]{:S(2)}, u32[]{:S(2)}) %collective-permute-start.19) | collective-permute-done | bytes 262176 | tf_op jit(solution)/shard_map/ppermute | solution.py:379
  53.1 0.7 %partial_kernel.3 = (bf16[64,1024]{1,0:T(8,128)(2,1)S(1)}, bf16[64,1024]{1,0:T(8,128)(2,1)S(1)}) custom-call(bf16[128,1024]{1,0:T(8,128)(2,1)S(1)} %get-tuple-element.81.refs_0_, bf16[128,1024]{1,0:T(8,128)(2,1)S(1)} %collective-permute-done.19.refs_1_, bf16[1024,1024]{1,0:T(8,128)(2,1)S(1)} %get-tuple-element.66.refs_2_, ...), custom_call_target="tpu_custom_call" | custom-call | flops 536870912 | bytes 4194304 | tf_op jit(solution)/shard_map/partial_kernel/pallas_call | solution.py:330
  53.8 2.7 %collective-permute-start.20 = (bf16[64,1024]{1,0:T(8,128)(2,1)S(1)}, bf16[64,1024]{1,0:T(8,128)(2,1)S(1)}, u32[]{:S(2)}, u32[]{:S(2)}) collective-permute-start(bf16[64,1024]{1,0:T(8,128)(2,1)S(1)} %get-tuple-element.83), channel_id=1, source_target_pairs={{0,8},{2,10},{4,12},{6,14},{8,0},{10,2},{12,4},{14,6},{1,9},{3,11}... | collective-permute-start | bytes 393224 | tf_op jit(solution)/shard_map/ppermute | solution.py:379
  56.5 1.0 %collective-permute-start.21 = (bf16[64,1024]{1,0:T(8,128)(2,1)S(1)}, bf16[64,1024]{1,0:T(8,128)(2,1)S(1)}, u32[]{:S(2)}, u32[]{:S(2)}) collective-permute-start(bf16[64,1024]{1,0:T(8,128)(2,1)S(1)} %get-tuple-element.84), channel_id=1, source_target_pairs={{0,12},{2,14},{4,8},{6,10},{8,4},{10,6},{12,0},{14,2},{1,13},{3,15... | collective-permute-start | bytes 393224 | tf_op jit(solution)/shard_map/ppermute | solution.py:379
  57.6 0.3 collective-permute-done.15.refs_1_
  57.9 0.7 %partial_kernel.2 = (f32[64,1024]{1,0:T(8,128)S(1)}, bf16[64,1024]{1,0:T(8,128)(2,1)S(1)}) custom-call(bf16[128,1024]{1,0:T(8,128)(2,1)S(1)} %get-tuple-element.64.refs_0_, bf16[128,1024]{1,0:T(8,128)(2,1)S(1)} %collective-permute-done.15.refs_1_, bf16[1024,1024]{1,0:T(8,128)(2,1)S(1)} %get-tuple-element.66.refs_2_, ...), custom_call_target="tpu_custom_call" | custom-call | flops 536870912 | bytes 4194304 | tf_op jit(solution)/shard_map/partial_kernel/pallas_call | solution.py:330
  58.6 1.4 %collective-permute-start.16 = (bf16[64,1024]{1,0:T(8,128)(2,1)S(1)}, bf16[64,1024]{1,0:T(8,128)(2,1)S(1)}, u32[]{:S(2)}, u32[]{:S(2)}) collective-permute-start(bf16[64,1024]{1,0:T(8,128)(2,1)S(1)} %get-tuple-element.68), channel_id=1, source_target_pairs={{0,4},{2,6},{4,0},{6,2},{8,12},{10,14},{12,8},{14,10},{1,5},{3,7},... | collective-permute-start | bytes 393224 | tf_op jit(solution)/shard_map/ppermute | solution.py:379
  60.0 0.5 fusion
  60.5 1.8 %add_multiply_fusion = f32[512,1024]{1,0:T(8,128)} fusion(f32[512,1024]{1,0:T(8,128)S(1)} %fusion, f32[512,1024]{1,0:T(8,128)S(1)} %fusion.5, f32[512,1024]{1,0:T(8,128)S(1)} %fusion.3, bf16[512,1024]{1,0:T(8,128)(2,1)S(1)} %collective-permute-done.18, bf16[512,512]{1,0:T(8,128)(2,1)S(1)} %collective-permute-done.17), kind=kOutput, calls=%fused_computation | convolution fusion | flops 270532608 | bytes 9175040 | tf_op jit(solution)/shard_map/dot_general | solution.py:434
  62.3 4.2 %collective-permute-done.16 = bf16[64,1024]{1,0:T(8,128)(2,1)S(1)} collective-permute-done((bf16[64,1024]{1,0:T(8,128)(2,1)S(1)}, bf16[64,1024]{1,0:T(8,128)(2,1)S(1)}, u32[]{:S(2)}, u32[]{:S(2)}) %collective-permute-start.16) | collective-permute-done | bytes 131104 | tf_op jit(solution)/shard_map/ppermute | solution.py:379
  66.5 0.8 %multiply_bitcast_fusion = f32[1,64,1024]{2,1,0:T(8,128)} fusion(bf16[64,1024]{1,0:T(8,128)(2,1)S(1)} %collective-permute-done.16, bf16[64,1024]{1,0:T(8,128)(2,1)S(1)} %collective-permute-done.21, f32[64,1024]{1,0:T(8,128)S(1)} %get-tuple-element.80, bf16[64,1024]{1,0:T(8,128)(2,1)S(1)} %collective-permute-done.20), kind=kLoop, calls=%fused_computation.18 | loop fusion | flops 458752 | bytes 917504 | tf_op jit(solution)/shard_map/broadcast_in_dim | solution.py:446
  (21 shorter events, 0.1 us)
Async XLA Ops:
  0.6 9.3 %copy-start.2 = (f32[3,3]{1,0:T(4,128)S(1)}, f32[3,3]{1,0:T(4,128)}, u32[]{:S(2)}) copy-start(f32[3,3]{1,0:T(4,128)} %param.8) | copy-start | bytes 112
  0.6 9.3 %copy-start.1 = (f32[3,3]{1,0:T(4,128)S(1)}, f32[3,3]{1,0:T(4,128)}, u32[]{:S(2)}) copy-start(f32[3,3]{1,0:T(4,128)} %param.9) | copy-start | bytes 112
  0.6 10.7 %collective-permute-start.3 = (bf16[64,1024]{1,0:T(8,128)(2,1)}, bf16[64,1024]{1,0:T(8,128)(2,1)S(1)}, u32[]{:S(2)}, u32[]{:S(2)}) collective-permute-start(bf16[64,1024]{1,0:T(8,128)(2,1)} %bitcast.14), channel_id=1, source_target_pairs={{0,8},{2,10},{4,12},{6,14},{8,0},{10,2},{12,4},{14,6},{1,9},{3,11}... | collective-permute-start | bytes 393224 | tf_op jit(solution)/shard_map/ppermute | solution.py:379
  4.8 8.3 %collective-permute-start.1 = (bf16[64,1024]{1,0:T(8,128)(2,1)}, bf16[64,1024]{1,0:T(8,128)(2,1)S(1)}, u32[]{:S(2)}, u32[]{:S(2)}) collective-permute-start(bf16[64,1024]{1,0:T(8,128)(2,1)} %bitcast.15), channel_id=1, source_target_pairs={{0,4},{2,6},{4,0},{6,2},{8,12},{10,14},{12,8},{14,10},{1,5},{3,7},... | collective-permute-start | bytes 393224 | tf_op jit(solution)/shard_map/ppermute | solution.py:379
  6.3 8.3 %collective-permute-start = (bf16[64,1024]{1,0:T(8,128)(2,1)}, bf16[64,1024]{1,0:T(8,128)(2,1)S(1)}, u32[]{:S(2)}, u32[]{:S(2)}) collective-permute-start(bf16[64,1024]{1,0:T(8,128)(2,1)} %bitcast.16), channel_id=1, source_target_pairs={{0,2},{2,0},{4,6},{6,4},{8,10},{10,8},{12,14},{14,12},{1,3},{3,1},... | collective-permute-start | bytes 393224 | tf_op jit(solution)/shard_map/ppermute | solution.py:379
  9.3 10.2 %collective-permute-start.10 = (bf16[64,1280]{1,0:T(8,128)(2,1)S(1)}, bf16[64,1280]{1,0:T(8,128)(2,1)S(1)}, u32[]{:S(2)}, u32[]{:S(2)}) collective-permute-start(bf16[64,1280]{1,0:T(8,128)(2,1)S(1)} %get-tuple-element.91), channel_id=1, source_target_pairs={{0,8},{2,10},{4,12},{6,14},{8,0},{10,2},{12,4},{14,6},{1,9},{3,11}... | collective-permute-start | bytes 491528 | tf_op jit(solution)/shard_map/ppermute | solution.py:379
  9.7 11.2 %collective-permute-start.11 = (bf16[64,1280]{1,0:T(8,128)(2,1)S(1)}, bf16[64,1280]{1,0:T(8,128)(2,1)S(1)}, u32[]{:S(2)}, u32[]{:S(2)}) collective-permute-start(bf16[64,1280]{1,0:T(8,128)(2,1)S(1)} %get-tuple-element.92), channel_id=1, source_target_pairs={{0,6},{2,4},{4,2},{6,0},{8,14},{10,12},{12,10},{14,8},{1,7},{3,5},... | collective-permute-start | bytes 491528 | tf_op jit(solution)/shard_map/ppermute | solution.py:379
  11.4 17.1 %collective-permute-start.12 = (bf16[64,1280]{1,0:T(8,128)(2,1)S(1)}, bf16[64,1280]{1,0:T(8,128)(2,1)S(1)}, u32[]{:S(2)}, u32[]{:S(2)}) collective-permute-start(bf16[64,1280]{1,0:T(8,128)(2,1)S(1)} %get-tuple-element.93), channel_id=1, source_target_pairs={{0,4},{2,6},{4,0},{6,2},{8,12},{10,14},{12,8},{14,10},{1,5},{3,7},... | collective-permute-start | bytes 491528 | tf_op jit(solution)/shard_map/ppermute | solution.py:379
  13.1 17.9 %collective-permute-start.13 = (bf16[64,1280]{1,0:T(8,128)(2,1)S(1)}, bf16[64,1280]{1,0:T(8,128)(2,1)S(1)}, u32[]{:S(2)}, u32[]{:S(2)}) collective-permute-start(bf16[64,1280]{1,0:T(8,128)(2,1)S(1)} %get-tuple-element.94), channel_id=1, source_target_pairs={{0,2},{2,0},{4,6},{6,4},{8,10},{10,8},{12,14},{14,12},{1,3},{3,1},... | collective-permute-start | bytes 491528 | tf_op jit(solution)/shard_map/ppermute | solution.py:379
  14.6 18.2 %collective-permute-start.7 = (bf16[64,1280]{1,0:T(8,128)(2,1)S(1)}, bf16[64,1280]{1,0:T(8,128)(2,1)S(1)}, u32[]{:S(2)}, u32[]{:S(2)}) collective-permute-start(bf16[64,1280]{1,0:T(8,128)(2,1)S(1)} %get-tuple-element.95), channel_id=1, source_target_pairs={{0,14},{2,12},{4,10},{6,8},{8,6},{10,4},{12,2},{14,0},{1,15},{3,13... | collective-permute-start | bytes 491528 | tf_op jit(solution)/shard_map/ppermute | solution.py:379
  19.6 13.5 %collective-permute-start.5 = (bf16[64,1024]{1,0:T(8,128)(2,1)S(1)}, bf16[64,1024]{1,0:T(8,128)(2,1)S(1)}, u32[]{:S(2)}, u32[]{:S(2)}) collective-permute-start(bf16[64,1024]{1,0:T(8,128)(2,1)S(1)} %collective-permute-done.3.refs_4_), channel_id=1, source_target_pairs={{0,4},{2,6},{4,0},{6,2},{8,12},{10,14},{12,8},{14,10},{1,5},{3,7},... | collective-permute-start | bytes 393224 | tf_op jit(solution)/shard_map/ppermute | solution.py:379
  21.0 17.1 %collective-permute-start.8 = (bf16[64,1280]{1,0:T(8,128)(2,1)S(1)}, bf16[64,1280]{1,0:T(8,128)(2,1)S(1)}, u32[]{:S(2)}, u32[]{:S(2)}) collective-permute-start(bf16[64,1280]{1,0:T(8,128)(2,1)S(1)} %get-tuple-element.89), channel_id=1, source_target_pairs={{0,10},{2,8},{4,14},{6,12},{8,2},{10,0},{12,6},{14,4},{1,11},{3,9}... | collective-permute-start | bytes 491528 | tf_op jit(solution)/shard_map/ppermute | solution.py:379
  28.5 11.3 %copy-start = (bf16[1,64,1024]{2,1,0:T(8,128)(2,1)S(1)}, bf16[1,64,1024]{2,1,0:T(8,128)(2,1)}, u32[]{:S(2)}) copy-start(bf16[1,64,1024]{2,1,0:T(8,128)(2,1)} %param.7) | copy-start | bytes 393220
  28.5 9.6 %collective-permute-start.9 = (bf16[64,1280]{1,0:T(8,128)(2,1)S(1)}, bf16[64,1280]{1,0:T(8,128)(2,1)S(1)}, u32[]{:S(2)}, u32[]{:S(2)}) collective-permute-start(bf16[64,1280]{1,0:T(8,128)(2,1)S(1)} %get-tuple-element.90), channel_id=1, source_target_pairs={{0,12},{2,14},{4,8},{6,10},{8,4},{10,6},{12,0},{14,2},{1,13},{3,15... | collective-permute-start | bytes 491528 | tf_op jit(solution)/shard_map/ppermute | solution.py:379
  31.0 7.1 %collective-permute-start.4 = (bf16[64,1024]{1,0:T(8,128)(2,1)S(1)}, bf16[64,1024]{1,0:T(8,128)(2,1)S(1)}, u32[]{:S(2)}, u32[]{:S(2)}) collective-permute-start(bf16[64,1024]{1,0:T(8,128)(2,1)S(1)} %collective-permute-done.3.refs_4_), channel_id=1, source_target_pairs={{0,2},{2,0},{4,6},{6,4},{8,10},{10,8},{12,14},{14,12},{1,3},{3,1},... | collective-permute-start | bytes 393224 | tf_op jit(solution)/shard_map/ppermute | solution.py:379
  32.7 5.6 %collective-permute-start.2 = (bf16[64,1024]{1,0:T(8,128)(2,1)S(1)}, bf16[64,1024]{1,0:T(8,128)(2,1)S(1)}, u32[]{:S(2)}, u32[]{:S(2)}) collective-permute-start(bf16[64,1024]{1,0:T(8,128)(2,1)S(1)} %collective-permute-done.1.refs_2_), channel_id=1, source_target_pairs={{0,2},{2,0},{4,6},{6,4},{8,10},{10,8},{12,14},{14,12},{1,3},{3,1},... | collective-permute-start | bytes 393224 | tf_op jit(solution)/shard_map/ppermute | solution.py:379
  33.0 6.7 %collective-permute-start.6 = (bf16[64,1024]{1,0:T(8,128)(2,1)S(1)}, bf16[64,1024]{1,0:T(8,128)(2,1)S(1)}, u32[]{:S(2)}, u32[]{:S(2)}) collective-permute-start(bf16[64,1024]{1,0:T(8,128)(2,1)S(1)} %collective-permute-done.5.refs_6_), channel_id=1, source_target_pairs={{0,2},{2,0},{4,6},{6,4},{8,10},{10,8},{12,14},{14,12},{1,3},{3,1},... | collective-permute-start | bytes 393224 | tf_op jit(solution)/shard_map/ppermute | solution.py:379
  39.8 20.2 %collective-permute-start.18 = (bf16[512,1024]{1,0:T(8,128)(2,1)S(1)}, bf16[512,1024]{1,0:T(8,128)(2,1)S(1)}, u32[]{:S(2)}, u32[]{:S(2)}) collective-permute-start(bf16[512,1024]{1,0:T(8,128)(2,1)S(1)} %stack_kernel.1), channel_id=1, source_target_pairs={{0,1},{1,0},{2,3},{3,2},{4,5},{5,4},{6,7},{7,6},{8,9},{9,8},{10,11... | collective-permute-start | bytes 3145736 | tf_op jit(solution)/shard_map/ppermute | solution.py:382
  40.6 2.0 %collective-permute-start.14 = (bf16[32,1024]{1,0:T(8,128)(2,1)S(1)}, bf16[32,1024]{1,0:T(8,128)(2,1)S(1)}, u32[]{:S(2)}, u32[]{:S(2)}) collective-permute-start(bf16[32,1024]{1,0:T(8,128)(2,1)S(1)} %get-tuple-element.57), channel_id=1, source_target_pairs={{0,1},{1,0},{2,3},{3,2},{4,5},{5,4},{6,7},{7,6},{8,9},{9,8},{10,11... | collective-permute-start | bytes 196616 | tf_op jit(solution)/shard_map/ppermute | solution.py:382
  43.9 9.2 %collective-permute-start.19 = (bf16[128,1024]{1,0:T(8,128)(2,1)S(1)}, bf16[128,1024]{1,0:T(8,128)(2,1)S(1)}, u32[]{:S(2)}, u32[]{:S(2)}) collective-permute-start(bf16[128,1024]{1,0:T(8,128)(2,1)S(1)} %get-tuple-element.82), channel_id=1, source_target_pairs={{0,2},{2,0},{4,6},{6,4},{8,10},{10,8},{12,14},{14,12},{1,3},{3,1},... | collective-permute-start | bytes 786440 | tf_op jit(solution)/shard_map/ppermute | solution.py:379
  46.6 13.4 %collective-permute-start.17 = (bf16[512,512]{1,0:T(8,128)(2,1)S(1)}, bf16[512,512]{1,0:T(8,128)(2,1)S(1)}, u32[]{:S(2)}, u32[]{:S(2)}) collective-permute-start(bf16[512,512]{1,0:T(8,128)(2,1)S(1)} %get-tuple-element.78), channel_id=1, source_target_pairs={{0,1},{1,0},{2,3},{3,2},{4,5},{5,4},{6,7},{7,6},{8,9},{9,8},{10,11... | collective-permute-start | bytes 1572872 | tf_op jit(solution)/shard_map/ppermute | solution.py:382
  47.1 10.8 %collective-permute-start.15 = (bf16[128,1024]{1,0:T(8,128)(2,1)S(1)}, bf16[128,1024]{1,0:T(8,128)(2,1)S(1)}, u32[]{:S(2)}, u32[]{:S(2)}) collective-permute-start(bf16[128,1024]{1,0:T(8,128)(2,1)S(1)} %get-tuple-element.65), channel_id=1, source_target_pairs={{0,2},{2,0},{4,6},{6,4},{8,10},{10,8},{12,14},{14,12},{1,3},{3,1},... | collective-permute-start | bytes 786440 | tf_op jit(solution)/shard_map/ppermute | solution.py:379
  53.8 12.7 %collective-permute-start.20 = (bf16[64,1024]{1,0:T(8,128)(2,1)S(1)}, bf16[64,1024]{1,0:T(8,128)(2,1)S(1)}, u32[]{:S(2)}, u32[]{:S(2)}) collective-permute-start(bf16[64,1024]{1,0:T(8,128)(2,1)S(1)} %get-tuple-element.83), channel_id=1, source_target_pairs={{0,8},{2,10},{4,12},{6,14},{8,0},{10,2},{12,4},{14,6},{1,9},{3,11}... | collective-permute-start | bytes 393224 | tf_op jit(solution)/shard_map/ppermute | solution.py:379
  56.5 10.0 %collective-permute-start.21 = (bf16[64,1024]{1,0:T(8,128)(2,1)S(1)}, bf16[64,1024]{1,0:T(8,128)(2,1)S(1)}, u32[]{:S(2)}, u32[]{:S(2)}) collective-permute-start(bf16[64,1024]{1,0:T(8,128)(2,1)S(1)} %get-tuple-element.84), channel_id=1, source_target_pairs={{0,12},{2,14},{4,8},{6,10},{8,4},{10,6},{12,0},{14,2},{1,13},{3,15... | collective-permute-start | bytes 393224 | tf_op jit(solution)/shard_map/ppermute | solution.py:379
  58.6 7.9 %collective-permute-start.16 = (bf16[64,1024]{1,0:T(8,128)(2,1)S(1)}, bf16[64,1024]{1,0:T(8,128)(2,1)S(1)}, u32[]{:S(2)}, u32[]{:S(2)}) collective-permute-start(bf16[64,1024]{1,0:T(8,128)(2,1)S(1)} %get-tuple-element.68), channel_id=1, source_target_pairs={{0,4},{2,6},{4,0},{6,2},{8,12},{10,14},{12,8},{14,10},{1,5},{3,7},... | collective-permute-start | bytes 393224 | tf_op jit(solution)/shard_map/ppermute | solution.py:379

commit v7 on v6

--- a/solution.py
+++ b/solution.py
@@ -409,10 +409,10 @@
     mats = matrix_call(place, query_kernel, support_kernel, count, columns, edge)
     here = lax.dynamic_slice(query_feats, (side * tile, 0), (tile, width))
     there = lax.dynamic_slice(query_feats, ((side ^ 1) * tile, 0), (tile, width))
-    ordered = held + [pieces[k] for k in [7, 5, 6, 4, 3, 2, 1, 0]]
+    ordered = held + [pieces[k] for k in [7, 5, 6, 4, 3, 1, 2, 0]]
     ordered, mats, here, there = lax.optimization_barrier((ordered, mats, here, there))
     held, landed = ordered[:count], ordered[count:]
-    for at, k in enumerate([7, 5, 6, 4, 3, 2, 1, 0]):
+    for at, k in enumerate([7, 5, 6, 4, 3, 1, 2, 0]):
         pieces[k] = landed[at]
     cells, rim = gather_call(place, pieces, tile, edge)
     rim = swapped(rim)

time: 67.5 us -> 67.1 us (level)
  starting transfers between devices: 32.1 us -> 30.3 us
  waiting for transfers between devices: 19 us -> 20.5 us
    ppermute x19, starting transfers between devices: 31.4 us -> 29.6 us  [exchanged(): lax.ppermute(value, ('blk', 'sub'), [(i, i ^ mask) for i in range(count)])]
    ppermute x19, waiting for transfers between devices: 18.8 us -> 20.3 us  [exchanged(): lax.ppermute(value, ('blk', 'sub'), [(i, i ^ mask) for i in range(count)])]
where the time goes in v7:
time: 67.1 us; the launch traced here: 66.9 us
  starting transfers between devices  30.3 us (45%)
  waiting for transfers between devices  20.5 us (31%)
  Pallas kernels  7.05 us (11%)
  local copies, waits for them, and re-layouts  4.28 us (6%)
  matrix products  3.19 us (5%)
  other arithmetic  0.86 us (1%)
  between operations  0.79 us (1%)
    ppermute x19, starting transfers between devices, exchanged(): lax.ppermute(value, ('blk', 'sub'), [(i, i ^ mask) for i in range(count)])  29.6 us
    ppermute x19, waiting for transfers between devices, exchanged(): lax.ppermute(value, ('blk', 'sub'), [(i, i ^ mask) for i in range(count)])  20.3 us
    dot_general x4, matrix products, query_term(): lax.dot_general(block, feats, (((0,), (0,)), ((), ())), preferred_element...  3.19 us
    dynamic_slice x1, local copies, waits for them, and re-layouts, tile_shards(): lax.dynamic_slice(query_feats, ((side ^ 1) * tile, 0), (tile, width))  2.66 us
    pallas_call x2, Pallas kernels, corr_call(): pl.pallas_call(lambda *refs: corr_kernel(group, columns, tile, *refs), ou...  2.37 us
    dynamic_slice x1, local copies, waits for them, and re-layouts, piece(): lax.dynamic_slice(volume, (0, (own ^ mask) * tile), (columns, tile + 2 *...  1.52 us
    pallas_call x2, Pallas kernels, partial_call(): pl.pallas_call(lambda *refs: partial_kernel(columns, *refs), out_shape=[j...  1.47 us
  transfers between devices with their start and end apart: 22, of which 10 were waited for; matrix products, arithmetic and copies ran while one was open for 11% of the time, Pallas kernels for 10%

profile of v7, /device:TPU:0, one launch (start us, length us, event | category | flops | bytes accessed | tf_op | source)
XLA Modules:
  0.0 66.9 jit_solution(15765124507724152726)
XLA Ops:
  0.6 4.1 %collective-permute-start.3 = (bf16[64,1024]{1,0:T(8,128)(2,1)}, bf16[64,1024]{1,0:T(8,128)(2,1)S(1)}, u32[]{:S(2)}, u32[]{:S(2)}) collective-permute-start(bf16[64,1024]{1,0:T(8,128)(2,1)} %bitcast.14), channel_id=1, source_target_pairs={{0,8},{2,10},{4,12},{6,14},{8,0},{10,2},{12,4},{14,6},{1,9},{3,11}... | collective-permute-start | bytes 393224 | tf_op jit(solution)/shard_map/ppermute | solution.py:379
  4.8 1.6 %collective-permute-start.1 = (bf16[64,1024]{1,0:T(8,128)(2,1)}, bf16[64,1024]{1,0:T(8,128)(2,1)S(1)}, u32[]{:S(2)}, u32[]{:S(2)}) collective-permute-start(bf16[64,1024]{1,0:T(8,128)(2,1)} %bitcast.15), channel_id=1, source_target_pairs={{0,4},{2,6},{4,0},{6,2},{8,12},{10,14},{12,8},{14,10},{1,5},{3,7},... | collective-permute-start | bytes 393224 | tf_op jit(solution)/shard_map/ppermute | solution.py:379
  6.3 1.5 %collective-permute-start = (bf16[64,1024]{1,0:T(8,128)(2,1)}, bf16[64,1024]{1,0:T(8,128)(2,1)S(1)}, u32[]{:S(2)}, u32[]{:S(2)}) collective-permute-start(bf16[64,1024]{1,0:T(8,128)(2,1)} %bitcast.16), channel_id=1, source_target_pairs={{0,2},{2,0},{4,6},{6,4},{8,10},{10,8},{12,14},{14,12},{1,3},{3,1},... | collective-permute-start | bytes 393224 | tf_op jit(solution)/shard_map/ppermute | solution.py:379
  7.8 1.5 %pad_dynamic-slice_fusion = (bf16[64,1280]{1,0:T(8,128)(2,1)S(1)}, bf16[64,1280]{1,0:T(8,128)(2,1)S(1)}, bf16[64,1280]{1,0:T(8,128)(2,1)S(1)}, bf16[64,1280]{1,0...) fusion(s32[]{:T(128)S(6)} %select_n.37, ...), kind=kLoop, calls=%fused_computation.8 | loop fusion | bytes 2359328 | tf_op jit(solution)/shard_map/dynamic_slice | solution.py:387
  9.3 0.4 collective-permute-start.10
  9.7 0.2 collective-permute-start.11
  9.9 1.4 %collective-permute-done.3.refs_4_ = bf16[64,1024]{1,0:T(8,128)(2,1)S(1)} collective-permute-done((bf16[64,1024]{1,0:T(8,128)(2,1)}, bf16[64,1024]{1,0:T(8,128)(2,1)S(1)}, u32[]{:S(2)}, u32[]{:S(2)}) %collective-permute-start.3) | collective-permute-done | bytes 131104 | tf_op jit(solution)/shard_map/ppermute | solution.py:379
  11.4 2.1 %collective-permute-start.12 = (bf16[64,1280]{1,0:T(8,128)(2,1)S(1)}, bf16[64,1280]{1,0:T(8,128)(2,1)S(1)}, u32[]{:S(2)}, u32[]{:S(2)}) collective-permute-start(bf16[64,1280]{1,0:T(8,128)(2,1)S(1)} %get-tuple-element.93), channel_id=1, source_target_pairs={{0,2},{2,0},{4,6},{6,4},{8,10},{10,8},{12,14},{14,12},{1,3},{3,1},... | collective-permute-start | bytes 491528 | tf_op jit(solution)/shard_map/ppermute | solution.py:379
  13.5 1.1 %collective-permute-start.13 = (bf16[64,1280]{1,0:T(8,128)(2,1)S(1)}, bf16[64,1280]{1,0:T(8,128)(2,1)S(1)}, u32[]{:S(2)}, u32[]{:S(2)}) collective-permute-start(bf16[64,1280]{1,0:T(8,128)(2,1)S(1)} %get-tuple-element.94), channel_id=1, source_target_pairs={{0,4},{2,6},{4,0},{6,2},{8,12},{10,14},{12,8},{14,10},{1,5},{3,7},... | collective-permute-start | bytes 491528 | tf_op jit(solution)/shard_map/ppermute | solution.py:379
  14.6 3.0 %collective-permute-start.7 = (bf16[64,1280]{1,0:T(8,128)(2,1)S(1)}, bf16[64,1280]{1,0:T(8,128)(2,1)S(1)}, u32[]{:S(2)}, u32[]{:S(2)}) collective-permute-start(bf16[64,1280]{1,0:T(8,128)(2,1)S(1)} %get-tuple-element.95), channel_id=1, source_target_pairs={{0,14},{2,12},{4,10},{6,8},{8,6},{10,4},{12,2},{14,0},{1,15},{3,13... | collective-permute-start | bytes 491528 | tf_op jit(solution)/shard_map/ppermute | solution.py:379
  17.6 2.0 %collective-permute-done.10.refs_4_ = bf16[64,1280]{1,0:T(8,128)(2,1)S(1)} collective-permute-done((bf16[64,1280]{1,0:T(8,128)(2,1)S(1)}, bf16[64,1280]{1,0:T(8,128)(2,1)S(1)}, u32[]{:S(2)}, u32[]{:S(2)}) %collective-permute-start.10) | collective-permute-done | bytes 163872 | tf_op jit(solution)/shard_map/ppermute | solution.py:379
  19.6 0.1 reshape.7.refs_1_
  19.7 0.1 pad_add_fusion.refs_0_
  19.8 1.2 %matrix_kernel.1 = (bf16[256,256]{1,0:T(8,128)(2,1)S(1)}, bf16[512,32]{1,0:T(8,128)(2,1)S(1)}, bf16[512,256]{1,0:T(8,128)(2,1)S(1)}, bf16[512,256]{1,0:T(8,128)(2,1)S(1)}) custom-call(s32[2]{0:T(128)S(1)} %pad_add_fusion.refs_0_, f32[36]{0:T(128)S(1)} %reshape.7.refs_1_), custom_call_target="tpu_custom_call" | custom-call | flops 2621440 | bytes 524288 | tf_op jit(solution)/shard_map/matrix_kernel/pallas_call | solution.py:171
  20.9 0.0 collective-permute-done.11.refs_5_
  21.0 3.9 %collective-permute-start.8 = (bf16[64,1280]{1,0:T(8,128)(2,1)S(1)}, bf16[64,1280]{1,0:T(8,128)(2,1)S(1)}, u32[]{:S(2)}, u32[]{:S(2)}) collective-permute-start(bf16[64,1280]{1,0:T(8,128)(2,1)S(1)} %get-tuple-element.89), channel_id=1, source_target_pairs={{0,10},{2,8},{4,14},{6,12},{8,2},{10,0},{12,6},{14,4},{1,11},{3,9}... | collective-permute-start | bytes 491528 | tf_op jit(solution)/shard_map/ppermute | solution.py:379
  24.9 1.0 %collective-permute-start.9 = (bf16[64,1280]{1,0:T(8,128)(2,1)S(1)}, bf16[64,1280]{1,0:T(8,128)(2,1)S(1)}, u32[]{:S(2)}, u32[]{:S(2)}) collective-permute-start(bf16[64,1280]{1,0:T(8,128)(2,1)S(1)} %get-tuple-element.90), channel_id=1, source_target_pairs={{0,12},{2,14},{4,8},{6,10},{8,4},{10,6},{12,0},{14,2},{1,13},{3,15... | collective-permute-start | bytes 491528 | tf_op jit(solution)/shard_map/ppermute | solution.py:379
  25.9 1.7 %collective-permute-done.13.refs_6_ = bf16[64,1280]{1,0:T(8,128)(2,1)S(1)} collective-permute-done((bf16[64,1280]{1,0:T(8,128)(2,1)S(1)}, bf16[64,1280]{1,0:T(8,128)(2,1)S(1)}, u32[]{:S(2)}, u32[]{:S(2)}) %collective-permute-start.13) | collective-permute-done | bytes 163872 | tf_op jit(solution)/shard_map/ppermute | solution.py:379
  27.7 1.0 %collective-permute-done.7.refs_1_ = bf16[64,1280]{1,0:T(8,128)(2,1)S(1)} collective-permute-done((bf16[64,1280]{1,0:T(8,128)(2,1)S(1)}, bf16[64,1280]{1,0:T(8,128)(2,1)S(1)}, u32[]{:S(2)}, u32[]{:S(2)}) %collective-permute-start.7) | collective-permute-done | bytes 163872 | tf_op jit(solution)/shard_map/ppermute | solution.py:379
  28.7 1.0 %collective-permute-start.2 = (bf16[64,1024]{1,0:T(8,128)(2,1)S(1)}, bf16[64,1024]{1,0:T(8,128)(2,1)S(1)}, u32[]{:S(2)}, u32[]{:S(2)}) collective-permute-start(bf16[64,1024]{1,0:T(8,128)(2,1)S(1)} %collective-permute-done.1.refs_2_), channel_id=1, source_target_pairs={{0,2},{2,0},{4,6},{6,4},{8,10},{10,8},{12,14},{14,12},{1,3},{3,1},... | collective-permute-start | bytes 393224 | tf_op jit(solution)/shard_map/ppermute | solution.py:379
  29.7 1.5 %collective-permute-done.5.refs_6_ = bf16[64,1024]{1,0:T(8,128)(2,1)S(1)} collective-permute-done((bf16[64,1024]{1,0:T(8,128)(2,1)S(1)}, bf16[64,1024]{1,0:T(8,128)(2,1)S(1)}, u32[]{:S(2)}, u32[]{:S(2)}) %collective-permute-start.5) | collective-permute-done | bytes 131104 | tf_op jit(solution)/shard_map/ppermute | solution.py:379
  31.2 1.6 %collective-permute-start.6 = (bf16[64,1024]{1,0:T(8,128)(2,1)S(1)}, bf16[64,1024]{1,0:T(8,128)(2,1)S(1)}, u32[]{:S(2)}, u32[]{:S(2)}) collective-permute-start(bf16[64,1024]{1,0:T(8,128)(2,1)S(1)} %collective-permute-done.5.refs_6_), channel_id=1, source_target_pairs={{0,2},{2,0},{4,6},{6,4},{8,10},{10,8},{12,14},{14,12},{1,3},{3,1},... | collective-permute-start | bytes 393224 | tf_op jit(solution)/shard_map/ppermute | solution.py:379
  32.8 2.7 %constant_dynamic-slice_fusion = (bf16[1024,1024]{1,0:T(8,128)(2,1)S(1)}, bf16[1024,1024]{1,0:T(8,128)(2,1)S(1)}) fusion(bf16[2048,1024]{1,0:T(8,128)(2,1)} %param.6, s32[]{:T(128)S(6)} %select_n.39, s32[]{:T(128)S(6)} %select_n.38), kind=kLoop, calls=%fused_computation.26 | loop fusion | bytes 8388616 | tf_op jit(solution)/shard_map/dynamic_slice | solution.py:411
  35.5 2.6 %collective-permute-done.8.refs_3_ = bf16[64,1280]{1,0:T(8,128)(2,1)S(1)} collective-permute-done((bf16[64,1280]{1,0:T(8,128)(2,1)S(1)}, bf16[64,1280]{1,0:T(8,128)(2,1)S(1)}, u32[]{:S(2)}, u32[]{:S(2)}) %collective-permute-start.8) | collective-permute-done | bytes 163872 | tf_op jit(solution)/shard_map/ppermute | solution.py:379
  38.1 1.3 %collective-permute-done.6.refs_7_ = bf16[64,1024]{1,0:T(8,128)(2,1)S(1)} collective-permute-done((bf16[64,1024]{1,0:T(8,128)(2,1)S(1)}, bf16[64,1024]{1,0:T(8,128)(2,1)S(1)}, u32[]{:S(2)}, u32[]{:S(2)}) %collective-permute-start.6) | collective-permute-done | bytes 131104 | tf_op jit(solution)/shard_map/ppermute | solution.py:379
  39.5 0.1 stack_kernel.1
  39.5 0.1 collective-permute-start.18
  39.6 0.7 %gather_kernel.1 = (bf16[640,1280]{1,0:T(8,128)(2,1)S(1)}, bf16[32,1024]{1,0:T(8,128)(2,1)S(1)}) custom-call(s32[2]{0:T(128)S(1)} %pad_add_fusion.refs_0_, bf16[64,1280]{1,0:T(8,128)(2,1)S(1)} %collective-permute-done.7.refs_1_, bf16[64,1280]{1,0:T(8,128)(2,1)S(1)} %collective-permute-done.9.refs_2_, bf16[64,1280]{1,0:T(8,128)(2,1)S(1)} %collective-permute-done.8.refs_3_, ...), custom_call_target="tpu_custom_call" | custom-call | flops 8192 | bytes 2621440 | tf_op jit(solution)/shard_map/gather_kernel/pallas_call | solution.py:209
  40.4 0.6 collective-permute-start.14
  40.9 1.3 %query_kernel.1.refs_5_ = f32[512,1024]{1,0:T(8,128)S(1)} custom-call(bf16[640,1280]{1,0:T(8,128)(2,1)S(1)} %get-tuple-element.56.refs_0_.refs_1_, bf16[512,256]{1,0:T(8,128)(2,1)S(1)} %get-tuple-element.60.refs_1_, bf16[512,256]{1,0:T(8,128)(2,1)S(1)} %get-tuple-element.61.refs_2_), custom_call_target="tpu_custom_call" | custom-call | flops 1073741824 | bytes 4194304 | tf_op jit(solution)/shard_map/query_kernel/pallas_call | solution.py:241
  42.2 0.2 collective-permute-done.14.refs_2_
  42.4 1.2 %corr_kernel.2 = (bf16[128,1024]{1,0:T(8,128)(2,1)S(1)}, bf16[128,1024]{1,0:T(8,128)(2,1)S(1)}, bf16[256,512]{1,0:T(8,128)(2,1)S(1)}, bf16[256,512]{1,0:T(8,128)(2,1)S(1)}) custom-call(s32[2]{0:T(128)S(1)} %pad_add_fusion.refs_0_, bf16[640,1280]{1,0:T(8,128)(2,1)S(1)} %get-tuple-element.56.refs_0_.refs_1_, ...), custom_call_target="tpu_custom_call" | custom-call | flops 268435456 | bytes 2097152 | tf_op jit(solution)/shard_map/corr_kernel/pallas_call | solution.py:299
  43.6 0.5 collective-permute-start.19
  44.1 1.2 %corr_kernel.3 = (bf16[128,1024]{1,0:T(8,128)(2,1)S(1)}, bf16[128,1024]{1,0:T(8,128)(2,1)S(1)}, bf16[512,512]{1,0:T(8,128)(2,1)S(1)}, bf16[512,512]{1,0:T(8,128)(2,1)S(1)}) custom-call(s32[2]{0:T(128)S(1)} %pad_add_fusion.refs_0_, bf16[640,1280]{1,0:T(8,128)(2,1)S(1)} %get-tuple-element.56.refs_0_.refs_1_, ...), custom_call_target="tpu_custom_call" | custom-call | flops 268435456 | bytes 2097152 | tf_op jit(solution)/shard_map/corr_kernel/pallas_call | solution.py:299
  45.3 0.1 collective-permute-start.17
  45.4 0.5 fusion.3
  45.8 1.6 %collective-permute-start.15 = (bf16[128,1024]{1,0:T(8,128)(2,1)S(1)}, bf16[128,1024]{1,0:T(8,128)(2,1)S(1)}, u32[]{:S(2)}, u32[]{:S(2)}) collective-permute-start(bf16[128,1024]{1,0:T(8,128)(2,1)S(1)} %get-tuple-element.65), channel_id=1, source_target_pairs={{0,2},{2,0},{4,6},{6,4},{8,10},{10,8},{12,14},{14,12},{1,3},{3,1},... | collective-permute-start | bytes 786440 | tf_op jit(solution)/shard_map/ppermute | solution.py:379
  47.5 0.5 fusion.5
  47.9 4.9 %collective-permute-done.19.refs_1_ = bf16[128,1024]{1,0:T(8,128)(2,1)S(1)} collective-permute-done((bf16[128,1024]{1,0:T(8,128)(2,1)S(1)}, bf16[128,1024]{1,0:T(8,128)(2,1)S(1)}, u32[]{:S(2)}, u32[]{:S(2)}) %collective-permute-start.19) | collective-permute-done | bytes 262176 | tf_op jit(solution)/shard_map/ppermute | solution.py:379
  52.8 0.7 %partial_kernel.3 = (bf16[64,1024]{1,0:T(8,128)(2,1)S(1)}, bf16[64,1024]{1,0:T(8,128)(2,1)S(1)}) custom-call(bf16[128,1024]{1,0:T(8,128)(2,1)S(1)} %get-tuple-element.81.refs_0_, bf16[128,1024]{1,0:T(8,128)(2,1)S(1)} %collective-permute-done.19.refs_1_, bf16[1024,1024]{1,0:T(8,128)(2,1)S(1)} %get-tuple-element.66.refs_2_, ...), custom_call_target="tpu_custom_call" | custom-call | flops 536870912 | bytes 4194304 | tf_op jit(solution)/shard_map/partial_kernel/pallas_call | solution.py:330
  53.5 2.8 %collective-permute-start.20 = (bf16[64,1024]{1,0:T(8,128)(2,1)S(1)}, bf16[64,1024]{1,0:T(8,128)(2,1)S(1)}, u32[]{:S(2)}, u32[]{:S(2)}) collective-permute-start(bf16[64,1024]{1,0:T(8,128)(2,1)S(1)} %get-tuple-element.83), channel_id=1, source_target_pairs={{0,8},{2,10},{4,12},{6,14},{8,0},{10,2},{12,4},{14,6},{1,9},{3,11}... | collective-permute-start | bytes 393224 | tf_op jit(solution)/shard_map/ppermute | solution.py:379
  56.3 1.3 %collective-permute-start.21 = (bf16[64,1024]{1,0:T(8,128)(2,1)S(1)}, bf16[64,1024]{1,0:T(8,128)(2,1)S(1)}, u32[]{:S(2)}, u32[]{:S(2)}) collective-permute-start(bf16[64,1024]{1,0:T(8,128)(2,1)S(1)} %get-tuple-element.84), channel_id=1, source_target_pairs={{0,12},{2,14},{4,8},{6,10},{8,4},{10,6},{12,0},{14,2},{1,13},{3,15... | collective-permute-start | bytes 393224 | tf_op jit(solution)/shard_map/ppermute | solution.py:379
  57.6 0.7 %partial_kernel.2 = (f32[64,1024]{1,0:T(8,128)S(1)}, bf16[64,1024]{1,0:T(8,128)(2,1)S(1)}) custom-call(bf16[128,1024]{1,0:T(8,128)(2,1)S(1)} %get-tuple-element.64.refs_0_, bf16[128,1024]{1,0:T(8,128)(2,1)S(1)} %collective-permute-done.15.refs_1_, bf16[1024,1024]{1,0:T(8,128)(2,1)S(1)} %get-tuple-element.66.refs_2_, ...), custom_call_target="tpu_custom_call" | custom-call | flops 536870912 | bytes 4194304 | tf_op jit(solution)/shard_map/partial_kernel/pallas_call | solution.py:330
  58.4 1.7 %collective-permute-start.16 = (bf16[64,1024]{1,0:T(8,128)(2,1)S(1)}, bf16[64,1024]{1,0:T(8,128)(2,1)S(1)}, u32[]{:S(2)}, u32[]{:S(2)}) collective-permute-start(bf16[64,1024]{1,0:T(8,128)(2,1)S(1)} %get-tuple-element.68), channel_id=1, source_target_pairs={{0,4},{2,6},{4,0},{6,2},{8,12},{10,14},{12,8},{14,10},{1,5},{3,7},... | collective-permute-start | bytes 393224 | tf_op jit(solution)/shard_map/ppermute | solution.py:379
  60.1 0.5 fusion
  60.5 1.8 %add_multiply_fusion = f32[512,1024]{1,0:T(8,128)} fusion(f32[512,1024]{1,0:T(8,128)S(1)} %fusion, f32[512,1024]{1,0:T(8,128)S(1)} %fusion.5, f32[512,1024]{1,0:T(8,128)S(1)} %fusion.3, bf16[512,1024]{1,0:T(8,128)(2,1)S(1)} %collective-permute-done.18, bf16[512,512]{1,0:T(8,128)(2,1)S(1)} %collective-permute-done.17), kind=kOutput, calls=%fused_computation | convolution fusion | flops 270532608 | bytes 9175040 | tf_op jit(solution)/shard_map/dot_general | solution.py:434
  62.4 3.8 %collective-permute-done.16 = bf16[64,1024]{1,0:T(8,128)(2,1)S(1)} collective-permute-done((bf16[64,1024]{1,0:T(8,128)(2,1)S(1)}, bf16[64,1024]{1,0:T(8,128)(2,1)S(1)}, u32[]{:S(2)}, u32[]{:S(2)}) %collective-permute-start.16) | collective-permute-done | bytes 131104 | tf_op jit(solution)/shard_map/ppermute | solution.py:379
  66.2 0.8 %multiply_bitcast_fusion = f32[1,64,1024]{2,1,0:T(8,128)} fusion(bf16[64,1024]{1,0:T(8,128)(2,1)S(1)} %collective-permute-done.16, bf16[64,1024]{1,0:T(8,128)(2,1)S(1)} %collective-permute-done.21, f32[64,1024]{1,0:T(8,128)S(1)} %get-tuple-element.80, bf16[64,1024]{1,0:T(8,128)(2,1)S(1)} %collective-permute-done.20), kind=kLoop, calls=%fused_computation.18 | loop fusion | flops 458752 | bytes 917504 | tf_op jit(solution)/shard_map/broadcast_in_dim | solution.py:446
  (21 shorter events, 0.1 us)
Async XLA Ops:
  0.6 9.3 %copy-start.2 = (f32[3,3]{1,0:T(4,128)S(1)}, f32[3,3]{1,0:T(4,128)}, u32[]{:S(2)}) copy-start(f32[3,3]{1,0:T(4,128)} %param.8) | copy-start | bytes 112
  0.6 9.3 %copy-start.1 = (f32[3,3]{1,0:T(4,128)S(1)}, f32[3,3]{1,0:T(4,128)}, u32[]{:S(2)}) copy-start(f32[3,3]{1,0:T(4,128)} %param.9) | copy-start | bytes 112
  0.6 10.7 %collective-permute-start.3 = (bf16[64,1024]{1,0:T(8,128)(2,1)}, bf16[64,1024]{1,0:T(8,128)(2,1)S(1)}, u32[]{:S(2)}, u32[]{:S(2)}) collective-permute-start(bf16[64,1024]{1,0:T(8,128)(2,1)} %bitcast.14), channel_id=1, source_target_pairs={{0,8},{2,10},{4,12},{6,14},{8,0},{10,2},{12,4},{14,6},{1,9},{3,11}... | collective-permute-start | bytes 393224 | tf_op jit(solution)/shard_map/ppermute | solution.py:379
  4.8 8.7 %collective-permute-start.1 = (bf16[64,1024]{1,0:T(8,128)(2,1)}, bf16[64,1024]{1,0:T(8,128)(2,1)S(1)}, u32[]{:S(2)}, u32[]{:S(2)}) collective-permute-start(bf16[64,1024]{1,0:T(8,128)(2,1)} %bitcast.15), channel_id=1, source_target_pairs={{0,4},{2,6},{4,0},{6,2},{8,12},{10,14},{12,8},{14,10},{1,5},{3,7},... | collective-permute-start | bytes 393224 | tf_op jit(solution)/shard_map/ppermute | solution.py:379
  6.3 8.3 %collective-permute-start = (bf16[64,1024]{1,0:T(8,128)(2,1)}, bf16[64,1024]{1,0:T(8,128)(2,1)S(1)}, u32[]{:S(2)}, u32[]{:S(2)}) collective-permute-start(bf16[64,1024]{1,0:T(8,128)(2,1)} %bitcast.16), channel_id=1, source_target_pairs={{0,2},{2,0},{4,6},{6,4},{8,10},{10,8},{12,14},{14,12},{1,3},{3,1},... | collective-permute-start | bytes 393224 | tf_op jit(solution)/shard_map/ppermute | solution.py:379
  9.3 10.2 %collective-permute-start.10 = (bf16[64,1280]{1,0:T(8,128)(2,1)S(1)}, bf16[64,1280]{1,0:T(8,128)(2,1)S(1)}, u32[]{:S(2)}, u32[]{:S(2)}) collective-permute-start(bf16[64,1280]{1,0:T(8,128)(2,1)S(1)} %get-tuple-element.91), channel_id=1, source_target_pairs={{0,8},{2,10},{4,12},{6,14},{8,0},{10,2},{12,4},{14,6},{1,9},{3,11}... | collective-permute-start | bytes 491528 | tf_op jit(solution)/shard_map/ppermute | solution.py:379
  9.7 11.2 %collective-permute-start.11 = (bf16[64,1280]{1,0:T(8,128)(2,1)S(1)}, bf16[64,1280]{1,0:T(8,128)(2,1)S(1)}, u32[]{:S(2)}, u32[]{:S(2)}) collective-permute-start(bf16[64,1280]{1,0:T(8,128)(2,1)S(1)} %get-tuple-element.92), channel_id=1, source_target_pairs={{0,6},{2,4},{4,2},{6,0},{8,14},{10,12},{12,10},{14,8},{1,7},{3,5},... | collective-permute-start | bytes 491528 | tf_op jit(solution)/shard_map/ppermute | solution.py:379
  11.4 13.5 %collective-permute-start.12 = (bf16[64,1280]{1,0:T(8,128)(2,1)S(1)}, bf16[64,1280]{1,0:T(8,128)(2,1)S(1)}, u32[]{:S(2)}, u32[]{:S(2)}) collective-permute-start(bf16[64,1280]{1,0:T(8,128)(2,1)S(1)} %get-tuple-element.93), channel_id=1, source_target_pairs={{0,2},{2,0},{4,6},{6,4},{8,10},{10,8},{12,14},{14,12},{1,3},{3,1},... | collective-permute-start | bytes 491528 | tf_op jit(solution)/shard_map/ppermute | solution.py:379
  13.5 14.2 %collective-permute-start.13 = (bf16[64,1280]{1,0:T(8,128)(2,1)S(1)}, bf16[64,1280]{1,0:T(8,128)(2,1)S(1)}, u32[]{:S(2)}, u32[]{:S(2)}) collective-permute-start(bf16[64,1280]{1,0:T(8,128)(2,1)S(1)} %get-tuple-element.94), channel_id=1, source_target_pairs={{0,4},{2,6},{4,0},{6,2},{8,12},{10,14},{12,8},{14,10},{1,5},{3,7},... | collective-permute-start | bytes 491528 | tf_op jit(solution)/shard_map/ppermute | solution.py:379
  14.6 14.1 %collective-permute-start.7 = (bf16[64,1280]{1,0:T(8,128)(2,1)S(1)}, bf16[64,1280]{1,0:T(8,128)(2,1)S(1)}, u32[]{:S(2)}, u32[]{:S(2)}) collective-permute-start(bf16[64,1280]{1,0:T(8,128)(2,1)S(1)} %get-tuple-element.95), channel_id=1, source_target_pairs={{0,14},{2,12},{4,10},{6,8},{8,6},{10,4},{12,2},{14,0},{1,15},{3,13... | collective-permute-start | bytes 491528 | tf_op jit(solution)/shard_map/ppermute | solution.py:379
  19.6 11.6 %collective-permute-start.5 = (bf16[64,1024]{1,0:T(8,128)(2,1)S(1)}, bf16[64,1024]{1,0:T(8,128)(2,1)S(1)}, u32[]{:S(2)}, u32[]{:S(2)}) collective-permute-start(bf16[64,1024]{1,0:T(8,128)(2,1)S(1)} %collective-permute-done.3.refs_4_), channel_id=1, source_target_pairs={{0,4},{2,6},{4,0},{6,2},{8,12},{10,14},{12,8},{14,10},{1,5},{3,7},... | collective-permute-start | bytes 393224 | tf_op jit(solution)/shard_map/ppermute | solution.py:379
  21.0 17.2 %collective-permute-start.8 = (bf16[64,1280]{1,0:T(8,128)(2,1)S(1)}, bf16[64,1280]{1,0:T(8,128)(2,1)S(1)}, u32[]{:S(2)}, u32[]{:S(2)}) collective-permute-start(bf16[64,1280]{1,0:T(8,128)(2,1)S(1)} %get-tuple-element.89), channel_id=1, source_target_pairs={{0,10},{2,8},{4,14},{6,12},{8,2},{10,0},{12,6},{14,4},{1,11},{3,9}... | collective-permute-start | bytes 491528 | tf_op jit(solution)/shard_map/ppermute | solution.py:379
  24.9 14.6 %copy-start = (bf16[1,64,1024]{2,1,0:T(8,128)(2,1)S(1)}, bf16[1,64,1024]{2,1,0:T(8,128)(2,1)}, u32[]{:S(2)}) copy-start(bf16[1,64,1024]{2,1,0:T(8,128)(2,1)} %param.7) | copy-start | bytes 393220
  24.9 13.2 %collective-permute-start.9 = (bf16[64,1280]{1,0:T(8,128)(2,1)S(1)}, bf16[64,1280]{1,0:T(8,128)(2,1)S(1)}, u32[]{:S(2)}, u32[]{:S(2)}) collective-permute-start(bf16[64,1280]{1,0:T(8,128)(2,1)S(1)} %get-tuple-element.90), channel_id=1, source_target_pairs={{0,12},{2,14},{4,8},{6,10},{8,4},{10,6},{12,0},{14,2},{1,13},{3,15... | collective-permute-start | bytes 491528 | tf_op jit(solution)/shard_map/ppermute | solution.py:379
  27.7 10.4 %collective-permute-start.4 = (bf16[64,1024]{1,0:T(8,128)(2,1)S(1)}, bf16[64,1024]{1,0:T(8,128)(2,1)S(1)}, u32[]{:S(2)}, u32[]{:S(2)}) collective-permute-start(bf16[64,1024]{1,0:T(8,128)(2,1)S(1)} %collective-permute-done.3.refs_4_), channel_id=1, source_target_pairs={{0,2},{2,0},{4,6},{6,4},{8,10},{10,8},{12,14},{14,12},{1,3},{3,1},... | collective-permute-start | bytes 393224 | tf_op jit(solution)/shard_map/ppermute | solution.py:379
  28.7 9.4 %collective-permute-start.2 = (bf16[64,1024]{1,0:T(8,128)(2,1)S(1)}, bf16[64,1024]{1,0:T(8,128)(2,1)S(1)}, u32[]{:S(2)}, u32[]{:S(2)}) collective-permute-start(bf16[64,1024]{1,0:T(8,128)(2,1)S(1)} %collective-permute-done.1.refs_2_), channel_id=1, source_target_pairs={{0,2},{2,0},{4,6},{6,4},{8,10},{10,8},{12,14},{14,12},{1,3},{3,1},... | collective-permute-start | bytes 393224 | tf_op jit(solution)/shard_map/ppermute | solution.py:379
  31.2 8.3 %collective-permute-start.6 = (bf16[64,1024]{1,0:T(8,128)(2,1)S(1)}, bf16[64,1024]{1,0:T(8,128)(2,1)S(1)}, u32[]{:S(2)}, u32[]{:S(2)}) collective-permute-start(bf16[64,1024]{1,0:T(8,128)(2,1)S(1)} %collective-permute-done.5.refs_6_), channel_id=1, source_target_pairs={{0,2},{2,0},{4,6},{6,4},{8,10},{10,8},{12,14},{14,12},{1,3},{3,1},... | collective-permute-start | bytes 393224 | tf_op jit(solution)/shard_map/ppermute | solution.py:379
  39.5 20.5 %collective-permute-start.18 = (bf16[512,1024]{1,0:T(8,128)(2,1)S(1)}, bf16[512,1024]{1,0:T(8,128)(2,1)S(1)}, u32[]{:S(2)}, u32[]{:S(2)}) collective-permute-start(bf16[512,1024]{1,0:T(8,128)(2,1)S(1)} %stack_kernel.1), channel_id=1, source_target_pairs={{0,1},{1,0},{2,3},{3,2},{4,5},{5,4},{6,7},{7,6},{8,9},{9,8},{10,11... | collective-permute-start | bytes 3145736 | tf_op jit(solution)/shard_map/ppermute | solution.py:382
  40.4 2.0 %collective-permute-start.14 = (bf16[32,1024]{1,0:T(8,128)(2,1)S(1)}, bf16[32,1024]{1,0:T(8,128)(2,1)S(1)}, u32[]{:S(2)}, u32[]{:S(2)}) collective-permute-start(bf16[32,1024]{1,0:T(8,128)(2,1)S(1)} %get-tuple-element.57), channel_id=1, source_target_pairs={{0,1},{1,0},{2,3},{3,2},{4,5},{5,4},{6,7},{7,6},{8,9},{9,8},{10,11... | collective-permute-start | bytes 196616 | tf_op jit(solution)/shard_map/ppermute | solution.py:382
  43.6 9.2 %collective-permute-start.19 = (bf16[128,1024]{1,0:T(8,128)(2,1)S(1)}, bf16[128,1024]{1,0:T(8,128)(2,1)S(1)}, u32[]{:S(2)}, u32[]{:S(2)}) collective-permute-start(bf16[128,1024]{1,0:T(8,128)(2,1)S(1)} %get-tuple-element.82), channel_id=1, source_target_pairs={{0,2},{2,0},{4,6},{6,4},{8,10},{10,8},{12,14},{14,12},{1,3},{3,1},... | collective-permute-start | bytes 786440 | tf_op jit(solution)/shard_map/ppermute | solution.py:379
  45.3 14.8 %collective-permute-start.17 = (bf16[512,512]{1,0:T(8,128)(2,1)S(1)}, bf16[512,512]{1,0:T(8,128)(2,1)S(1)}, u32[]{:S(2)}, u32[]{:S(2)}) collective-permute-start(bf16[512,512]{1,0:T(8,128)(2,1)S(1)} %get-tuple-element.78), channel_id=1, source_target_pairs={{0,1},{1,0},{2,3},{3,2},{4,5},{5,4},{6,7},{7,6},{8,9},{9,8},{10,11... | collective-permute-start | bytes 1572872 | tf_op jit(solution)/shard_map/ppermute | solution.py:382
  45.8 11.8 %collective-permute-start.15 = (bf16[128,1024]{1,0:T(8,128)(2,1)S(1)}, bf16[128,1024]{1,0:T(8,128)(2,1)S(1)}, u32[]{:S(2)}, u32[]{:S(2)}) collective-permute-start(bf16[128,1024]{1,0:T(8,128)(2,1)S(1)} %get-tuple-element.65), channel_id=1, source_target_pairs={{0,2},{2,0},{4,6},{6,4},{8,10},{10,8},{12,14},{14,12},{1,3},{3,1},... | collective-permute-start | bytes 786440 | tf_op jit(solution)/shard_map/ppermute | solution.py:379
  53.5 12.6 %collective-permute-start.20 = (bf16[64,1024]{1,0:T(8,128)(2,1)S(1)}, bf16[64,1024]{1,0:T(8,128)(2,1)S(1)}, u32[]{:S(2)}, u32[]{:S(2)}) collective-permute-start(bf16[64,1024]{1,0:T(8,128)(2,1)S(1)} %get-tuple-element.83), channel_id=1, source_target_pairs={{0,8},{2,10},{4,12},{6,14},{8,0},{10,2},{12,4},{14,6},{1,9},{3,11}... | collective-permute-start | bytes 393224 | tf_op jit(solution)/shard_map/ppermute | solution.py:379
  56.3 9.8 %collective-permute-start.21 = (bf16[64,1024]{1,0:T(8,128)(2,1)S(1)}, bf16[64,1024]{1,0:T(8,128)(2,1)S(1)}, u32[]{:S(2)}, u32[]{:S(2)}) collective-permute-start(bf16[64,1024]{1,0:T(8,128)(2,1)S(1)} %get-tuple-element.84), channel_id=1, source_target_pairs={{0,12},{2,14},{4,8},{6,10},{8,4},{10,6},{12,0},{14,2},{1,13},{3,15... | collective-permute-start | bytes 393224 | tf_op jit(solution)/shard_map/ppermute | solution.py:379
  58.4 7.8 %collective-permute-start.16 = (bf16[64,1024]{1,0:T(8,128)(2,1)S(1)}, bf16[64,1024]{1,0:T(8,128)(2,1)S(1)}, u32[]{:S(2)}, u32[]{:S(2)}) collective-permute-start(bf16[64,1024]{1,0:T(8,128)(2,1)S(1)} %get-tuple-element.68), channel_id=1, source_target_pairs={{0,4},{2,6},{4,0},{6,2},{8,12},{10,14},{12,8},{14,10},{1,5},{3,7},... | collective-permute-start | bytes 393224 | tf_op jit(solution)/shard_map/ppermute | solution.py:379

commit v8 on v7

--- a/solution.py
+++ b/solution.py
@@ -409,10 +409,10 @@
     mats = matrix_call(place, query_kernel, support_kernel, count, columns, edge)
     here = lax.dynamic_slice(query_feats, (side * tile, 0), (tile, width))
     there = lax.dynamic_slice(query_feats, ((side ^ 1) * tile, 0), (tile, width))
-    ordered = held + [pieces[k] for k in [7, 5, 6, 4, 3, 1, 2, 0]]
+    ordered = held + [pieces[k] for k in [7, 5, 6, 3, 4, 1, 2, 0]]
     ordered, mats, here, there = lax.optimization_barrier((ordered, mats, here, there))
     held, landed = ordered[:count], ordered[count:]
-    for at, k in enumerate([7, 5, 6, 4, 3, 1, 2, 0]):
+    for at, k in enumerate([7, 5, 6, 3, 4, 1, 2, 0]):
         pieces[k] = landed[at]
     cells, rim = gather_call(place, pieces, tile, edge)
     rim = swapped(rim)
@@ -455,8 +455,7 @@
         planes == 1
         and shape["pair"] == 2
         and shape["sub"] == 2
-        and count >= 4
-        and count & (count - 1) == 0
+        and count == 8
         and count * columns <= 1024
         and columns % 16 == 0
         and QW % columns == 0

time: 67.1 us -> 67.1 us (level)
  transfers between devices with their start and end apart: 22 -> 22, of which waited for: 10 -> 9; matrix products, arithmetic and copies ran while one was open for 11% -> 11% of each run, Pallas kernels for 10% -> 10%
where the time goes in v8:
time: 67.1 us; the launch traced here: 66.9 us
  starting transfers between devices  29.7 us (44%)
  waiting for transfers between devices  21.1 us (31%)
  Pallas kernels  7.05 us (11%)
  local copies, waits for them, and re-layouts  4.28 us (6%)
  matrix products  3.19 us (5%)
  other arithmetic  0.86 us (1%)
  between operations  0.79 us (1%)
    ppermute x19, starting transfers between devices, exchanged(): lax.ppermute(value, ('blk', 'sub'), [(i, i ^ mask) for i in range(count)])  29 us
    ppermute x19, waiting for transfers between devices, exchanged(): lax.ppermute(value, ('blk', 'sub'), [(i, i ^ mask) for i in range(count)])  20.9 us
    dot_general x4, matrix products, query_term(): lax.dot_general(block, feats, (((0,), (0,)), ((), ())), preferred_element...  3.19 us
    dynamic_slice x1, local copies, waits for them, and re-layouts, tile_shards(): lax.dynamic_slice(query_feats, ((side ^ 1) * tile, 0), (tile, width))  2.66 us
    pallas_call x2, Pallas kernels, corr_call(): pl.pallas_call(lambda *refs: corr_kernel(group, columns, tile, *refs), ou...  2.37 us
    dynamic_slice x1, local copies, waits for them, and re-layouts, piece(): lax.dynamic_slice(volume, (0, (own ^ mask) * tile), (columns, tile + 2 *...  1.52 us
    pallas_call x2, Pallas kernels, partial_call(): pl.pallas_call(lambda *refs: partial_kernel(columns, *refs), out_shape=[j...  1.47 us
  transfers between devices with their start and end apart: 22, of which 9 were waited for; matrix products, arithmetic and copies ran while one was open for 11% of the time, Pallas kernels for 10%

profile of v8, /device:TPU:0, one launch (start us, length us, event | category | flops | bytes accessed | tf_op | source)
XLA Modules:
  0.0 66.9 jit_solution(9265132052729962371)
XLA Ops:
  0.6 4.1 %collective-permute-start.3 = (bf16[64,1024]{1,0:T(8,128)(2,1)}, bf16[64,1024]{1,0:T(8,128)(2,1)S(1)}, u32[]{:S(2)}, u32[]{:S(2)}) collective-permute-start(bf16[64,1024]{1,0:T(8,128)(2,1)} %bitcast.14), channel_id=1, source_target_pairs={{0,8},{2,10},{4,12},{6,14},{8,0},{10,2},{12,4},{14,6},{1,9},{3,11}... | collective-permute-start | bytes 393224 | tf_op jit(solution)/shard_map/ppermute | solution.py:379
  4.8 1.6 %collective-permute-start.1 = (bf16[64,1024]{1,0:T(8,128)(2,1)}, bf16[64,1024]{1,0:T(8,128)(2,1)S(1)}, u32[]{:S(2)}, u32[]{:S(2)}) collective-permute-start(bf16[64,1024]{1,0:T(8,128)(2,1)} %bitcast.15), channel_id=1, source_target_pairs={{0,4},{2,6},{4,0},{6,2},{8,12},{10,14},{12,8},{14,10},{1,5},{3,7},... | collective-permute-start | bytes 393224 | tf_op jit(solution)/shard_map/ppermute | solution.py:379
  6.3 1.5 %collective-permute-start = (bf16[64,1024]{1,0:T(8,128)(2,1)}, bf16[64,1024]{1,0:T(8,128)(2,1)S(1)}, u32[]{:S(2)}, u32[]{:S(2)}) collective-permute-start(bf16[64,1024]{1,0:T(8,128)(2,1)} %bitcast.16), channel_id=1, source_target_pairs={{0,2},{2,0},{4,6},{6,4},{8,10},{10,8},{12,14},{14,12},{1,3},{3,1},... | collective-permute-start | bytes 393224 | tf_op jit(solution)/shard_map/ppermute | solution.py:379
  7.8 1.5 %pad_dynamic-slice_fusion = (bf16[64,1280]{1,0:T(8,128)(2,1)S(1)}, bf16[64,1280]{1,0:T(8,128)(2,1)S(1)}, bf16[64,1280]{1,0:T(8,128)(2,1)S(1)}, bf16[64,1280]{1,0...) fusion(s32[]{:T(128)S(6)} %select_n.37, ...), kind=kLoop, calls=%fused_computation.8 | loop fusion | bytes 2359328 | tf_op jit(solution)/shard_map/dynamic_slice | solution.py:387
  9.3 0.5 collective-permute-start.10
  9.8 0.1 collective-permute-start.11
  9.9 1.4 %collective-permute-done.3.refs_4_ = bf16[64,1024]{1,0:T(8,128)(2,1)S(1)} collective-permute-done((bf16[64,1024]{1,0:T(8,128)(2,1)}, bf16[64,1024]{1,0:T(8,128)(2,1)S(1)}, u32[]{:S(2)}, u32[]{:S(2)}) %collective-permute-start.3) | collective-permute-done | bytes 131104 | tf_op jit(solution)/shard_map/ppermute | solution.py:379
  11.4 1.5 %collective-permute-start.12 = (bf16[64,1280]{1,0:T(8,128)(2,1)S(1)}, bf16[64,1280]{1,0:T(8,128)(2,1)S(1)}, u32[]{:S(2)}, u32[]{:S(2)}) collective-permute-start(bf16[64,1280]{1,0:T(8,128)(2,1)S(1)} %get-tuple-element.93), channel_id=1, source_target_pairs={{0,2},{2,0},{4,6},{6,4},{8,10},{10,8},{12,14},{14,12},{1,3},{3,1},... | collective-permute-start | bytes 491528 | tf_op jit(solution)/shard_map/ppermute | solution.py:379
  12.9 1.2 %collective-permute-start.13 = (bf16[64,1280]{1,0:T(8,128)(2,1)S(1)}, bf16[64,1280]{1,0:T(8,128)(2,1)S(1)}, u32[]{:S(2)}, u32[]{:S(2)}) collective-permute-start(bf16[64,1280]{1,0:T(8,128)(2,1)S(1)} %get-tuple-element.94), channel_id=1, source_target_pairs={{0,4},{2,6},{4,0},{6,2},{8,12},{10,14},{12,8},{14,10},{1,5},{3,7},... | collective-permute-start | bytes 491528 | tf_op jit(solution)/shard_map/ppermute | solution.py:379
  14.2 0.0 collective-permute-done.refs_1_
  14.2 2.4 %collective-permute-start.7 = (bf16[64,1280]{1,0:T(8,128)(2,1)S(1)}, bf16[64,1280]{1,0:T(8,128)(2,1)S(1)}, u32[]{:S(2)}, u32[]{:S(2)}) collective-permute-start(bf16[64,1280]{1,0:T(8,128)(2,1)S(1)} %get-tuple-element.95), channel_id=1, source_target_pairs={{0,14},{2,12},{4,10},{6,8},{8,6},{10,4},{12,2},{14,0},{1,15},{3,13... | collective-permute-start | bytes 491528 | tf_op jit(solution)/shard_map/ppermute | solution.py:379
  16.5 3.5 %collective-permute-done.10.refs_5_ = bf16[64,1280]{1,0:T(8,128)(2,1)S(1)} collective-permute-done((bf16[64,1280]{1,0:T(8,128)(2,1)S(1)}, bf16[64,1280]{1,0:T(8,128)(2,1)S(1)}, u32[]{:S(2)}, u32[]{:S(2)}) %collective-permute-start.10) | collective-permute-done | bytes 163872 | tf_op jit(solution)/shard_map/ppermute | solution.py:379
  20.1 0.1 reshape.7.refs_1_
  20.2 0.1 pad_add_fusion.refs_0_
  20.3 1.2 %matrix_kernel.1 = (bf16[256,256]{1,0:T(8,128)(2,1)S(1)}, bf16[512,32]{1,0:T(8,128)(2,1)S(1)}, bf16[512,256]{1,0:T(8,128)(2,1)S(1)}, bf16[512,256]{1,0:T(8,128)(2,1)S(1)}) custom-call(s32[2]{0:T(128)S(1)} %pad_add_fusion.refs_0_, f32[36]{0:T(128)S(1)} %reshape.7.refs_1_), custom_call_target="tpu_custom_call" | custom-call | flops 2621440 | bytes 524288 | tf_op jit(solution)/shard_map/matrix_kernel/pallas_call | solution.py:171
  21.5 3.2 %collective-permute-start.8 = (bf16[64,1280]{1,0:T(8,128)(2,1)S(1)}, bf16[64,1280]{1,0:T(8,128)(2,1)S(1)}, u32[]{:S(2)}, u32[]{:S(2)}) collective-permute-start(bf16[64,1280]{1,0:T(8,128)(2,1)S(1)} %get-tuple-element.89), channel_id=1, source_target_pairs={{0,10},{2,8},{4,14},{6,12},{8,2},{10,0},{12,6},{14,4},{1,11},{3,9}... | collective-permute-start | bytes 491528 | tf_op jit(solution)/shard_map/ppermute | solution.py:379
  24.7 1.3 %collective-permute-start.9 = (bf16[64,1280]{1,0:T(8,128)(2,1)S(1)}, bf16[64,1280]{1,0:T(8,128)(2,1)S(1)}, u32[]{:S(2)}, u32[]{:S(2)}) collective-permute-start(bf16[64,1280]{1,0:T(8,128)(2,1)S(1)} %get-tuple-element.90), channel_id=1, source_target_pairs={{0,12},{2,14},{4,8},{6,10},{8,4},{10,6},{12,0},{14,2},{1,13},{3,15... | collective-permute-start | bytes 491528 | tf_op jit(solution)/shard_map/ppermute | solution.py:379
  26.0 1.4 %collective-permute-start.4 = (bf16[64,1024]{1,0:T(8,128)(2,1)S(1)}, bf16[64,1024]{1,0:T(8,128)(2,1)S(1)}, u32[]{:S(2)}, u32[]{:S(2)}) collective-permute-start(bf16[64,1024]{1,0:T(8,128)(2,1)S(1)} %collective-permute-done.3.refs_4_), channel_id=1, source_target_pairs={{0,2},{2,0},{4,6},{6,4},{8,10},{10,8},{12,14},{14,12},{1,3},{3,1},... | collective-permute-start | bytes 393224 | tf_op jit(solution)/shard_map/ppermute | solution.py:379
  27.4 1.3 %collective-permute-done.7.refs_1_ = bf16[64,1280]{1,0:T(8,128)(2,1)S(1)} collective-permute-done((bf16[64,1280]{1,0:T(8,128)(2,1)S(1)}, bf16[64,1280]{1,0:T(8,128)(2,1)S(1)}, u32[]{:S(2)}, u32[]{:S(2)}) %collective-permute-start.7) | collective-permute-done | bytes 163872 | tf_op jit(solution)/shard_map/ppermute | solution.py:379
  28.7 0.6 collective-permute-start.2
  29.3 2.0 %collective-permute-done.5.refs_6_ = bf16[64,1024]{1,0:T(8,128)(2,1)S(1)} collective-permute-done((bf16[64,1024]{1,0:T(8,128)(2,1)S(1)}, bf16[64,1024]{1,0:T(8,128)(2,1)S(1)}, u32[]{:S(2)}, u32[]{:S(2)}) %collective-permute-start.5) | collective-permute-done | bytes 131104 | tf_op jit(solution)/shard_map/ppermute | solution.py:379
  31.3 1.5 %collective-permute-start.6 = (bf16[64,1024]{1,0:T(8,128)(2,1)S(1)}, bf16[64,1024]{1,0:T(8,128)(2,1)S(1)}, u32[]{:S(2)}, u32[]{:S(2)}) collective-permute-start(bf16[64,1024]{1,0:T(8,128)(2,1)S(1)} %collective-permute-done.5.refs_6_), channel_id=1, source_target_pairs={{0,2},{2,0},{4,6},{6,4},{8,10},{10,8},{12,14},{14,12},{1,3},{3,1},... | collective-permute-start | bytes 393224 | tf_op jit(solution)/shard_map/ppermute | solution.py:379
  32.9 2.7 %constant_dynamic-slice_fusion = (bf16[1024,1024]{1,0:T(8,128)(2,1)S(1)}, bf16[1024,1024]{1,0:T(8,128)(2,1)S(1)}) fusion(bf16[2048,1024]{1,0:T(8,128)(2,1)} %param.6, s32[]{:T(128)S(6)} %select_n.39, s32[]{:T(128)S(6)} %select_n.38), kind=kLoop, calls=%fused_computation.26 | loop fusion | bytes 8388616 | tf_op jit(solution)/shard_map/dynamic_slice | solution.py:411
  35.5 2.8 %collective-permute-done.8.refs_3_ = bf16[64,1280]{1,0:T(8,128)(2,1)S(1)} collective-permute-done((bf16[64,1280]{1,0:T(8,128)(2,1)S(1)}, bf16[64,1280]{1,0:T(8,128)(2,1)S(1)}, u32[]{:S(2)}, u32[]{:S(2)}) %collective-permute-start.8) | collective-permute-done | bytes 163872 | tf_op jit(solution)/shard_map/ppermute | solution.py:379
  38.3 1.1 %collective-permute-done.6.refs_7_ = bf16[64,1024]{1,0:T(8,128)(2,1)S(1)} collective-permute-done((bf16[64,1024]{1,0:T(8,128)(2,1)S(1)}, bf16[64,1024]{1,0:T(8,128)(2,1)S(1)}, u32[]{:S(2)}, u32[]{:S(2)}) %collective-permute-start.6) | collective-permute-done | bytes 131104 | tf_op jit(solution)/shard_map/ppermute | solution.py:379
  39.4 0.1 stack_kernel.1
  39.5 0.1 collective-permute-start.18
  39.6 0.7 %gather_kernel.1 = (bf16[640,1280]{1,0:T(8,128)(2,1)S(1)}, bf16[32,1024]{1,0:T(8,128)(2,1)S(1)}) custom-call(s32[2]{0:T(128)S(1)} %pad_add_fusion.refs_0_, bf16[64,1280]{1,0:T(8,128)(2,1)S(1)} %collective-permute-done.7.refs_1_, bf16[64,1280]{1,0:T(8,128)(2,1)S(1)} %collective-permute-done.9.refs_2_, bf16[64,1280]{1,0:T(8,128)(2,1)S(1)} %collective-permute-done.8.refs_3_, ...), custom_call_target="tpu_custom_call" | custom-call | flops 8192 | bytes 2621440 | tf_op jit(solution)/shard_map/gather_kernel/pallas_call | solution.py:209
  40.3 0.6 collective-permute-start.14
  40.9 1.2 %query_kernel.1.refs_5_ = f32[512,1024]{1,0:T(8,128)S(1)} custom-call(bf16[640,1280]{1,0:T(8,128)(2,1)S(1)} %get-tuple-element.56.refs_0_.refs_1_, bf16[512,256]{1,0:T(8,128)(2,1)S(1)} %get-tuple-element.60.refs_1_, bf16[512,256]{1,0:T(8,128)(2,1)S(1)} %get-tuple-element.61.refs_2_), custom_call_target="tpu_custom_call" | custom-call | flops 1073741824 | bytes 4194304 | tf_op jit(solution)/shard_map/query_kernel/pallas_call | solution.py:241
  42.1 0.2 collective-permute-done.14.refs_2_
  42.3 1.2 %corr_kernel.2 = (bf16[128,1024]{1,0:T(8,128)(2,1)S(1)}, bf16[128,1024]{1,0:T(8,128)(2,1)S(1)}, bf16[256,512]{1,0:T(8,128)(2,1)S(1)}, bf16[256,512]{1,0:T(8,128)(2,1)S(1)}) custom-call(s32[2]{0:T(128)S(1)} %pad_add_fusion.refs_0_, bf16[640,1280]{1,0:T(8,128)(2,1)S(1)} %get-tuple-element.56.refs_0_.refs_1_, ...), custom_call_target="tpu_custom_call" | custom-call | flops 268435456 | bytes 2097152 | tf_op jit(solution)/shard_map/corr_kernel/pallas_call | solution.py:299
  43.5 0.6 collective-permute-start.19
  44.2 1.2 %corr_kernel.3 = (bf16[128,1024]{1,0:T(8,128)(2,1)S(1)}, bf16[128,1024]{1,0:T(8,128)(2,1)S(1)}, bf16[512,512]{1,0:T(8,128)(2,1)S(1)}, bf16[512,512]{1,0:T(8,128)(2,1)S(1)}) custom-call(s32[2]{0:T(128)S(1)} %pad_add_fusion.refs_0_, bf16[640,1280]{1,0:T(8,128)(2,1)S(1)} %get-tuple-element.56.refs_0_.refs_1_, ...), custom_call_target="tpu_custom_call" | custom-call | flops 268435456 | bytes 2097152 | tf_op jit(solution)/shard_map/corr_kernel/pallas_call | solution.py:299
  45.4 0.1 collective-permute-start.17
  45.5 0.5 fusion.3
  45.9 1.5 %collective-permute-start.15 = (bf16[128,1024]{1,0:T(8,128)(2,1)S(1)}, bf16[128,1024]{1,0:T(8,128)(2,1)S(1)}, u32[]{:S(2)}, u32[]{:S(2)}) collective-permute-start(bf16[128,1024]{1,0:T(8,128)(2,1)S(1)} %get-tuple-element.65), channel_id=1, source_target_pairs={{0,2},{2,0},{4,6},{6,4},{8,10},{10,8},{12,14},{14,12},{1,3},{3,1},... | collective-permute-start | bytes 786440 | tf_op jit(solution)/shard_map/ppermute | solution.py:379
  47.4 0.5 fusion.5
  47.9 4.9 %collective-permute-done.19.refs_1_ = bf16[128,1024]{1,0:T(8,128)(2,1)S(1)} collective-permute-done((bf16[128,1024]{1,0:T(8,128)(2,1)S(1)}, bf16[128,1024]{1,0:T(8,128)(2,1)S(1)}, u32[]{:S(2)}, u32[]{:S(2)}) %collective-permute-start.19) | collective-permute-done | bytes 262176 | tf_op jit(solution)/shard_map/ppermute | solution.py:379
  52.8 0.7 %partial_kernel.3 = (bf16[64,1024]{1,0:T(8,128)(2,1)S(1)}, bf16[64,1024]{1,0:T(8,128)(2,1)S(1)}) custom-call(bf16[128,1024]{1,0:T(8,128)(2,1)S(1)} %get-tuple-element.81.refs_0_, bf16[128,1024]{1,0:T(8,128)(2,1)S(1)} %collective-permute-done.19.refs_1_, bf16[1024,1024]{1,0:T(8,128)(2,1)S(1)} %get-tuple-element.66.refs_2_, ...), custom_call_target="tpu_custom_call" | custom-call | flops 536870912 | bytes 4194304 | tf_op jit(solution)/shard_map/partial_kernel/pallas_call | solution.py:330
  53.5 2.7 %collective-permute-start.20 = (bf16[64,1024]{1,0:T(8,128)(2,1)S(1)}, bf16[64,1024]{1,0:T(8,128)(2,1)S(1)}, u32[]{:S(2)}, u32[]{:S(2)}) collective-permute-start(bf16[64,1024]{1,0:T(8,128)(2,1)S(1)} %get-tuple-element.83), channel_id=1, source_target_pairs={{0,8},{2,10},{4,12},{6,14},{8,0},{10,2},{12,4},{14,6},{1,9},{3,11}... | collective-permute-start | bytes 393224 | tf_op jit(solution)/shard_map/ppermute | solution.py:379
  56.2 1.5 %collective-permute-start.21 = (bf16[64,1024]{1,0:T(8,128)(2,1)S(1)}, bf16[64,1024]{1,0:T(8,128)(2,1)S(1)}, u32[]{:S(2)}, u32[]{:S(2)}) collective-permute-start(bf16[64,1024]{1,0:T(8,128)(2,1)S(1)} %get-tuple-element.84), channel_id=1, source_target_pairs={{0,12},{2,14},{4,8},{6,10},{8,4},{10,6},{12,0},{14,2},{1,13},{3,15... | collective-permute-start | bytes 393224 | tf_op jit(solution)/shard_map/ppermute | solution.py:379
  57.7 0.7 %partial_kernel.2 = (f32[64,1024]{1,0:T(8,128)S(1)}, bf16[64,1024]{1,0:T(8,128)(2,1)S(1)}) custom-call(bf16[128,1024]{1,0:T(8,128)(2,1)S(1)} %get-tuple-element.64.refs_0_, bf16[128,1024]{1,0:T(8,128)(2,1)S(1)} %collective-permute-done.15.refs_1_, bf16[1024,1024]{1,0:T(8,128)(2,1)S(1)} %get-tuple-element.66.refs_2_, ...), custom_call_target="tpu_custom_call" | custom-call | flops 536870912 | bytes 4194304 | tf_op jit(solution)/shard_map/partial_kernel/pallas_call | solution.py:330
  58.4 1.7 %collective-permute-start.16 = (bf16[64,1024]{1,0:T(8,128)(2,1)S(1)}, bf16[64,1024]{1,0:T(8,128)(2,1)S(1)}, u32[]{:S(2)}, u32[]{:S(2)}) collective-permute-start(bf16[64,1024]{1,0:T(8,128)(2,1)S(1)} %get-tuple-element.68), channel_id=1, source_target_pairs={{0,4},{2,6},{4,0},{6,2},{8,12},{10,14},{12,8},{14,10},{1,5},{3,7},... | collective-permute-start | bytes 393224 | tf_op jit(solution)/shard_map/ppermute | solution.py:379
  60.1 0.5 fusion
  60.6 1.8 %add_multiply_fusion = f32[512,1024]{1,0:T(8,128)} fusion(f32[512,1024]{1,0:T(8,128)S(1)} %fusion, f32[512,1024]{1,0:T(8,128)S(1)} %fusion.5, f32[512,1024]{1,0:T(8,128)S(1)} %fusion.3, bf16[512,1024]{1,0:T(8,128)(2,1)S(1)} %collective-permute-done.18, bf16[512,512]{1,0:T(8,128)(2,1)S(1)} %collective-permute-done.17), kind=kOutput, calls=%fused_computation | convolution fusion | flops 270532608 | bytes 9175040 | tf_op jit(solution)/shard_map/dot_general | solution.py:434
  62.4 3.7 %collective-permute-done.16 = bf16[64,1024]{1,0:T(8,128)(2,1)S(1)} collective-permute-done((bf16[64,1024]{1,0:T(8,128)(2,1)S(1)}, bf16[64,1024]{1,0:T(8,128)(2,1)S(1)}, u32[]{:S(2)}, u32[]{:S(2)}) %collective-permute-start.16) | collective-permute-done | bytes 131104 | tf_op jit(solution)/shard_map/ppermute | solution.py:379
  66.2 0.8 %multiply_bitcast_fusion = f32[1,64,1024]{2,1,0:T(8,128)} fusion(bf16[64,1024]{1,0:T(8,128)(2,1)S(1)} %collective-permute-done.16, bf16[64,1024]{1,0:T(8,128)(2,1)S(1)} %collective-permute-done.21, f32[64,1024]{1,0:T(8,128)S(1)} %get-tuple-element.80, bf16[64,1024]{1,0:T(8,128)(2,1)S(1)} %collective-permute-done.20), kind=kLoop, calls=%fused_computation.18 | loop fusion | flops 458752 | bytes 917504 | tf_op jit(solution)/shard_map/broadcast_in_dim | solution.py:446
  (21 shorter events, 0.1 us)
Async XLA Ops:
  0.6 9.3 %copy-start.2 = (f32[3,3]{1,0:T(4,128)S(1)}, f32[3,3]{1,0:T(4,128)}, u32[]{:S(2)}) copy-start(f32[3,3]{1,0:T(4,128)} %param.8) | copy-start | bytes 112
  0.6 9.3 %copy-start.1 = (f32[3,3]{1,0:T(4,128)S(1)}, f32[3,3]{1,0:T(4,128)}, u32[]{:S(2)}) copy-start(f32[3,3]{1,0:T(4,128)} %param.9) | copy-start | bytes 112
  0.6 10.7 %collective-permute-start.3 = (bf16[64,1024]{1,0:T(8,128)(2,1)}, bf16[64,1024]{1,0:T(8,128)(2,1)S(1)}, u32[]{:S(2)}, u32[]{:S(2)}) collective-permute-start(bf16[64,1024]{1,0:T(8,128)(2,1)} %bitcast.14), channel_id=1, source_target_pairs={{0,8},{2,10},{4,12},{6,14},{8,0},{10,2},{12,4},{14,6},{1,9},{3,11}... | collective-permute-start | bytes 393224 | tf_op jit(solution)/shard_map/ppermute | solution.py:379
  4.8 8.2 %collective-permute-start.1 = (bf16[64,1024]{1,0:T(8,128)(2,1)}, bf16[64,1024]{1,0:T(8,128)(2,1)S(1)}, u32[]{:S(2)}, u32[]{:S(2)}) collective-permute-start(bf16[64,1024]{1,0:T(8,128)(2,1)} %bitcast.15), channel_id=1, source_target_pairs={{0,4},{2,6},{4,0},{6,2},{8,12},{10,14},{12,8},{14,10},{1,5},{3,7},... | collective-permute-start | bytes 393224 | tf_op jit(solution)/shard_map/ppermute | solution.py:379
  6.3 7.8 %collective-permute-start = (bf16[64,1024]{1,0:T(8,128)(2,1)}, bf16[64,1024]{1,0:T(8,128)(2,1)S(1)}, u32[]{:S(2)}, u32[]{:S(2)}) collective-permute-start(bf16[64,1024]{1,0:T(8,128)(2,1)} %bitcast.16), channel_id=1, source_target_pairs={{0,2},{2,0},{4,6},{6,4},{8,10},{10,8},{12,14},{14,12},{1,3},{3,1},... | collective-permute-start | bytes 393224 | tf_op jit(solution)/shard_map/ppermute | solution.py:379
  9.3 10.7 %collective-permute-start.10 = (bf16[64,1280]{1,0:T(8,128)(2,1)S(1)}, bf16[64,1280]{1,0:T(8,128)(2,1)S(1)}, u32[]{:S(2)}, u32[]{:S(2)}) collective-permute-start(bf16[64,1280]{1,0:T(8,128)(2,1)S(1)} %get-tuple-element.91), channel_id=1, source_target_pairs={{0,6},{2,4},{4,2},{6,0},{8,14},{10,12},{12,10},{14,8},{1,7},{3,5},... | collective-permute-start | bytes 491528 | tf_op jit(solution)/shard_map/ppermute | solution.py:379
  9.8 11.6 %collective-permute-start.11 = (bf16[64,1280]{1,0:T(8,128)(2,1)S(1)}, bf16[64,1280]{1,0:T(8,128)(2,1)S(1)}, u32[]{:S(2)}, u32[]{:S(2)}) collective-permute-start(bf16[64,1280]{1,0:T(8,128)(2,1)S(1)} %get-tuple-element.92), channel_id=1, source_target_pairs={{0,8},{2,10},{4,12},{6,14},{8,0},{10,2},{12,4},{14,6},{1,9},{3,11}... | collective-permute-start | bytes 491528 | tf_op jit(solution)/shard_map/ppermute | solution.py:379
  11.4 13.3 %collective-permute-start.12 = (bf16[64,1280]{1,0:T(8,128)(2,1)S(1)}, bf16[64,1280]{1,0:T(8,128)(2,1)S(1)}, u32[]{:S(2)}, u32[]{:S(2)}) collective-permute-start(bf16[64,1280]{1,0:T(8,128)(2,1)S(1)} %get-tuple-element.93), channel_id=1, source_target_pairs={{0,2},{2,0},{4,6},{6,4},{8,10},{10,8},{12,14},{14,12},{1,3},{3,1},... | collective-permute-start | bytes 491528 | tf_op jit(solution)/shard_map/ppermute | solution.py:379
  12.9 13.0 %collective-permute-start.13 = (bf16[64,1280]{1,0:T(8,128)(2,1)S(1)}, bf16[64,1280]{1,0:T(8,128)(2,1)S(1)}, u32[]{:S(2)}, u32[]{:S(2)}) collective-permute-start(bf16[64,1280]{1,0:T(8,128)(2,1)S(1)} %get-tuple-element.94), channel_id=1, source_target_pairs={{0,4},{2,6},{4,0},{6,2},{8,12},{10,14},{12,8},{14,10},{1,5},{3,7},... | collective-permute-start | bytes 491528 | tf_op jit(solution)/shard_map/ppermute | solution.py:379
  14.2 14.5 %collective-permute-start.7 = (bf16[64,1280]{1,0:T(8,128)(2,1)S(1)}, bf16[64,1280]{1,0:T(8,128)(2,1)S(1)}, u32[]{:S(2)}, u32[]{:S(2)}) collective-permute-start(bf16[64,1280]{1,0:T(8,128)(2,1)S(1)} %get-tuple-element.95), channel_id=1, source_target_pairs={{0,14},{2,12},{4,10},{6,8},{8,6},{10,4},{12,2},{14,0},{1,15},{3,13... | collective-permute-start | bytes 491528 | tf_op jit(solution)/shard_map/ppermute | solution.py:379
  20.1 11.2 %collective-permute-start.5 = (bf16[64,1024]{1,0:T(8,128)(2,1)S(1)}, bf16[64,1024]{1,0:T(8,128)(2,1)S(1)}, u32[]{:S(2)}, u32[]{:S(2)}) collective-permute-start(bf16[64,1024]{1,0:T(8,128)(2,1)S(1)} %collective-permute-done.3.refs_4_), channel_id=1, source_target_pairs={{0,4},{2,6},{4,0},{6,2},{8,12},{10,14},{12,8},{14,10},{1,5},{3,7},... | collective-permute-start | bytes 393224 | tf_op jit(solution)/shard_map/ppermute | solution.py:379
  21.5 16.8 %collective-permute-start.8 = (bf16[64,1280]{1,0:T(8,128)(2,1)S(1)}, bf16[64,1280]{1,0:T(8,128)(2,1)S(1)}, u32[]{:S(2)}, u32[]{:S(2)}) collective-permute-start(bf16[64,1280]{1,0:T(8,128)(2,1)S(1)} %get-tuple-element.89), channel_id=1, source_target_pairs={{0,10},{2,8},{4,14},{6,12},{8,2},{10,0},{12,6},{14,4},{1,11},{3,9}... | collective-permute-start | bytes 491528 | tf_op jit(solution)/shard_map/ppermute | solution.py:379
  24.7 14.8 %copy-start = (bf16[1,64,1024]{2,1,0:T(8,128)(2,1)S(1)}, bf16[1,64,1024]{2,1,0:T(8,128)(2,1)}, u32[]{:S(2)}) copy-start(bf16[1,64,1024]{2,1,0:T(8,128)(2,1)} %param.7) | copy-start | bytes 393220
  24.7 13.6 %collective-permute-start.9 = (bf16[64,1280]{1,0:T(8,128)(2,1)S(1)}, bf16[64,1280]{1,0:T(8,128)(2,1)S(1)}, u32[]{:S(2)}, u32[]{:S(2)}) collective-permute-start(bf16[64,1280]{1,0:T(8,128)(2,1)S(1)} %get-tuple-element.90), channel_id=1, source_target_pairs={{0,12},{2,14},{4,8},{6,10},{8,4},{10,6},{12,0},{14,2},{1,13},{3,15... | collective-permute-start | bytes 491528 | tf_op jit(solution)/shard_map/ppermute | solution.py:379
  26.0 12.3 %collective-permute-start.4 = (bf16[64,1024]{1,0:T(8,128)(2,1)S(1)}, bf16[64,1024]{1,0:T(8,128)(2,1)S(1)}, u32[]{:S(2)}, u32[]{:S(2)}) collective-permute-start(bf16[64,1024]{1,0:T(8,128)(2,1)S(1)} %collective-permute-done.3.refs_4_), channel_id=1, source_target_pairs={{0,2},{2,0},{4,6},{6,4},{8,10},{10,8},{12,14},{14,12},{1,3},{3,1},... | collective-permute-start | bytes 393224 | tf_op jit(solution)/shard_map/ppermute | solution.py:379
  28.7 9.6 %collective-permute-start.2 = (bf16[64,1024]{1,0:T(8,128)(2,1)S(1)}, bf16[64,1024]{1,0:T(8,128)(2,1)S(1)}, u32[]{:S(2)}, u32[]{:S(2)}) collective-permute-start(bf16[64,1024]{1,0:T(8,128)(2,1)S(1)} %collective-permute-done.1.refs_2_), channel_id=1, source_target_pairs={{0,2},{2,0},{4,6},{6,4},{8,10},{10,8},{12,14},{14,12},{1,3},{3,1},... | collective-permute-start | bytes 393224 | tf_op jit(solution)/shard_map/ppermute | solution.py:379
  31.3 8.1 %collective-permute-start.6 = (bf16[64,1024]{1,0:T(8,128)(2,1)S(1)}, bf16[64,1024]{1,0:T(8,128)(2,1)S(1)}, u32[]{:S(2)}, u32[]{:S(2)}) collective-permute-start(bf16[64,1024]{1,0:T(8,128)(2,1)S(1)} %collective-permute-done.5.refs_6_), channel_id=1, source_target_pairs={{0,2},{2,0},{4,6},{6,4},{8,10},{10,8},{12,14},{14,12},{1,3},{3,1},... | collective-permute-start | bytes 393224 | tf_op jit(solution)/shard_map/ppermute | solution.py:379
  39.5 20.6 %collective-permute-start.18 = (bf16[512,1024]{1,0:T(8,128)(2,1)S(1)}, bf16[512,1024]{1,0:T(8,128)(2,1)S(1)}, u32[]{:S(2)}, u32[]{:S(2)}) collective-permute-start(bf16[512,1024]{1,0:T(8,128)(2,1)S(1)} %stack_kernel.1), channel_id=1, source_target_pairs={{0,1},{1,0},{2,3},{3,2},{4,5},{5,4},{6,7},{7,6},{8,9},{9,8},{10,11... | collective-permute-start | bytes 3145736 | tf_op jit(solution)/shard_map/ppermute | solution.py:382
  40.3 2.0 %collective-permute-start.14 = (bf16[32,1024]{1,0:T(8,128)(2,1)S(1)}, bf16[32,1024]{1,0:T(8,128)(2,1)S(1)}, u32[]{:S(2)}, u32[]{:S(2)}) collective-permute-start(bf16[32,1024]{1,0:T(8,128)(2,1)S(1)} %get-tuple-element.57), channel_id=1, source_target_pairs={{0,1},{1,0},{2,3},{3,2},{4,5},{5,4},{6,7},{7,6},{8,9},{9,8},{10,11... | collective-permute-start | bytes 196616 | tf_op jit(solution)/shard_map/ppermute | solution.py:382
  43.5 9.2 %collective-permute-start.19 = (bf16[128,1024]{1,0:T(8,128)(2,1)S(1)}, bf16[128,1024]{1,0:T(8,128)(2,1)S(1)}, u32[]{:S(2)}, u32[]{:S(2)}) collective-permute-start(bf16[128,1024]{1,0:T(8,128)(2,1)S(1)} %get-tuple-element.82), channel_id=1, source_target_pairs={{0,2},{2,0},{4,6},{6,4},{8,10},{10,8},{12,14},{14,12},{1,3},{3,1},... | collective-permute-start | bytes 786440 | tf_op jit(solution)/shard_map/ppermute | solution.py:379
  45.4 14.8 %collective-permute-start.17 = (bf16[512,512]{1,0:T(8,128)(2,1)S(1)}, bf16[512,512]{1,0:T(8,128)(2,1)S(1)}, u32[]{:S(2)}, u32[]{:S(2)}) collective-permute-start(bf16[512,512]{1,0:T(8,128)(2,1)S(1)} %get-tuple-element.78), channel_id=1, source_target_pairs={{0,1},{1,0},{2,3},{3,2},{4,5},{5,4},{6,7},{7,6},{8,9},{9,8},{10,11... | collective-permute-start | bytes 1572872 | tf_op jit(solution)/shard_map/ppermute | solution.py:382
  45.9 11.8 %collective-permute-start.15 = (bf16[128,1024]{1,0:T(8,128)(2,1)S(1)}, bf16[128,1024]{1,0:T(8,128)(2,1)S(1)}, u32[]{:S(2)}, u32[]{:S(2)}) collective-permute-start(bf16[128,1024]{1,0:T(8,128)(2,1)S(1)} %get-tuple-element.65), channel_id=1, source_target_pairs={{0,2},{2,0},{4,6},{6,4},{8,10},{10,8},{12,14},{14,12},{1,3},{3,1},... | collective-permute-start | bytes 786440 | tf_op jit(solution)/shard_map/ppermute | solution.py:379
  53.5 12.7 %collective-permute-start.20 = (bf16[64,1024]{1,0:T(8,128)(2,1)S(1)}, bf16[64,1024]{1,0:T(8,128)(2,1)S(1)}, u32[]{:S(2)}, u32[]{:S(2)}) collective-permute-start(bf16[64,1024]{1,0:T(8,128)(2,1)S(1)} %get-tuple-element.83), channel_id=1, source_target_pairs={{0,8},{2,10},{4,12},{6,14},{8,0},{10,2},{12,4},{14,6},{1,9},{3,11}... | collective-permute-start | bytes 393224 | tf_op jit(solution)/shard_map/ppermute | solution.py:379
  56.2 10.0 %collective-permute-start.21 = (bf16[64,1024]{1,0:T(8,128)(2,1)S(1)}, bf16[64,1024]{1,0:T(8,128)(2,1)S(1)}, u32[]{:S(2)}, u32[]{:S(2)}) collective-permute-start(bf16[64,1024]{1,0:T(8,128)(2,1)S(1)} %get-tuple-element.84), channel_id=1, source_target_pairs={{0,12},{2,14},{4,8},{6,10},{8,4},{10,6},{12,0},{14,2},{1,13},{3,15... | collective-permute-start | bytes 393224 | tf_op jit(solution)/shard_map/ppermute | solution.py:379
  58.4 7.7 %collective-permute-start.16 = (bf16[64,1024]{1,0:T(8,128)(2,1)S(1)}, bf16[64,1024]{1,0:T(8,128)(2,1)S(1)}, u32[]{:S(2)}, u32[]{:S(2)}) collective-permute-start(bf16[64,1024]{1,0:T(8,128)(2,1)S(1)} %get-tuple-element.68), channel_id=1, source_target_pairs={{0,4},{2,6},{4,0},{6,2},{8,12},{10,14},{12,8},{14,10},{1,5},{3,7},... | collective-permute-start | bytes 393224 | tf_op jit(solution)/shard_map/ppermute | solution.py:379
